TPU v7x, 32 devices: a whole 2x2x4 slice. The times are simulated.
32 devices in a mesh: dp: 8 (over z, x), space: 4 (over y, core).
Axes of the slice: x: 2, y: 2, z: 4, core: 2. Of those that a mesh axis runs over, the one named last changes fastest.
Arguments:
- latents: bfloat16 [48, 8, 32, 1280], P('dp', 'space'), may hold values from -42 to 42
- buckets: int32 [48, 2], P('dp'), may hold values from 6 to 32, as said below
- gn_gain: float32 [1280], replicated, may hold values from 0.1 to 1.9
- gn_shift: float32 [1280], replicated, may hold values from -3 to 3
- conv_weight: bfloat16 [9, 1280, 1280], P(None, 'dp'), may hold values from -0.0546875 to 0.0546875
- time_bias: float32 [48, 1280], P('dp'), may hold values from -5 to 5
Outputs:
- result: bfloat16 [48, 8, 32, 1280], P('dp', 'space')
Inputs may be any that keep to these rules, and one draw needn't show every extreme that they name: `buckets`: column 0 is a frame's height, column 1 its width; heights are at least 6 and at most 8, widths at least 24 and at most 32; in every draw some frame has height 8 and width 32.
All inputs are finite; a program needn't handle non-finite values.
Results may differ from a plain program's by a relative error of at most 0.0035.
Values may be sent and summed in bfloat16 or wider, within the bound.
No kernel may reach another device: no remote copies, remote signals or barrier semaphores. Data moves between devices by JAX's collectives and lax.ppermute only.
A program may use at most 64 MiB of HBM per device.

v0:
```python
import jax
import jax.numpy as jnp
from jax import lax
from jax.sharding import PartitionSpec as P

GROUPS = 32


eps = 1e-05


def with_halo(x, sides, width):
    for axis, dim in sides:
        size, length = (lax.axis_size(axis), x.shape[dim])
        up = [(i, (i + 1) % size) for i in range(size - 1)]
        down = [(j, i) for i, j in up]
        last = lax.slice_in_dim(x, length - width, length, axis=dim)
        first = lax.slice_in_dim(x, 0, width, axis=dim)
        before = lax.ppermute(last, axis, up)
        after = lax.ppermute(first, axis, down)
        x = jnp.concatenate([before, x, after], axis=dim)
    return x


def tap_product(window, panel):
    return lax.dot_general(
        window, panel, (((3,), (1,)), ((), ())), preferred_element_type=jnp.float32
    )


def on_device(latents, buckets, gn_gain, gn_shift, conv_weight, time_bias):
    frames, rows, cols, chans = latents.shape
    members = chans // GROUPS
    row_ids = lax.axis_index("space") * rows + jnp.arange(rows, dtype=jnp.int32)
    col_ids = jnp.arange(cols, dtype=jnp.int32)
    valid = (
        (row_ids[None, :, None] < buckets[:, 0][:, None, None])
        & (col_ids[None, None, :] < buckets[:, 1][:, None, None])
    ).astype(jnp.float32)
    count = (buckets[:, 0] * buckets[:, 1]).astype(jnp.float32)[:, None] * members
    values = latents.astype(jnp.float32).reshape(frames, rows, cols, GROUPS, members)
    weight_mask = valid[:, :, :, None, None]
    total = lax.psum(jnp.sum(values * weight_mask, axis=(1, 2, 4)), "space")
    mean = total / count
    centered = values - mean[:, None, None, :, None]
    spread = lax.psum(jnp.sum(centered * centered * weight_mask, axis=(1, 2, 4)), "space") / count
    normed = (centered / jnp.sqrt(spread[:, None, None, :, None] + eps)).reshape(
        frames, rows, cols, chans
    )
    normed = normed * gn_gain + gn_shift
    act = (valid[..., None] * jax.nn.silu(normed)).astype(jnp.bfloat16)
    extended = with_halo(act, (("space", 1),), 1)
    padded = jnp.pad(extended, ((0, 0), (0, 0), (1, 1), (0, 0)))

    def add_tap(index, accum):
        window = lax.dynamic_slice(
            padded, (0, index // 3, index % 3, 0), (frames, rows, cols, chans)
        )
        panel = lax.dynamic_index_in_dim(conv_weight, index, 0, keepdims=False)
        return accum + tap_product(window, lax.all_gather(panel, "dp", axis=0, tiled=True))

    conv = lax.fori_loop(0, 9, add_tap, jnp.zeros((frames, rows, cols, chans), jnp.float32))
    conv_out = conv.astype(jnp.bfloat16)
    summed = latents.astype(jnp.float32) + valid[..., None] * (
        conv_out.astype(jnp.float32) + time_bias[:, None, None, :]
    )
    return summed.astype(jnp.bfloat16)


def solution(mesh):
    in_specs = (
        P("dp", "space", None, None),
        P("dp", None),
        P(),
        P(),
        P(None, "dp", None),
        P("dp", None),
    )
    out_specs = P("dp", "space", None, None)
    return jax.shard_map(
        on_device, mesh=mesh, in_specs=in_specs, out_specs=out_specs, check_vma=False
    )
```

profile of v0, /device:TPU:0, one launch (start us, length us, event | category | flops | bytes accessed | tf_op | source)
XLA Modules:
  0.0 674.8 jit_solution(2371292868569001316)
XLA Ops:
  10.1 8.4 %psum.14 = f32[6,32]{1,0:T(8,128)S(1)} all-reduce(f32[6,32]{1,0:T(8,128)S(1)} %reduce_sum.25), channel_id=1, replica_groups=mesh['dp'=8,'space'=4] {'space'}, use_global_device_ids=true, to_apply=%region_2.0 | all-reduce | flops 192 | bytes 1536 | tf_op jit(solution)/shard_map/psum | solution.py:43
  19.5 5.8 psum.15
  30.6 2.2 collective-permute-done.1
  32.8 1.9 fusion.12
  34.7 630.7 %while.16 = (s32[]{:T(128)}, f32[6,2,32,1280]{3,2,1,0:T(8,128)}, bf16[6,4,34,1280]{3,2,1,0:T(8,128)(2,1)}, bf16[9,160,1280]{2,1,0:T(8,128)(2,1)}, s32[]{:T(128)}...) while((s32[]{:T(128)}, f32[6,2,32,1280]{3,2,1,0:T(8,128)}, ...), condition=%wide.region_7.8_spmd.clone, body=%wide.region_6.7_spmd.clone.sunk | while | flops 1259274240 | bytes 20070744 | solution.py:62
  36.6 70.1 %all-gather.6.cloned.1.call-done = bf16[1,1280,1280]{2,1,0:T(8,128)(2,1)} async-done(((bf16[1,160,1280]{2,1,0:T(8,128)(2,1)}), bf16[1,1280,1280]{2,1,0:T(8,128)(2,1)}) %all-gather.6.cloned.1.call-update) | async-done | bytes 3276816 | tf_op jit(solution)/shard_map/while/body/eval_jaxpr/all_gather | solution.py:60
  106.7 5.1 fusion.27
  113.6 61.7 %all-gather.6.cloned.1.call-done = bf16[1,1280,1280]{2,1,0:T(8,128)(2,1)} async-done(((bf16[1,160,1280]{2,1,0:T(8,128)(2,1)}), bf16[1,1280,1280]{2,1,0:T(8,128)(2,1)}) %all-gather.6.cloned.1.call-update) | async-done | bytes 3276816 | tf_op jit(solution)/shard_map/while/body/eval_jaxpr/all_gather | solution.py:60
  175.4 5.7 fusion.27
  182.9 61.7 %all-gather.6.cloned.1.call-done = bf16[1,1280,1280]{2,1,0:T(8,128)(2,1)} async-done(((bf16[1,160,1280]{2,1,0:T(8,128)(2,1)}), bf16[1,1280,1280]{2,1,0:T(8,128)(2,1)}) %all-gather.6.cloned.1.call-update) | async-done | bytes 3276816 | tf_op jit(solution)/shard_map/while/body/eval_jaxpr/all_gather | solution.py:60
  244.7 5.7 fusion.27
  252.2 61.4 %all-gather.6.cloned.1.call-done = bf16[1,1280,1280]{2,1,0:T(8,128)(2,1)} async-done(((bf16[1,160,1280]{2,1,0:T(8,128)(2,1)}), bf16[1,1280,1280]{2,1,0:T(8,128)(2,1)}) %all-gather.6.cloned.1.call-update) | async-done | bytes 3276816 | tf_op jit(solution)/shard_map/while/body/eval_jaxpr/all_gather | solution.py:60
  313.7 5.7 fusion.27
  321.3 61.4 %all-gather.6.cloned.1.call-done = bf16[1,1280,1280]{2,1,0:T(8,128)(2,1)} async-done(((bf16[1,160,1280]{2,1,0:T(8,128)(2,1)}), bf16[1,1280,1280]{2,1,0:T(8,128)(2,1)}) %all-gather.6.cloned.1.call-update) | async-done | bytes 3276816 | tf_op jit(solution)/shard_map/while/body/eval_jaxpr/all_gather | solution.py:60
  382.7 5.7 fusion.27
  390.3 61.4 %all-gather.6.cloned.1.call-done = bf16[1,1280,1280]{2,1,0:T(8,128)(2,1)} async-done(((bf16[1,160,1280]{2,1,0:T(8,128)(2,1)}), bf16[1,1280,1280]{2,1,0:T(8,128)(2,1)}) %all-gather.6.cloned.1.call-update) | async-done | bytes 3276816 | tf_op jit(solution)/shard_map/while/body/eval_jaxpr/all_gather | solution.py:60
  451.7 5.7 fusion.27
  459.3 61.8 %all-gather.6.cloned.1.call-done = bf16[1,1280,1280]{2,1,0:T(8,128)(2,1)} async-done(((bf16[1,160,1280]{2,1,0:T(8,128)(2,1)}), bf16[1,1280,1280]{2,1,0:T(8,128)(2,1)}) %all-gather.6.cloned.1.call-update) | async-done | bytes 3276816 | tf_op jit(solution)/shard_map/while/body/eval_jaxpr/all_gather | solution.py:60
  521.0 5.7 fusion.27
  528.6 61.8 %all-gather.6.cloned.1.call-done = bf16[1,1280,1280]{2,1,0:T(8,128)(2,1)} async-done(((bf16[1,160,1280]{2,1,0:T(8,128)(2,1)}), bf16[1,1280,1280]{2,1,0:T(8,128)(2,1)}) %all-gather.6.cloned.1.call-update) | async-done | bytes 3276816 | tf_op jit(solution)/shard_map/while/body/eval_jaxpr/all_gather | solution.py:60
  590.3 5.7 fusion.27
  597.9 61.7 %all-gather.6.cloned.1.call-done = bf16[1,1280,1280]{2,1,0:T(8,128)(2,1)} async-done(((bf16[1,160,1280]{2,1,0:T(8,128)(2,1)}), bf16[1,1280,1280]{2,1,0:T(8,128)(2,1)}) %all-gather.6.cloned.1.call-update) | async-done | bytes 3276816 | tf_op jit(solution)/shard_map/while/body/eval_jaxpr/all_gather | solution.py:60
  659.7 5.7 fusion.27
  665.4 2.9 fusion.20
  (59 shorter events, 26.0 us)
Async XLA Ops:
  6.5 12.2 %copy-start = (bf16[6,2,32,1280]{3,2,1,0:T(8,128)(2,1)S(1)}, bf16[6,2,32,1280]{3,2,1,0:T(8,128)(2,1)}, u32[]{:S(2)}) copy-start(bf16[6,2,32,1280]{3,2,1,0:T(8,128)(2,1)} %param.8) | copy-start | bytes 2949124
  6.5 19.0 %copy-start.2 = (f32[1280]{0:T(1024)S(1)}, f32[1280]{0:T(1024)}, u32[]{:S(2)}) copy-start(f32[1280]{0:T(1024)} %param.11) | copy-start | bytes 15364
  6.5 19.0 %copy-start.3 = (f32[1280]{0:T(1024)S(1)}, f32[1280]{0:T(1024)}, u32[]{:S(2)}) copy-start(f32[1280]{0:T(1024)} %param.10) | copy-start | bytes 15364
  27.2 3.3 collective-permute-start
  28.9 3.9 collective-permute-start.1
  34.7 630.7 %copy-start.1 = (f32[6,1280]{1,0:T(8,128)S(1)}, f32[6,1280]{1,0:T(8,128)}, u32[]{:S(2)}) copy-start(f32[6,1280]{1,0:T(8,128)} %param.13) | copy-start | bytes 92164
  34.7 71.9 %all-gather.6.cloned.1.call-start = ((), (), s32[]{:S(2)}) async-start(), calls=%async_computation | async-start | bytes 3686400 | tf_op jit(solution)/shard_map/while/body/eval_jaxpr/all_gather | solution.py:60
  111.8 63.6 %all-gather.6.cloned.1.call-start = ((), (), s32[]{:S(2)}) async-start(), calls=%async_computation | async-start | bytes 3686400 | tf_op jit(solution)/shard_map/while/body/eval_jaxpr/all_gather | solution.py:60
  181.1 63.6 %all-gather.6.cloned.1.call-start = ((), (), s32[]{:S(2)}) async-start(), calls=%async_computation | async-start | bytes 3686400 | tf_op jit(solution)/shard_map/while/body/eval_jaxpr/all_gather | solution.py:60
  250.4 63.3 %all-gather.6.cloned.1.call-start = ((), (), s32[]{:S(2)}) async-start(), calls=%async_computation | async-start | bytes 3686400 | tf_op jit(solution)/shard_map/while/body/eval_jaxpr/all_gather | solution.py:60
  319.4 63.3 %all-gather.6.cloned.1.call-start = ((), (), s32[]{:S(2)}) async-start(), calls=%async_computation | async-start | bytes 3686400 | tf_op jit(solution)/shard_map/while/body/eval_jaxpr/all_gather | solution.py:60
  388.4 63.3 %all-gather.6.cloned.1.call-start = ((), (), s32[]{:S(2)}) async-start(), calls=%async_computation | async-start | bytes 3686400 | tf_op jit(solution)/shard_map/while/body/eval_jaxpr/all_gather | solution.py:60
  457.4 63.6 %all-gather.6.cloned.1.call-start = ((), (), s32[]{:S(2)}) async-start(), calls=%async_computation | async-start | bytes 3686400 | tf_op jit(solution)/shard_map/while/body/eval_jaxpr/all_gather | solution.py:60
  526.7 63.6 %all-gather.6.cloned.1.call-start = ((), (), s32[]{:S(2)}) async-start(), calls=%async_computation | async-start | bytes 3686400 | tf_op jit(solution)/shard_map/while/body/eval_jaxpr/all_gather | solution.py:60
  596.1 63.6 %all-gather.6.cloned.1.call-start = ((), (), s32[]{:S(2)}) async-start(), calls=%async_computation | async-start | bytes 3686400 | tf_op jit(solution)/shard_map/while/body/eval_jaxpr/all_gather | solution.py:60
Sparse Core Ops, SparseCore 0:
  37.7 68.8 all-gather.5
  114.8 60.5 all-gather.5
  184.1 60.5 all-gather.5
  253.1 60.5 all-gather.5
  322.1 60.5 all-gather.5
  391.1 60.5 all-gather.5
  460.4 60.5 all-gather.5
  529.8 60.5 all-gather.5
  599.1 60.5 all-gather.5
where the time goes:
time: 675 us
  waiting for transfers between devices  566 us (84%)
  matrix products  50.9 us (8%)
  local copies, waits for them, and re-layouts  18.2 us (3%)
  blocking collectives  14.1 us (2%)
  between operations  13.2 us (2%)
  other arithmetic  9.07 us (1%)
    all_gather x9, waiting for transfers between devices, add_tap(): lax.all_gather(panel, 'dp', axis=0, tiled=True)  563 us
    dot_general x9, matrix products, tap_product(): lax.dot_general(window, panel, (((3,), (1,)), ((), ())), preferred_elemen...  50.9 us
    dynamic_slice x9, local copies, waits for them, and re-layouts, add_tap(): panel = lax.dynamic_index_in_dim(conv_weight, index, 0, keepdims=False)  16 us
  transfers between devices with their start and end apart: 11, of which 11 were waited for; matrix products, arithmetic and copies ran while one was open for 0% of the time, Pallas kernels for 0%

commit v1 on v0

--- a/solution.py
+++ b/solution.py
@@ -4,9 +4,8 @@
 from jax.sharding import PartitionSpec as P
 
 GROUPS = 32
-
-
-eps = 1e-05
+EPS = 1e-05
+FRAME_BYTES = 8 << 20
 
 
 def with_halo(x, sides, width):
@@ -28,7 +27,7 @@
     )
 
 
-def on_device(latents, buckets, gn_gain, gn_shift, conv_weight, time_bias):
+def row_plan(latents, buckets, gn_gain, gn_shift, conv_weight, time_bias):
     frames, rows, cols, chans = latents.shape
     members = chans // GROUPS
     row_ids = lax.axis_index("space") * rows + jnp.arange(rows, dtype=jnp.int32)
@@ -44,7 +43,7 @@
     mean = total / count
     centered = values - mean[:, None, None, :, None]
     spread = lax.psum(jnp.sum(centered * centered * weight_mask, axis=(1, 2, 4)), "space") / count
-    normed = (centered / jnp.sqrt(spread[:, None, None, :, None] + eps)).reshape(
+    normed = (centered / jnp.sqrt(spread[:, None, None, :, None] + EPS)).reshape(
         frames, rows, cols, chans
     )
     normed = normed * gn_gain + gn_shift
@@ -62,6 +61,157 @@
     conv = lax.fori_loop(0, 9, add_tap, jnp.zeros((frames, rows, cols, chans), jnp.float32))
     conv_out = conv.astype(jnp.bfloat16)
     summed = latents.astype(jnp.float32) + valid[..., None] * (
+        conv_out.astype(jnp.float32) + time_bias[:, None, None, :]
+    )
+    return summed.astype(jnp.bfloat16)
+
+
+class Grid:
+    def __init__(self, mesh):
+        dp, space = mesh.shape["dp"], mesh.shape["space"]
+        self.X = self.C = 2
+        self.Z, self.Y = dp // 2, space // 2
+        self.places = [
+            (z, x, y, c)
+            for z in range(self.Z)
+            for x in range(2)
+            for y in range(self.Y)
+            for c in range(2)
+        ]
+
+    def linear(self, z, x, y, c):
+        return ((z * 2 + x) * self.Y + y) * 2 + c
+
+    def permute(self, value, target):
+        pairs = []
+        for place in self.places:
+            goal = target(*place)
+            if goal is not None:
+                pairs.append((self.linear(*place), self.linear(*goal)))
+        return lax.ppermute(value, ("dp", "space"), pairs)
+
+
+def pick(flag, first, second):
+    return jnp.where(flag == 0, first, second)
+
+
+def by_source(grid, rounds, y, flip):
+    ordered = []
+    per_round = [
+        [pick(flip, row[bit], row[1 - bit]) for bit in range(2)] for row in rounds
+    ]
+    for source in range(grid.Y):
+        for bit in range(2):
+            options = [per_round[i][bit] for i in range(grid.Y)]
+            index = (y - source) % grid.Y
+            ordered.append(lax.select_n(index, *options) if grid.Y > 2 else pick(index, *options))
+    return ordered
+
+
+def gather_line(grid, piece, z):
+    Z = grid.Z
+    below, above = [], []
+    up = down = piece
+    for step in range(1, Z):
+        up = grid.permute(
+            up, lambda z, x, y, c, s=step: (z + 1, x, y, c) if s - 1 <= z < Z - 1 else None
+        )
+        down = grid.permute(
+            down, lambda z, x, y, c, s=step: (z - 1, x, y, c) if 1 <= z <= Z - s else None
+        )
+        below.append(up)
+        above.append(down)
+    pieces = []
+    for source in range(Z):
+        value = piece
+        for step in range(1, Z):
+            if source + step < Z:
+                value = jnp.where(z == source + step, below[step - 1], value)
+            if source - step >= 0:
+                value = jnp.where(z == source - step, above[step - 1], value)
+        pieces.append(value)
+    return pieces
+
+
+def on_device(grid, latents, buckets, gn_gain, gn_shift, conv_weight, time_bias):
+    frames, rows, cols, chans = latents.shape
+    members = chans // GROUPS
+    taps, shard, _ = conv_weight.shape
+    Y, Z = grid.Y, grid.Z
+    part = shard // Y
+    dp_index, space_index = lax.axis_index("dp"), lax.axis_index("space")
+    z, x = dp_index // 2, dp_index % 2
+    y, c = space_index // 2, space_index % 2
+
+    rounds = [
+        [
+            grid.permute(latents, lambda z, x, y, c, i=i, j=j: (z, c ^ j, (y + i) % Y, x))
+            for j in range(2)
+        ]
+        for i in range(Y)
+    ]
+    other_buckets = grid.permute(
+        buckets, lambda z, x, y, c: (z, c, y, x)
+    )
+    mine = lax.dynamic_slice_in_dim(conv_weight, y * part, part, 1)
+    half = chans // 2
+    piece = lax.dynamic_slice_in_dim(mine, c * half, half, 2)
+    pieces = gather_line(grid, piece, z)
+    held = jnp.concatenate(pieces, axis=1)
+    swapped = grid.permute(held, lambda z, x, y, c: (z, x, y, 1 - c))
+    kernel = jnp.concatenate([pick(c, held, swapped), pick(c, swapped, held)], axis=2)
+
+    full = jnp.concatenate(by_source(grid, rounds, y, x), axis=1)
+    height = full.shape[1]
+    row_ids = jnp.arange(height, dtype=jnp.int32)
+    col_ids = jnp.arange(cols, dtype=jnp.int32)
+
+    def valid_of(ids, sizes):
+        return (
+            (ids[None, :, None] < sizes[:, 0][:, None, None])
+            & (col_ids[None, None, :] < sizes[:, 1][:, None, None])
+        ).astype(jnp.float32)
+
+    valid = valid_of(row_ids, other_buckets)
+    count = (other_buckets[:, 0] * other_buckets[:, 1]).astype(jnp.float32)[:, None] * members
+    values = full.astype(jnp.float32)
+    mask = valid[..., None]
+
+    def per_group(sums):
+        grouped = jnp.sum(sums.reshape(frames, GROUPS, members), axis=2) / count
+        return jnp.repeat(grouped, members, axis=1)[:, None, None, :]
+
+    mean = per_group(jnp.sum(values * mask, axis=(1, 2)))
+    centered = values - mean
+    spread = per_group(jnp.sum(centered * centered * mask, axis=(1, 2)))
+    normed = centered / jnp.sqrt(spread + EPS) * gn_gain + gn_shift
+    act = (mask * jax.nn.silu(normed)).astype(jnp.bfloat16)
+
+    conv = lax.conv_general_dilated(
+        act,
+        kernel.reshape(3, 3, Z * part, chans),
+        (1, 1),
+        ((1, 1), (1, 1)),
+        dimension_numbers=("NHWC", "HWOI", "NHWC"),
+        preferred_element_type=jnp.float32,
+    ).astype(jnp.bfloat16)
+
+    back = []
+    for i in range(Y):
+        row = []
+        for j in range(2):
+            first = rows * (((y + i) % Y) * 2 + (x ^ j))
+            block = lax.dynamic_slice_in_dim(conv, first, rows, 1)
+            row.append(
+                grid.permute(block, lambda z, x, y, c, i=i, j=j: (z, c, (y + i) % Y, x ^ j))
+            )
+        back.append(row)
+    parts = by_source(grid, back, y, c)
+    stacked = jnp.stack(parts).reshape(Y, 2, frames, rows, cols, Z, part)
+    conv_out = jnp.transpose(stacked, (2, 3, 4, 5, 1, 0, 6)).reshape(frames, rows, cols, chans)
+
+    own_valid = valid_of(space_index * rows + jnp.arange(rows, dtype=jnp.int32), buckets)
+    summed = latents.astype(jnp.float32) + own_valid[..., None] * (
         conv_out.astype(jnp.float32) + time_bias[:, None, None, :]
     )
     return summed.astype(jnp.bfloat16)
@@ -76,7 +226,14 @@
         P(None, "dp", None),
         P("dp", None),
     )
-    out_specs = P("dp", "space", None, None)
+    grid = Grid(mesh)
+
+    def body(latents, *rest):
+        whole_frames = latents.size * latents.dtype.itemsize * mesh.shape["space"]
+        if whole_frames > FRAME_BYTES:
+            return row_plan(latents, *rest)
+        return on_device(grid, latents, *rest)
+
     return jax.shard_map(
-        on_device, mesh=mesh, in_specs=in_specs, out_specs=out_specs, check_vma=False
-    )
+        body, mesh=mesh, in_specs=in_specs, out_specs=P("dp", "space", None, None), check_vma=False
+    )

time: 675 us -> 207 us (0.31)
  waiting for transfers between devices: 566 us -> 66.1 us
  other arithmetic: 9.07 us -> 50 us
  starting transfers between devices: 3 us -> 37.1 us
  matrix products: 50.9 us -> 28 us
  blocking collectives: 14.1 us -> 0 us
  between operations: 13.2 us -> 0.4 us
    all_gather x9 -> x0, waiting for transfers between devices: 563 us -> none  [add_tap(): lax.all_gather(panel, 'dp', axis=0, tiled=True)]
    ppermute x2 -> x16, waiting for transfers between devices: 2.55 us -> 66.1 us  [permute(): return lax.ppermute(value, ('dp', 'space'), pairs)]
    dot_general x9 -> x0, matrix products: 50.9 us -> none  [tap_product(): lax.dot_general(window, panel, (((3,), (1,)), ((), ())), preferred_elemen...]
    ppermute x2 -> x16, starting transfers between devices: 2.98 us -> 37.1 us  [permute(): return lax.ppermute(value, ('dp', 'space'), pairs)]
    conv_general_dilated x0 -> x1, matrix products: none -> 28 us  [on_device(): lax.conv_general_dilated(act, kernel.reshape(3, 3, Z * part, chans), (1,...]
    convert_element_type x0 -> x6, local copies, waits for them, and re-layouts: none -> 14.3 us  [the longest x3 13.5 us: on_device(): conv_out.astype(jnp.float32) + time_bias[:, None, None, :]]
    psum x2 -> x0, blocking collectives: 14.1 us -> none  [the longest x1 8.38 us: on_device(): total = lax.psum(jnp.sum(values * weight_mask, axis=(1, 2, 4)), 'space')]
    dynamic_slice x9 -> x1, local copies, waits for them, and re-layouts: 16 us -> 2.89 us  [on_device(): piece = lax.dynamic_slice_in_dim(mine, c * half, half, 2)]
  transfers between devices with their start and end apart: 11 -> 16, of which waited for: 11 -> 5; matrix products, arithmetic and copies ran while one was open for 0% -> 15% of each run, Pallas kernels for 0% -> 0%
where the time goes in v1:
time: 207 us; the launch traced here: 206 us
  waiting for transfers between devices  66.1 us (32%)
  other arithmetic  50 us (24%)
  starting transfers between devices  37.1 us (18%)
  matrix products  28 us (14%)
  local copies, waits for them, and re-layouts  24.7 us (12%)
    ppermute x16, waiting for transfers between devices, permute(): return lax.ppermute(value, ('dp', 'space'), pairs)  66.1 us
    ppermute x16, starting transfers between devices, permute(): return lax.ppermute(value, ('dp', 'space'), pairs)  37.1 us
    conv_general_dilated x1, matrix products, on_device(): lax.conv_general_dilated(act, kernel.reshape(3, 3, Z * part, chans), (1,...  28 us
    convert_element_type x3, local copies, waits for them, and re-layouts, on_device(): conv_out.astype(jnp.float32) + time_bias[:, None, None, :]  13.5 us
    select_n x2, other arithmetic, pick(): return jnp.where(flag == 0, first, second)  8.42 us
    convert_element_type x1, other arithmetic, on_device(): act = (mask * jax.nn.silu(normed)).astype(jnp.bfloat16)  7.23 us
    reduce_sum x1, other arithmetic, on_device(): spread = per_group(jnp.sum(centered * centered * mask, axis=(1, 2)))  6.44 us
    concatenate x1, other arithmetic, on_device(): jnp.concatenate([pick(c, held, swapped), pick(c, swapped, held)], axis=2)  5.64 us
  transfers between devices with their start and end apart: 16, of which 5 were waited for; matrix products, arithmetic and copies ran while one was open for 15% of the time, Pallas kernels for 0%

profile of v1, /device:TPU:0, one launch (start us, length us, event | category | flops | bytes accessed | tf_op | source)
XLA Modules:
  0.0 206.2 jit_solution(12967785570521233567)
XLA Ops:
  0.0 2.9 %constant_dynamic-slice_fusion.4 = bf16[9,80,640]{2,1,0:T(8,128)(2,1)} fusion(bf16[9,160,1280]{2,1,0:T(8,128)(2,1)} %param.10, s32[]{:T(128)S(6)} %select_n.242, s32[]{:T(128)S(6)} %select_n.244), kind=kLoop, calls=%fused_computation.61 | loop fusion | bytes 1843208 | tf_op jit(solution)/shard_map/dynamic_slice | solution.py:158
  2.9 5.9 %collective-permute-start.5 = (bf16[9,80,640]{2,1,0:T(8,128)(2,1)}, bf16[9,80,640]{2,1,0:T(8,128)(2,1)}, u32[]{:S(2)}, u32[]{:S(2)}) collective-permute-start(bf16[9,80,640]{2,1,0:T(8,128)(2,1)} %constant_dynamic-slice_fusion.4), channel_id=1, source_target_pairs={{0,8},{1,9},{2,10},{3,11},{4,12},{5,13},{6,14},{7,15},{8,16},{9,17... | collective-permute-start | bytes 2764808 | tf_op jit(solution)/shard_map/ppermute | solution.py:91
  10.0 2.2 %copy.32 = bf16[6,2,32,1280]{3,1,2,0:T(2,128)(2,1)S(1)} copy(bf16[6,2,32,1280]{3,2,1,0:T(8,128)(2,1)} %param.6) | data formatting | bytes 1966080 | tf_op args[0]
  13.0 2.7 %collective-permute-start.2 = (bf16[6,2,32,1280]{3,1,2,0:T(2,128)(2,1)S(1)}, bf16[6,2,32,1280]{3,1,2,0:T(2,128)(2,1)S(1)}, u32[]{:S(2)}, u32[]{:S(2)}) collective-permute-start(bf16[6,2,32,1280]{3,1,2,0:T(2,128)(2,1)S(1)} %copy.32), channel_id=1, source_target_pairs={{0,4},{1,0},{2,6},{3,2},{4,5},{5,1},{6,7},{7,3},{8,12},{9,8},{10,1... | collective-permute-start | bytes 2949128 | tf_op jit(solution)/shard_map/ppermute | solution.py:91
  19.3 8.4 %collective-permute-done.5 = bf16[9,80,640]{2,1,0:T(8,128)(2,1)} collective-permute-done((bf16[9,80,640]{2,1,0:T(8,128)(2,1)}, bf16[9,80,640]{2,1,0:T(8,128)(2,1)}, u32[]{:S(2)}, u32[]{:S(2)}) %collective-permute-start.5) | collective-permute-done | bytes 921632 | tf_op jit(solution)/shard_map/ppermute | solution.py:91
  27.7 12.4 %collective-permute-start.4 = (bf16[6,2,32,1280]{3,1,2,0:T(2,128)(2,1)S(1)}, bf16[6,2,32,1280]{3,1,2,0:T(2,128)(2,1)S(1)}, u32[]{:S(2)}, u32[]{:S(2)}) collective-permute-start(bf16[6,2,32,1280]{3,1,2,0:T(2,128)(2,1)S(1)} %copy.32), channel_id=1, source_target_pairs={{0,6},{1,2},{2,4},{3,0},{4,7},{5,3},{6,5},{7,1},{8,14},{9,10},{10,... | collective-permute-start | bytes 2949128 | tf_op jit(solution)/shard_map/ppermute | solution.py:91
  43.3 29.9 %collective-permute-done.4 = bf16[6,2,32,1280]{3,1,2,0:T(2,128)(2,1)S(1)} collective-permute-done((bf16[6,2,32,1280]{3,1,2,0:T(2,128)(2,1)S(1)}, bf16[6,2,32,1280]{3,1,2,0:T(2,128)(2,1)S(1)}, u32[]{:S(2)}, u32[]{:S(2)}) %collective-permute-start.4) | collective-permute-done | bytes 983072 | tf_op jit(solution)/shard_map/ppermute | solution.py:91
  76.0 5.0 %fusion.7 = f32[6,1280]{1,0:T(8,128)S(1)} fusion(f32[6,8,32]{1,2,0:T(8,128)S(1)} %and_convert_fusion, bf16[6,2,32,1280]{3,1,2,0:T(2,128)(2,1)S(1)} %bitcast.57, bf16[6,2,32,1280]{3,1,2,0:T(2,128)(2,1)S(1)} %bitcast.60, bf16[6,2,32,1280]{3,1,2,0:T(2,128)(2,1)S(1)} %bitcast.63, bf16[6,2,32,1280]{3,1,2,0:T(2,128)(2,1)S(1)} %bitcast.54), kind=kLoop, calls=%fused_computation.10 | loop fusion | flops 19653120 | bytes 3969024 | tf_op jit(solution)/shard_map/reduce_sum | solution.py:184
  84.5 6.4 %fusion.4 = f32[6,1280]{1,0:T(8,128)S(1)} fusion(f32[6,1280]{1,0:T(8,128)S(1)} %sub.25, f32[6,8,32]{1,2,0:T(8,128)S(1)} %and_convert_fusion, bf16[6,2,32,1280]{3,1,2,0:T(2,128)(2,1)S(1)} %bitcast.58, bf16[6,2,32,1280]{3,1,2,0:T(2,128)(2,1)S(1)} %bitcast.61, bf16[6,2,32,1280]{3,1,2,0:T(2,128)(2,1)} %bitcast.64, bf16[6,2,32,1280]{3,1,2,0:T(2,128)(2,1)S(1)} %bitcast.55), kind=kLoop, calls=%fused_computation.7 | loop fusion | flops 23585280 | bytes 3999744 | tf_op jit(solution)/shard_map/reduce_sum | solution.py:186
  91.5 14.5 %collective-permute-done.10 = bf16[9,80,640]{2,1,0:T(8,128)(2,1)} collective-permute-done((bf16[9,80,640]{2,1,0:T(8,128)(2,1)}, bf16[9,80,640]{2,1,0:T(8,128)(2,1)}, u32[]{:S(2)}, u32[]{:S(2)}) %collective-permute-start.10) | collective-permute-done | bytes 921632 | tf_op jit(solution)/shard_map/ppermute | solution.py:91
  106.1 4.5 %select_select_fusion.3 = (bf16[9,80,640]{2,1,0:T(8,128)(2,1)S(1)}, bf16[9,80,640]{2,1,0:T(8,128)(2,1)S(1)}, bf16[9,80,640]{2,1,0:T(8,128)(2,1)S(1)}, bf16[9,80,640]{2,1,0:T(8,128)(2,1)S(1)}) fusion(bf16[9,80,640]{2,1,0:T(8,128)(2,1)} %collective-permute-done.7, bf16[9,80,640]{2,1,0:T(8,128)(2,1)} %collective-permute-done.6, ...), kind=kLoop, calls=%fused_computation.36 | loop fusion | flops 5529600 | bytes 10137612 | tf_op jit(solution)/shard_map/jit(_where)/select_n | solution.py:129
  110.6 4.1 %pad_maximum_fusion.2 = bf16[9,320,640]{2,1,0:T(8,128)(2,1)} fusion(bf16[9,80,640]{2,1,0:T(8,128)(2,1)S(1)} %get-tuple-element.14, bf16[9,80,640]{2,1,0:T(8,128)(2,1)S(1)} %get-tuple-element.13, bf16[9,80,640]{2,1,0:T(8,128)(2,1)S(1)} %get-tuple-element.12, bf16[9,80,640]{2,1,0:T(8,128)(2,1)S(1)} %get-tuple-element.11), kind=kLoop, calls=%fused_computation.19 | loop fusion | flops 14745600 | bytes 7372800 | tf_op jit(solution)/shard_map/concatenate | solution.py:160
  114.7 7.2 %fusion.12 = bf16[8,6,32,1280]{3,0,2,1:T(8,128)(2,1)S(1)} fusion(f32[1280]{0:T(1024)S(1)} %copy-done.10, f32[1280]{0:T(1024)S(1)} %copy-done.11, f32[6,1280]{1,0:T(8,128)S(1)} %sqrt.13, f32[6,1280]{1,0:T(8,128)S(1)} %sub.25, f32[6,8,32]{1,2,0:T(8,128)S(1)} %and_convert_fusion, bf16[6,2,32,1280]{3,1,2,0:T(2,128)(2,1)S(1)} %bitcast.59, ...), kind=kLoop, calls=%fused_computation.17 | loop fusion | flops 35389440 | bytes 7942144 | tf_op jit(solution)/shard_map/convert_element_type | solution.py:188
  123.7 4.4 %fusion.8 = bf16[8,6,8,7,1280]{4,0,3,2,1:T(8,128)(2,1)} fusion(bf16[8,6,7,2,1280]{4,0,3,2,1:T(8,128)(2,1)} %slice.26, bf16[8,6,8,5,1280]{4,0,3,2,1:T(8,128)(2,1)S(1)} %bitcast.53), kind=kLoop, calls=%fused_computation.13 | loop fusion | flops 20643840 | bytes 13516800 | tf_op jit(solution)/shard_map/conv_general_dilated | solution.py:190
  128.1 6.6 %broadcast_select_fusion.1 = (bf16[9,320,640]{2,1,0:T(8,128)(2,1)S(1)}, bf16[9,320,640]{2,1,0:T(8,128)(2,1)}) fusion(bf16[9,320,640]{2,1,0:T(8,128)(2,1)} %collective-permute-done.11, pred[]{:T(512)S(6)} %eq.62, bf16[9,80,640]{2,1,0:T(8,128)(2,1)} %copy-done.6, bf16[9,80,640]{2,1,0:T(8,128)(2,1)} %copy-done.5, bf16[9,80,640]{2,1,0:T(8,128)(2,1)} %copy-done.4, ...), kind=kLoop, calls=%fused_computation.21 | loop fusion | flops 18432000 | bytes 14745601 | tf_op jit(solution)/shard_map/jit(_where)/select_n | solution.py:95
  134.7 5.6 %pad_maximum_fusion = bf16[9,320,1280]{2,1,0:T(8,128)(2,1)} fusion(bf16[9,320,640]{2,1,0:T(8,128)(2,1)} %get-tuple-element.6, bf16[9,320,640]{2,1,0:T(8,128)(2,1)S(1)} %get-tuple-element.5), kind=kLoop, calls=%fused_computation.12 | loop fusion | flops 14745600 | bytes 14745600 | tf_op jit(solution)/shard_map/concatenate | solution.py:162
  140.3 28.0 %select_convert_fusion = bf16[8,48,5,320]{3,1,2,0:T(8,128)(2,1)S(1)} fusion(bf16[3,3,320,1280]{3,2,1,0:T(8,128)(2,1)} %bitcast.67, bf16[8,6,8,7,1280]{4,0,3,2,1:T(8,128)(2,1)} %fusion.8, pred[48,5]{0,1:T(8,128)(4,1)S(1)} %copy-done.12), kind=kOutput, calls=%fused_computation.22 | convolution fusion | flops 12977356800 | bytes 15483120 | tf_op jit(solution)/shard_map/conv_general_dilated | solution.py:190
  170.9 2.2 %collective-permute-start.13 = (bf16[6,2,32,320]{3,2,1,0:T(8,128)(2,1)S(1)}, bf16[6,2,32,320]{3,2,1,0:T(8,128)(2,1)S(1)}, u32[]{:S(2)}, u32[]{:S(2)}) collective-permute-start(bf16[6,2,32,320]{3,2,1,0:T(8,128)(2,1)S(1)} %bitcast.74), channel_id=1, source_target_pairs={{0,1},{1,5},{2,3},{3,7},{4,0},{5,4},{6,2},{7,6},{8,9},{9,13},{10,1... | collective-permute-start | bytes 737288 | tf_op jit(solution)/shard_map/ppermute | solution.py:91
  175.8 6.2 %collective-permute-done.13 = bf16[6,2,32,320]{3,2,1,0:T(8,128)(2,1)S(1)} collective-permute-done((bf16[6,2,32,320]{3,2,1,0:T(8,128)(2,1)S(1)}, bf16[6,2,32,320]{3,2,1,0:T(8,128)(2,1)S(1)}, u32[]{:S(2)}, u32[]{:S(2)}) %collective-permute-start.13) | collective-permute-done | bytes 245792 | tf_op jit(solution)/shard_map/ppermute | solution.py:91
  182.0 7.0 %collective-permute-done.15 = bf16[6,2,32,320]{3,2,1,0:T(8,128)(2,1)S(1)} collective-permute-done((bf16[6,2,32,320]{3,2,1,0:T(8,128)(2,1)S(1)}, bf16[6,2,32,320]{3,2,1,0:T(8,128)(2,1)S(1)}, u32[]{:S(2)}, u32[]{:S(2)}) %collective-permute-start.15) | collective-permute-done | bytes 245792 | tf_op jit(solution)/shard_map/ppermute | solution.py:91
  189.5 3.2 %reshape.162 = f32[2,2,6,2,32,4,80]{6,5,4,3,2,1,0:T(4,128)} reshape(f32[4,6,2,32,320]{4,3,2,1,0:T(8,128)S(1)} %maximum_convert_fusion) | data formatting | bytes 3932160 | tf_op jit(solution)/shard_map/convert_element_type | solution.py:215
  192.7 4.3 %copy.39 = f32[6,2,32,4,2,2,80]{6,5,4,3,2,1,0:T(2,128)S(1)} copy(f32[6,2,32,4,2,2,80]{6,3,2,1,0,4,5:T(4,128)} %bitcast.66) | data formatting | bytes 3932160 | tf_op jit(solution)/shard_map/convert_element_type | solution.py:215
  197.0 6.0 %reshape.158 = f32[6,2,32,1280]{3,2,1,0:T(8,128)} reshape(f32[6,2,32,4,2,2,80]{6,5,4,3,2,1,0:T(2,128)S(1)} %copy.39) | data formatting | bytes 3932160 | tf_op jit(solution)/shard_map/convert_element_type | solution.py:215
  203.1 3.1 %add_convert_fusion = bf16[6,2,32,1280]{3,2,1,0:T(8,128)(2,1)} fusion(f32[6,2,32,1280]{3,2,1,0:T(8,128)} %reshape.158, bf16[6,2,32,1280]{3,2,1,0:T(8,128)(2,1)} %param.6, f32[6,1280]{1,0:T(8,128)S(1)} %copy-done.9, f32[6,2,32]{2,1,0:T(2,128)S(1)} %and_convert_fusion.1), kind=kLoop, calls=%fused_computation.23 | loop fusion | flops 2457600 | bytes 3964416 | tf_op jit(solution)/shard_map/convert_element_type | solution.py:217
  (81 shorter events, 23.0 us)
Async XLA Ops:
  2.9 24.8 %collective-permute-start.5 = (bf16[9,80,640]{2,1,0:T(8,128)(2,1)}, bf16[9,80,640]{2,1,0:T(8,128)(2,1)}, u32[]{:S(2)}, u32[]{:S(2)}) collective-permute-start(bf16[9,80,640]{2,1,0:T(8,128)(2,1)} %constant_dynamic-slice_fusion.4), channel_id=1, source_target_pairs={{0,8},{1,9},{2,10},{3,11},{4,12},{5,13},{6,14},{7,15},{8,16},{9,17... | collective-permute-start | bytes 2764808 | tf_op jit(solution)/shard_map/ppermute | solution.py:91
  8.7 31.6 %collective-permute-start.8 = (bf16[9,80,640]{2,1,0:T(8,128)(2,1)}, bf16[9,80,640]{2,1,0:T(8,128)(2,1)}, u32[]{:S(2)}, u32[]{:S(2)}) collective-permute-start(bf16[9,80,640]{2,1,0:T(8,128)(2,1)} %constant_dynamic-slice_fusion.4), channel_id=1, source_target_pairs={{8,0},{9,1},{10,2},{11,3},{12,4},{13,5},{14,6},{15,7},{16,8},{17,9... | collective-permute-start | bytes 2764808 | tf_op jit(solution)/shard_map/ppermute | solution.py:91
  12.3 29.8 %collective-permute-start.1 = (bf16[6,2,32,1280]{3,1,2,0:T(2,128)(2,1)S(1)}, bf16[6,2,32,1280]{3,1,2,0:T(2,128)(2,1)S(1)}, u32[]{:S(2)}, u32[]{:S(2)}) collective-permute-start(bf16[6,2,32,1280]{3,1,2,0:T(2,128)(2,1)S(1)} %copy.32), channel_id=1, source_target_pairs={{0,0},{1,4},{2,2},{3,6},{4,1},{5,5},{6,3},{7,7},{8,8},{9,12},{10,1... | collective-permute-start | bytes 2949128 | tf_op jit(solution)/shard_map/ppermute | solution.py:91
  13.0 30.3 %collective-permute-start.2 = (bf16[6,2,32,1280]{3,1,2,0:T(2,128)(2,1)S(1)}, bf16[6,2,32,1280]{3,1,2,0:T(2,128)(2,1)S(1)}, u32[]{:S(2)}, u32[]{:S(2)}) collective-permute-start(bf16[6,2,32,1280]{3,1,2,0:T(2,128)(2,1)S(1)} %copy.32), channel_id=1, source_target_pairs={{0,4},{1,0},{2,6},{3,2},{4,5},{5,1},{6,7},{7,3},{8,12},{9,8},{10,1... | collective-permute-start | bytes 2949128 | tf_op jit(solution)/shard_map/ppermute | solution.py:91
  15.7 2.2 %collective-permute-start = (s32[6,2]{0,1:T(2,128)}, s32[6,2]{0,1:T(2,128)S(1)}, u32[]{:S(2)}, u32[]{:S(2)}) collective-permute-start(s32[6,2]{0,1:T(2,128)} %param.7), channel_id=1, source_target_pairs={{0,0},{1,4},{2,2},{3,6},{4,1},{5,5},{6,3},{7,7},{8,8},{9,12},{10,1... | collective-permute-start | bytes 152 | tf_op jit(solution)/shard_map/ppermute | solution.py:91
  17.9 25.5 %collective-permute-start.3 = (bf16[6,2,32,1280]{3,1,2,0:T(2,128)(2,1)S(1)}, bf16[6,2,32,1280]{3,1,2,0:T(2,128)(2,1)S(1)}, u32[]{:S(2)}, u32[]{:S(2)}) collective-permute-start(bf16[6,2,32,1280]{3,1,2,0:T(2,128)(2,1)S(1)} %copy.32), channel_id=1, source_target_pairs={{0,2},{1,6},{2,0},{3,4},{4,3},{5,7},{6,1},{7,5},{8,10},{9,14},{10,... | collective-permute-start | bytes 2949128 | tf_op jit(solution)/shard_map/ppermute | solution.py:91
  27.7 45.5 %collective-permute-start.4 = (bf16[6,2,32,1280]{3,1,2,0:T(2,128)(2,1)S(1)}, bf16[6,2,32,1280]{3,1,2,0:T(2,128)(2,1)S(1)}, u32[]{:S(2)}, u32[]{:S(2)}) collective-permute-start(bf16[6,2,32,1280]{3,1,2,0:T(2,128)(2,1)S(1)} %copy.32), channel_id=1, source_target_pairs={{0,6},{1,2},{2,4},{3,0},{4,7},{5,3},{6,5},{7,1},{8,14},{9,10},{10,... | collective-permute-start | bytes 2949128 | tf_op jit(solution)/shard_map/ppermute | solution.py:91
  40.4 40.8 %collective-permute-start.6 = (bf16[9,80,640]{2,1,0:T(8,128)(2,1)}, bf16[9,80,640]{2,1,0:T(8,128)(2,1)}, u32[]{:S(2)}, u32[]{:S(2)}) collective-permute-start(bf16[9,80,640]{2,1,0:T(8,128)(2,1)} %collective-permute-done.5), channel_id=1, source_target_pairs={{8,16},{9,17},{10,18},{11,19},{12,20},{13,21},{14,22},{15,23},{16,... | collective-permute-start | bytes 2764808 | tf_op jit(solution)/shard_map/ppermute | solution.py:91
  42.0 31.2 %copy-start.7 = (bf16[6,2,32,1280]{3,1,2,0:T(2,128)(2,1)}, bf16[6,2,32,1280]{3,1,2,0:T(2,128)(2,1)S(1)}, u32[]{:S(2)}) copy-start(bf16[6,2,32,1280]{3,1,2,0:T(2,128)(2,1)S(1)} %collective-permute-done.1) | copy-start | bytes 2949124
  42.0 40.8 %collective-permute-start.9 = (bf16[9,80,640]{2,1,0:T(8,128)(2,1)}, bf16[9,80,640]{2,1,0:T(8,128)(2,1)}, u32[]{:S(2)}, u32[]{:S(2)}) collective-permute-start(bf16[9,80,640]{2,1,0:T(8,128)(2,1)} %collective-permute-done.8), channel_id=1, source_target_pairs={{8,0},{9,1},{10,2},{11,3},{12,4},{13,5},{14,6},{15,7},{16,8},{17,9... | collective-permute-start | bytes 2764808 | tf_op jit(solution)/shard_map/ppermute | solution.py:91
  43.3 29.9 %copy-start.8 = (bf16[6,2,32,1280]{3,1,2,0:T(2,128)(2,1)}, bf16[6,2,32,1280]{3,1,2,0:T(2,128)(2,1)S(1)}, u32[]{:S(2)}) copy-start(bf16[6,2,32,1280]{3,1,2,0:T(2,128)(2,1)S(1)} %collective-permute-done.2) | copy-start | bytes 2949124
  81.2 10.4 %collective-permute-start.7 = (bf16[9,80,640]{2,1,0:T(8,128)(2,1)}, bf16[9,80,640]{2,1,0:T(8,128)(2,1)}, u32[]{:S(2)}, u32[]{:S(2)}) collective-permute-start(bf16[9,80,640]{2,1,0:T(8,128)(2,1)} %collective-permute-done.6), channel_id=1, source_target_pairs={{16,24},{17,25},{18,26},{19,27},{20,28},{21,29},{22,30},{23,31}} | collective-permute-start | bytes 2764808 | tf_op jit(solution)/shard_map/ppermute | solution.py:91
  82.8 23.3 %collective-permute-start.10 = (bf16[9,80,640]{2,1,0:T(8,128)(2,1)}, bf16[9,80,640]{2,1,0:T(8,128)(2,1)}, u32[]{:S(2)}, u32[]{:S(2)}) collective-permute-start(bf16[9,80,640]{2,1,0:T(8,128)(2,1)} %collective-permute-done.9), channel_id=1, source_target_pairs={{8,0},{9,1},{10,2},{11,3},{12,4},{13,5},{14,6},{15,7}} | collective-permute-start | bytes 2764808 | tf_op jit(solution)/shard_map/ppermute | solution.py:91
  91.5 23.2 %copy-start.1 = (bf16[6,8,8,1280]{3,1,2,0:T(8,128)(2,1)S(1)}, bf16[6,8,8,1280]{3,1,2,0:T(8,128)(2,1)}, u32[]{:S(2)}) copy-start(bf16[6,8,8,1280]{3,1,2,0:T(8,128)(2,1)} %copy-done) | copy-start | bytes 2949124
  91.5 23.2 %copy-start.10 = (f32[1280]{0:T(1024)S(1)}, f32[1280]{0:T(1024)}, u32[]{:S(2)}) copy-start(f32[1280]{0:T(1024)} %param.9) | copy-start | bytes 15364
  91.5 23.2 %copy-start.11 = (f32[1280]{0:T(1024)S(1)}, f32[1280]{0:T(1024)}, u32[]{:S(2)}) copy-start(f32[1280]{0:T(1024)} %param.8) | copy-start | bytes 15364
  114.7 13.4 %collective-permute-start.11 = (bf16[9,320,640]{2,1,0:T(8,128)(2,1)}, bf16[9,320,640]{2,1,0:T(8,128)(2,1)}, u32[]{:S(2)}, u32[]{:S(2)}) collective-permute-start(bf16[9,320,640]{2,1,0:T(8,128)(2,1)} %pad_maximum_fusion.2), channel_id=1, source_target_pairs={{0,1},{1,0},{2,3},{3,2},{4,5},{5,4},{6,7},{7,6},{8,9},{9,8},{10,11... | collective-permute-start | bytes 11059208 | tf_op jit(solution)/shard_map/ppermute | solution.py:91
  123.7 4.4 %copy-start.3 = (bf16[9,80,640]{2,1,0:T(8,128)(2,1)S(1)}, bf16[9,80,640]{2,1,0:T(8,128)(2,1)}, u32[]{:S(2)}) copy-start(bf16[9,80,640]{2,1,0:T(8,128)(2,1)} %copy-done.2) | copy-start | bytes 2764804
  134.7 5.6 %copy-start.12 = (pred[48,5]{0,1:T(8,128)(4,1)S(1)}, pred[48,5]{0,1:T(8,128)(4,1)}, u32[]{:S(2)}) copy-start(pred[48,5]{0,1:T(8,128)(4,1)} %constant.120) | copy-start | bytes 724
  170.2 5.7 %collective-permute-start.12 = (bf16[6,2,32,320]{3,2,1,0:T(8,128)(2,1)S(1)}, bf16[6,2,32,320]{3,2,1,0:T(8,128)(2,1)S(1)}, u32[]{:S(2)}, u32[]{:S(2)}) collective-permute-start(bf16[6,2,32,320]{3,2,1,0:T(8,128)(2,1)S(1)} %bitcast.73), channel_id=1, source_target_pairs={{0,0},{1,4},{2,2},{3,6},{4,1},{5,5},{6,3},{7,7},{8,8},{9,12},{10,1... | collective-permute-start | bytes 737288 | tf_op jit(solution)/shard_map/ppermute | solution.py:91
  170.9 11.1 %collective-permute-start.13 = (bf16[6,2,32,320]{3,2,1,0:T(8,128)(2,1)S(1)}, bf16[6,2,32,320]{3,2,1,0:T(8,128)(2,1)S(1)}, u32[]{:S(2)}, u32[]{:S(2)}) collective-permute-start(bf16[6,2,32,320]{3,2,1,0:T(8,128)(2,1)S(1)} %bitcast.74), channel_id=1, source_target_pairs={{0,1},{1,5},{2,3},{3,7},{4,0},{5,4},{6,2},{7,6},{8,9},{9,13},{10,1... | collective-permute-start | bytes 737288 | tf_op jit(solution)/shard_map/ppermute | solution.py:91
  173.2 8.9 %collective-permute-start.14 = (bf16[6,2,32,320]{3,2,1,0:T(8,128)(2,1)S(1)}, bf16[6,2,32,320]{3,2,1,0:T(8,128)(2,1)S(1)}, u32[]{:S(2)}, u32[]{:S(2)}) collective-permute-start(bf16[6,2,32,320]{3,2,1,0:T(8,128)(2,1)S(1)} %bitcast.75), channel_id=1, source_target_pairs={{0,2},{1,6},{2,0},{3,4},{4,3},{5,7},{6,1},{7,5},{8,10},{9,14},{10,... | collective-permute-start | bytes 737288 | tf_op jit(solution)/shard_map/ppermute | solution.py:91
  174.5 14.6 %collective-permute-start.15 = (bf16[6,2,32,320]{3,2,1,0:T(8,128)(2,1)S(1)}, bf16[6,2,32,320]{3,2,1,0:T(8,128)(2,1)S(1)}, u32[]{:S(2)}, u32[]{:S(2)}) collective-permute-start(bf16[6,2,32,320]{3,2,1,0:T(8,128)(2,1)S(1)} %bitcast.76), channel_id=1, source_target_pairs={{0,3},{1,7},{2,1},{3,5},{4,2},{5,6},{6,0},{7,4},{8,11},{9,15},{10,... | collective-permute-start | bytes 737288 | tf_op jit(solution)/shard_map/ppermute | solution.py:91
  192.7 10.4 %copy-start.9 = (f32[6,1280]{1,0:T(8,128)S(1)}, f32[6,1280]{1,0:T(8,128)}, u32[]{:S(2)}) copy-start(f32[6,1280]{1,0:T(8,128)} %param.11) | copy-start | bytes 92164
  (5 other events, 17.3 us)

commit v2 on v0

--- a/solution.py
+++ b/solution.py
@@ -1,12 +1,15 @@
+import functools
+
 import jax
 import jax.numpy as jnp
 from jax import lax
+from jax.experimental import pallas as pl
+from jax.experimental.pallas import tpu as pltpu
 from jax.sharding import PartitionSpec as P
 
 GROUPS = 32
-
-
-eps = 1e-05
+EPS = 1e-05
+FRAME_BYTES = 8 << 20
 
 
 def with_halo(x, sides, width):
@@ -28,7 +31,7 @@
     )
 
 
-def on_device(latents, buckets, gn_gain, gn_shift, conv_weight, time_bias):
+def row_plan(latents, buckets, gn_gain, gn_shift, conv_weight, time_bias):
     frames, rows, cols, chans = latents.shape
     members = chans // GROUPS
     row_ids = lax.axis_index("space") * rows + jnp.arange(rows, dtype=jnp.int32)
@@ -44,7 +47,7 @@
     mean = total / count
     centered = values - mean[:, None, None, :, None]
     spread = lax.psum(jnp.sum(centered * centered * weight_mask, axis=(1, 2, 4)), "space") / count
-    normed = (centered / jnp.sqrt(spread[:, None, None, :, None] + eps)).reshape(
+    normed = (centered / jnp.sqrt(spread[:, None, None, :, None] + EPS)).reshape(
         frames, rows, cols, chans
     )
     normed = normed * gn_gain + gn_shift
@@ -65,6 +68,515 @@
         conv_out.astype(jnp.float32) + time_bias[:, None, None, :]
     )
     return summed.astype(jnp.bfloat16)
+
+
+class Grid:
+    def __init__(self, mesh):
+        dp, space = mesh.shape["dp"], mesh.shape["space"]
+        self.X = self.C = 2
+        self.Z, self.Y = dp // 2, space // 2
+        self.places = [
+            (z, x, y, c)
+            for z in range(self.Z)
+            for x in range(2)
+            for y in range(self.Y)
+            for c in range(2)
+        ]
+
+    def linear(self, z, x, y, c):
+        return ((z * 2 + x) * self.Y + y) * 2 + c
+
+    def permute(self, value, target):
+        pairs = []
+        for place in self.places:
+            goal = target(*place)
+            if goal is not None:
+                pairs.append((self.linear(*place), self.linear(*goal)))
+        return lax.ppermute(value, ("dp", "space"), pairs)
+
+
+LANES = 128
+ANY = pl.BlockSpec(memory_space=pl.ANY)
+VMEM = pl.BlockSpec(memory_space=pltpu.VMEM)
+SMEM = pl.BlockSpec(memory_space=pltpu.SMEM)
+
+
+def params(mib):
+    return pltpu.CompilerParams(vmem_limit_bytes=mib << 20)
+
+
+def start_all(pairs, sems):
+    copies = [pltpu.make_async_copy(src, dst, sems.at[n]) for n, (src, dst) in enumerate(pairs)]
+    for copy in copies:
+        copy.start()
+    return copies
+
+
+def piece_kernel(part, cuts, where, weight, *refs):
+    outs, sems = refs[:-1], refs[-1]
+    half = weight.shape[2] // 2
+    rows = pl.ds(pl.multiple_of(where[2] * part, part), part)
+    lanes = pl.ds(pl.multiple_of(where[3] * half, half), half)
+    pairs = [
+        (weight.at[pl.ds(first, count), rows, lanes], out)
+        for (first, count), out in zip(cuts, outs)
+    ]
+    for copy in start_all(pairs, sems):
+        copy.wait()
+
+
+def own_pieces(where, weight, part, cuts):
+    half = weight.shape[2] // 2
+    return pl.pallas_call(
+        functools.partial(piece_kernel, part, cuts),
+        out_shape=[jax.ShapeDtypeStruct((n, part, half), weight.dtype) for _, n in cuts],
+        in_specs=[SMEM, ANY],
+        out_specs=[ANY] * len(cuts),
+        scratch_shapes=[pltpu.SemaphoreType.DMA((len(cuts),))],
+        compiler_params=params(4),
+        cost_estimate=pl.CostEstimate(flops=0, transcendentals=0, bytes_accessed=4 << 20),
+        name="own_pieces",
+    )(where, weight)
+
+
+def exact_dot(value, ones):
+    total = None
+    for _ in range(3):
+        top = value.astype(jnp.bfloat16)
+        term = jnp.dot(top, ones, preferred_element_type=jnp.float32)
+        total = term if total is None else total + term
+        value = value - top.astype(jnp.float32)
+    return total
+
+
+def act_kernel(begin, where, sizes, gain, shift, group, group_t, *refs):
+    rounds, act, sums, scale = refs[:4], refs[4], refs[5], refs[6]
+    frames, rows, cols, chans = rounds[0].shape
+    members = chans // GROUPS
+    x, y = where[1], where[2]
+    tiles = chans // LANES
+    first_row = [rows * (2 * (y ^ (k // 2)) + (x ^ (k % 2))) for k in range(4)]
+    col_ids = lax.broadcasted_iota(jnp.int32, (cols, LANES), 0)
+
+    def limit(f, k, r):
+        return jnp.where(first_row[k] + r < sizes[begin + f, 0], sizes[begin + f, 1], 0)
+
+    def fold(v):
+        return jnp.sum(v.reshape(cols // 8, 8, LANES), axis=0)
+
+    def keep(kind, value):
+        for f in range(frames):
+            scale[8 * kind + f] = value[f : f + 1]
+
+    sums[...] = jnp.zeros_like(sums)
+
+    def add_sums(f, _):
+        masks = [[col_ids < limit(f, k, r) for r in range(rows)] for k in range(4)]
+        for t in range(tiles):
+            lanes = slice(t * LANES, (t + 1) * LANES)
+            total = jnp.zeros((8, LANES), jnp.float32)
+            for k in range(4):
+                for r in range(rows):
+                    v = rounds[k][f, r, :, lanes].astype(jnp.float32)
+                    total += fold(jnp.where(masks[k][r], v, 0.0))
+            sums[f, :, lanes] = total
+        return 0
+
+    lax.fori_loop(0, frames, add_sums, 0)
+    ids = lax.broadcasted_iota(jnp.int32, (8, LANES), 0)
+    count = jnp.ones((8, LANES), jnp.float32)
+    for f in range(frames):
+        cells = (sizes[begin + f, 0] * sizes[begin + f, 1] * members).astype(jnp.float32)
+        count = jnp.where(ids == f, cells, count)
+    mean = exact_dot(jnp.sum(sums[...], axis=1), group[...]) / count
+    keep(0, exact_dot(mean, group_t[...]))
+
+    def add_squares(f, _):
+        masks = [[col_ids < limit(f, k, r) for r in range(rows)] for k in range(4)]
+        for t in range(tiles):
+            lanes = slice(t * LANES, (t + 1) * LANES)
+            middle = scale[f, :, lanes]
+            total = jnp.zeros((8, LANES), jnp.float32)
+            for k in range(4):
+                for r in range(rows):
+                    v = rounds[k][f, r, :, lanes].astype(jnp.float32) - middle
+                    total += fold(jnp.where(masks[k][r], v * v, 0.0))
+            sums[f, :, lanes] = total
+        return 0
+
+    lax.fori_loop(0, frames, add_squares, 0)
+    spread = exact_dot(jnp.sum(sums[...], axis=1), group[...]) / count
+    keep(1, exact_dot(1.0 / jnp.sqrt(spread + EPS), group_t[...]) * gain[...])
+
+    def activate(f, _):
+        for t in range(tiles):
+            lanes = slice(t * LANES, (t + 1) * LANES)
+            middle = scale[f, :, lanes]
+            factor = scale[8 + f, :, lanes]
+            offset = shift[:, lanes]
+            for k in range(4):
+                for r in range(rows):
+                    v = rounds[k][f, r, :, lanes].astype(jnp.float32)
+                    v = (v - middle) * factor + offset
+                    v = v / (1.0 + jnp.exp(-v))
+                    v = jnp.where(col_ids < limit(f, k, r), v, 0.0)
+                    act[first_row[k] + r + 1, f, :, lanes] = v.astype(jnp.bfloat16)
+        return 0
+
+    lax.fori_loop(0, frames, activate, 0)
+    edge = jnp.zeros((frames, cols, chans), jnp.bfloat16)
+    act[0] = edge
+    act[act.shape[0] - 1] = edge
+
+
+def group_matrix(chans):
+    member = jnp.arange(chans, dtype=jnp.int32)[:, None] // (chans // GROUPS)
+    return (member == jnp.arange(LANES, dtype=jnp.int32)[None, :]).astype(jnp.bfloat16)
+
+
+def activation(where, sizes, gain, shift, group, rounds, begin):
+    frames, rows, cols, chans = rounds[0].shape
+    elements = 4 * rounds[0].size
+    return pl.pallas_call(
+        functools.partial(act_kernel, begin),
+        out_shape=jax.ShapeDtypeStruct((4 * rows + 2, frames, cols, chans), jnp.bfloat16),
+        in_specs=[SMEM, SMEM] + [VMEM] * 8,
+        out_specs=VMEM,
+        scratch_shapes=[
+            pltpu.VMEM((8, 8, chans), jnp.float32),
+            pltpu.VMEM((16, 1, chans), jnp.float32),
+        ],
+        compiler_params=params(8),
+        cost_estimate=pl.CostEstimate(
+            flops=2 * elements, transcendentals=0, bytes_accessed=elements
+        ),
+        name="activation",
+    )(where, sizes, gain[None, :], shift[None, :], *group, *rounds)
+
+
+def shifted_sum(left, middle, right, cols):
+    size = middle.shape[0]
+    col = lax.broadcasted_iota(jnp.int32, middle.shape, 0) % cols
+    left = jnp.where(col == 0, 0.0, pltpu.roll(left, 1, 0))
+    right = jnp.where(col == cols - 1, 0.0, pltpu.roll(right, size - 1, 0))
+    return middle + left + right
+
+
+def conv_rows(act, weight, first_tap, taps, base, chunk, line, cols):
+    columns = []
+    for dc in range(3):
+        total = None
+        for dr in range(3):
+            tap = 3 * dr + dc - first_tap
+            if not 0 <= tap < taps:
+                continue
+            window = act[pl.ds(pl.multiple_of(base + dr * line, cols), chunk), :]
+            term = lax.dot_general(
+                window,
+                weight[tap],
+                (((1,), (1,)), ((), ())),
+                preferred_element_type=jnp.float32,
+            )
+            total = term if total is None else total + term
+        columns.append(total)
+    return shifted_sum(*columns, cols)
+
+
+def conv_kernel(rows, cols, part, first_tap, counts, halves, own_taps, more, where, *refs):
+    takes_sums, gives_sums, unread = more
+    z, x, y, c = (where[n] for n in range(4))
+    acts, refs = refs[:halves], refs[halves:]
+    own, refs = (refs[0], refs[1:]) if own_taps else (None, refs)
+    given, refs = refs[: 2 * len(counts)], refs[2 * len(counts) :]
+    sums_in, refs = (refs[:halves], refs[halves:]) if takes_sums else (None, refs)
+    refs = refs[unread:]
+    outs, refs = refs[: halves if gives_sums else 4], refs[halves if gives_sums else 4 :]
+    weight, refs = refs[0], refs[1:]
+    results, sems = refs[:-1], refs[-1]
+    half = weight.shape[2] // 2
+    taps, width = weight.shape[0], weight.shape[1]
+    pairs = []
+    if own_taps:
+        low = jnp.where(z < 2, 0, 1)
+        places = [
+            jnp.where(z == 0, 1, z - 1) - low,
+            jnp.where(z < 3, 2, 0),
+        ]
+        pairs.append(
+            (
+                own.at[
+                    pl.ds(first_tap, own_taps), pl.ds(pl.multiple_of(y * part, part), part), :
+                ],
+                weight.at[:, pl.ds(pl.multiple_of((z - low) * part, part), part), :],
+            )
+        )
+    else:
+        places = [0]
+    for n, (tap, size, slot) in enumerate(counts):
+        goal = pl.ds(pl.multiple_of(places[slot] * part, part), part)
+        for m, side in enumerate((c, 1 - c)):
+            lanes = pl.ds(pl.multiple_of(side * half, half), half)
+            pairs.append((given[2 * n + m], weight.at[pl.ds(tap, size), goal, lanes]))
+    for copy in start_all(pairs, sems):
+        copy.wait()
+    for n, act in enumerate(acts):
+        frames = act.shape[0] // (10 * cols) if act.shape[0] % (10 * cols) == 0 else 0
+        line = frames * cols
+        size = act.shape[0] - 2 * line
+        chunk = size // 2
+
+        def body(m, _, act=act, n=n, frames=frames, line=line, chunk=chunk):
+            base = pl.multiple_of(m * chunk, chunk)
+            value = conv_rows(act, weight, first_tap, taps, base, chunk, line, cols)
+            if takes_sums:
+                value += sums_in[n][pl.ds(base, chunk), :]
+            if gives_sums:
+                outs[n][pl.ds(base, chunk), :] = value
+            else:
+                value = value.astype(jnp.bfloat16).reshape(chunk // line, frames, cols, width)
+                results[n][pl.ds(m * (chunk // line), chunk // line)] = value
+            return 0
+
+        lax.fori_loop(0, size // chunk, body, 0)
+    if gives_sums:
+        return
+    for k, out in enumerate(outs):
+        first = rows * (2 * (y ^ (k // 2)) + (x ^ (k % 2)))
+        for n, result in enumerate(results):
+            frames = result.shape[1]
+            out[:, n * frames : (n + 1) * frames, :, 0:width] = result[pl.ds(first, rows)]
+        if out.shape[3] > width:
+            blank = out.shape[:3] + (out.shape[3] - width,)
+            out[:, :, :, width:] = jnp.zeros(blank, out.dtype)
+
+
+def convolution(
+    where, acts, own, given, counts, first_tap, taps, slots, part, rows, sums=None, ends=True, after=()
+):
+    padded, frames, cols, chans = acts[0].shape
+    height = padded - 2
+    width = part * slots
+    lanes = -(-width // LANES) * LANES
+    halves = len(acts)
+    if ends:
+        out = jax.ShapeDtypeStruct((rows, frames * halves, cols, lanes), jnp.bfloat16)
+        out_shape = [out] * 4
+        results = [pltpu.VMEM((height, frames, cols, width), jnp.bfloat16)] * halves
+    else:
+        out_shape = [jax.ShapeDtypeStruct((height * frames * cols, width), jnp.float32)] * halves
+        results = []
+    operands = [act.reshape(padded * frames * cols, chans) for act in acts]
+    specs = [VMEM] * halves
+    if own is not None:
+        operands.append(own)
+        specs.append(ANY)
+    operands += given
+    specs += [ANY] * len(given)
+    if sums is not None:
+        operands += sums
+        specs += [VMEM] * halves
+    operands += after
+    specs += [ANY] * len(after)
+    return pl.pallas_call(
+        functools.partial(
+            conv_kernel,
+            rows,
+            cols,
+            part,
+            first_tap,
+            counts,
+            halves,
+            taps if own is not None else 0,
+            (sums is not None, not ends, len(after)),
+        ),
+        out_shape=out_shape,
+        in_specs=[SMEM] + specs,
+        out_specs=[VMEM] * len(out_shape),
+        scratch_shapes=[pltpu.VMEM((taps, width, chans), jnp.bfloat16)]
+        + results
+        + [pltpu.SemaphoreType.DMA((len(given) + 1,))],
+        compiler_params=params(24),
+        cost_estimate=pl.CostEstimate(
+            flops=2 * height * frames * cols * taps * chans * 256,
+            transcendentals=0,
+            bytes_accessed=taps * width * chans * 2,
+        ),
+        name="convolution",
+    )(where, *operands)
+
+
+def result_kernel(where, sizes, latents, bias, *refs):
+    main, last, out = refs[:4], refs[4:8], refs[8]
+    main_buf, last_buf, sems = refs[9:]
+    frames, rows, cols, chans = latents.shape
+    part = chans // 16
+    z, y, c = where[0], where[2], where[3]
+    pairs = []
+    for k in range(4):
+        place = 2 * (c ^ (k % 2)) + (y ^ (k // 2))
+        pairs.append((main[k], main_buf.at[place]))
+        pairs.append((last[k], last_buf.at[place]))
+    for copy in start_all(pairs, sems):
+        copy.wait()
+    first_row = rows * (2 * y + c)
+    col_ids = lax.broadcasted_iota(jnp.int32, (cols, chans), 0)
+
+    def finish(low):
+        def body(f, _):
+            for r in range(rows):
+                chunks = []
+                for shard in range(4):
+                    for q in range(4):
+                        if low <= shard < low + 3:
+                            lanes = slice((shard - low) * part, (shard - low + 1) * part)
+                            chunk = main_buf[q, r, f, :, lanes]
+                        else:
+                            chunk = last_buf[q, r, f, :, 0:part]
+                        chunks.append(chunk.astype(jnp.float32))
+                value = jnp.concatenate(chunks, axis=1) + bias[f]
+                limit = jnp.where(first_row + r < sizes[f, 0], sizes[f, 1], 0)
+                value = latents[f, r].astype(jnp.float32) + jnp.where(col_ids < limit, value, 0.0)
+                out[f, r] = value.astype(jnp.bfloat16)
+            return 0
+
+        lax.fori_loop(0, frames, body, 0)
+
+    @pl.when(z < 2)
+    def _():
+        finish(0)
+
+    @pl.when(z >= 2)
+    def _():
+        finish(1)
+
+
+def final_result(where, sizes, latents, bias, main, last):
+    return pl.pallas_call(
+        result_kernel,
+        out_shape=jax.ShapeDtypeStruct(latents.shape, latents.dtype),
+        in_specs=[SMEM, SMEM, VMEM, VMEM] + [ANY] * 8,
+        out_specs=VMEM,
+        scratch_shapes=[
+            pltpu.VMEM((4,) + main[0].shape, jnp.bfloat16),
+            pltpu.VMEM((4,) + last[0].shape, jnp.bfloat16),
+            pltpu.SemaphoreType.DMA((8,)),
+        ],
+        compiler_params=params(12),
+        cost_estimate=pl.CostEstimate(
+            flops=4 * latents.size, transcendentals=0, bytes_accessed=8 * latents.size
+        ),
+        name="final_result",
+    )(where, sizes, latents, bias[:, None, :], *main, *last)
+
+
+def frame_plan(grid, latents, buckets, gn_gain, gn_shift, conv_weight, time_bias):
+    frames, rows, cols, chans = latents.shape
+    taps = conv_weight.shape[0]
+    part = conv_weight.shape[1] // 2
+    early, late = 6, taps - 6
+    dp_index, space_index = lax.axis_index("dp"), lax.axis_index("space")
+    z, x = dp_index // 2, dp_index % 2
+    y, c = space_index // 2, space_index % 2
+    where = jnp.stack([z, x, y, c]).astype(jnp.int32)
+
+    def spread(values):
+        return [
+            grid.permute(v, lambda z, x, y, c, k=k: (z, c, y ^ (k // 2), x ^ (k % 2)))
+            for k, v in enumerate(values)
+        ]
+
+    def spread_in(value):
+        return [
+            grid.permute(value, lambda z, x, y, c, k=k: (z, c ^ (k % 2), y ^ (k // 2), x))
+            for k in range(4)
+        ]
+
+    def up(value, first):
+        return grid.permute(value, lambda z, x, y, c: (z + 1, x, y, c) if first <= z < 3 else None)
+
+    def down(value, last):
+        return grid.permute(value, lambda z, x, y, c: (z - 1, x, y, c) if 1 <= z <= last else None)
+
+    def swap(value):
+        return grid.permute(value, lambda z, x, y, c: (z, x, y, 1 - c))
+
+    group = group_matrix(chans)
+    group = (group, group.T)
+    half = frames // 2
+
+    (piece,) = own_pieces(where, conv_weight, part, ((0, taps),))
+    sizes = grid.permute(buckets, lambda z, x, y, c: (z, c, y, x))
+    up1, down1 = up(piece, 0), down(piece, 3)
+    rounds0 = spread_in(latents[:half])
+    rest = latents[half:]
+    up1, down1, rounds0, rest = lax.optimization_barrier((up1, down1, rounds0, rest))
+
+    up2, down2 = up(up1, 1), down(down1, 2)
+    rounds1 = spread_in(rest)
+    slot1 = jnp.where(z == 0, down1, up1)
+    slot1_other = swap(slot1)
+    act0 = activation(where, sizes, gn_gain, gn_shift, group, rounds0, 0)
+    up2, down2, rounds1, act0, slot1, slot1_other = lax.optimization_barrier(
+        (up2, down2, rounds1, act0, slot1, slot1_other)
+    )
+
+    near = lax.optimization_barrier((up2, down2, up1, down1))
+    up3 = [up(up2[:early], 2), up(up2[early:], 2)]
+    down3 = [down(down2[:early], 1), down(down2[early:], 1)]
+    slot2 = jnp.where(z == 0, near[1], jnp.where(z == 3, near[0], near[3]))
+    slot2_other = swap(slot2)
+    act1 = activation(where, sizes, gn_gain, gn_shift, group, rounds1, half)
+    acts = [act0, act1]
+    main = convolution(
+        where,
+        acts,
+        conv_weight,
+        [slot1, slot1_other, slot2, slot2_other],
+        ((0, taps, 0), (0, taps, 1)),
+        0,
+        taps,
+        3,
+        part,
+        rows,
+    )
+
+    def pick_last(n, taken):
+        a, b, c_, d = taken
+        return jnp.where(z < 2, jnp.where(z == 0, a, b), jnp.where(z == 2, c_, d))
+
+    first_cut, second_cut = slice(0, early), slice(early, taps)
+    taken = lax.optimization_barrier((down3[0], down2[first_cut], up2[first_cut], up3[0], main))
+    slot3 = pick_last(0, taken[:4])
+    sums = convolution(
+        where,
+        acts,
+        None,
+        [slot3, swap(slot3)],
+        ((0, early, 0),),
+        0,
+        early,
+        1,
+        part,
+        rows,
+        ends=False,
+        after=taken[4][:1],
+    )
+    taken = lax.optimization_barrier((down3[1], down2[second_cut], up2[second_cut], up3[1]))
+    slot3 = pick_last(1, taken)
+    last = convolution(
+        where,
+        acts,
+        None,
+        [slot3, swap(slot3)],
+        ((0, late, 0),),
+        early,
+        late,
+        1,
+        part,
+        rows,
+        sums=sums,
+    )
+    return final_result(where, buckets, latents, time_bias, spread(main), spread(last))
 
 
 def solution(mesh):
@@ -76,7 +588,13 @@
         P(None, "dp", None),
         P("dp", None),
     )
-    out_specs = P("dp", "space", None, None)
+    grid = Grid(mesh)
+
+    def body(latents, *rest):
+        if (grid.Z, grid.Y) == (4, 2) and latents.shape[1] == 2:
+            return frame_plan(grid, latents, *rest)
+        return row_plan(latents, *rest)
+
     return jax.shard_map(
-        on_device, mesh=mesh, in_specs=in_specs, out_specs=out_specs, check_vma=False
-    )
+        body, mesh=mesh, in_specs=in_specs, out_specs=P("dp", "space", None, None), check_vma=False
+    )

time: 675 us -> 156 us (0.23)
  waiting for transfers between devices: 566 us -> 46.5 us
  matrix products: 50.9 us -> 0 us
  Pallas kernels: 0 us -> 40.1 us
  starting transfers between devices: 3 us -> 40.2 us
  blocking collectives: 14.1 us -> 0 us
  between operations: 13.2 us -> 0.59 us
    all_gather x9 -> x0, waiting for transfers between devices: 563 us -> none  [add_tap(): lax.all_gather(panel, 'dp', axis=0, tiled=True)]
    dot_general x9 -> x0, matrix products: 50.9 us -> none  [tap_product(): lax.dot_general(window, panel, (((3,), (1,)), ((), ())), preferred_elemen...]
    ppermute x2 -> x29, waiting for transfers between devices: 2.55 us -> 46.5 us  [permute(): return lax.ppermute(value, ('dp', 'space'), pairs)]
    pallas_call x0 -> x7, Pallas kernels: none -> 40.1 us  [the longest x3 24.6 us: convolution(): pl.pallas_call(functools.partial(conv_kernel, rows, cols, part, first_tap...]
    ppermute x2 -> x29, starting transfers between devices: 2.98 us -> 40.2 us  [permute(): return lax.ppermute(value, ('dp', 'space'), pairs)]
    dynamic_slice x9 -> x0, local copies, waits for them, and re-layouts: 16 us -> none  [add_tap(): panel = lax.dynamic_index_in_dim(conv_weight, index, 0, keepdims=False)]
    psum x2 -> x0, blocking collectives: 14.1 us -> none  [the longest x1 8.38 us: on_device(): total = lax.psum(jnp.sum(values * weight_mask, axis=(1, 2, 4)), 'space')]
    unnamed x8 -> x39, local copies, waits for them, and re-layouts: 0.01 us -> 12.3 us
  transfers between devices with their start and end apart: 11 -> 29, of which waited for: 11 -> 6; matrix products, arithmetic and copies ran while one was open for 0% -> 6% of each run, Pallas kernels for 0% -> 23%
where the time goes in v2:
time: 156 us; the launch traced here: 154 us
  waiting for transfers between devices  46.5 us (30%)
  starting transfers between devices  40.2 us (26%)
  Pallas kernels  40.1 us (26%)
  local copies, waits for them, and re-layouts  20.4 us (13%)
  other arithmetic  6.63 us (4%)
    ppermute x29, waiting for transfers between devices, permute(): return lax.ppermute(value, ('dp', 'space'), pairs)  46.5 us
    ppermute x29, starting transfers between devices, permute(): return lax.ppermute(value, ('dp', 'space'), pairs)  40.2 us
    pallas_call x3, Pallas kernels, convolution(): pl.pallas_call(functools.partial(conv_kernel, rows, cols, part, first_tap...  24.6 us
    unnamed x39, local copies, waits for them, and re-layouts  12.3 us
    pallas_call x2, Pallas kernels, activation(): pl.pallas_call(functools.partial(act_kernel, begin), out_shape=jax.ShapeD...  10.7 us
    pallas_call x1, Pallas kernels, final_result(): pl.pallas_call(result_kernel, out_shape=jax.ShapeDtypeStruct(latents.shap...  4.15 us
  transfers between devices with their start and end apart: 29, of which 6 were waited for; matrix products, arithmetic and copies ran while one was open for 6% of the time, Pallas kernels for 23%

profile of v2, /device:TPU:0, one launch (start us, length us, event | category | flops | bytes accessed | tf_op | source)
XLA Modules:
  0.0 154.4 jit_solution(11750222726063084722)
XLA Ops:
  0.0 2.1 %fusion.5 = (bf16[3,2,32,1280]{3,2,1,0:T(8,128)(2,1)}, bf16[3,2,32,1280]{3,2,1,0:T(8,128)(2,1)S(1)}) fusion(bf16[6,2,32,1280]{3,2,1,0:T(8,128)(2,1)} %latents.1), kind=kLoop, calls=%fused_computation.16 | loop fusion | bytes 1966080 | tf_op jit(solution)/shard_map/slice | solution.py:511
  3.0 2.0 %copy-done.1 = bf16[9,160,1280]{2,1,0:T(8,128)(2,1)S(1)} copy-done((bf16[9,160,1280]{2,1,0:T(8,128)(2,1)S(1)}, bf16[9,160,1280]{2,1,0:T(8,128)(2,1)}, u32[]{:S(2)}) %copy-start.1) | copy-done | bytes 3686424
  5.7 5.9 %collective-permute-start = (bf16[9,80,640]{2,1,0:T(8,128)(2,1)S(1)}, bf16[9,80,640]{2,1,0:T(8,128)(2,1)}, u32[]{:S(2)}, u32[]{:S(2)}) collective-permute-start(bf16[9,80,640]{2,1,0:T(8,128)(2,1)S(1)} %own_pieces.1), channel_id=1, source_target_pairs={{0,8},{1,9},{2,10},{3,11},{4,12},{5,13},{6,14},{7,15},{8,16},{9,17... | collective-permute-start | bytes 2764808 | tf_op jit(solution)/shard_map/ppermute | solution.py:95
  12.9 2.7 %collective-permute-start.3 = (bf16[3,2,32,1280]{3,2,1,0:T(8,128)(2,1)S(1)}, bf16[3,2,32,1280]{3,2,1,0:T(8,128)(2,1)S(1)}, u32[]{:S(2)}, u32[]{:S(2)}) collective-permute-start(bf16[3,2,32,1280]{3,2,1,0:T(8,128)(2,1)S(1)} %get-tuple-element.82), channel_id=1, source_target_pairs={{0,4},{1,0},{2,6},{3,2},{4,5},{5,1},{6,7},{7,3},{8,12},{9,8},{10,1... | collective-permute-start | bytes 1474568 | tf_op jit(solution)/shard_map/ppermute | solution.py:95
  18.1 8.8 %collective-permute-done.3.refs_1_ = bf16[3,2,32,1280]{3,2,1,0:T(8,128)(2,1)S(1)} collective-permute-done((bf16[3,2,32,1280]{3,2,1,0:T(8,128)(2,1)S(1)}, bf16[3,2,32,1280]{3,2,1,0:T(8,128)(2,1)S(1)}, u32[]{:S(2)}, u32[]{:S(2)}) %collective-permute-start.3) | collective-permute-done | bytes 491552 | tf_op jit(solution)/shard_map/ppermute | solution.py:95
  27.7 12.0 %collective-permute-done.4.refs_2_ = bf16[3,2,32,1280]{3,2,1,0:T(8,128)(2,1)S(1)} collective-permute-done((bf16[3,2,32,1280]{3,2,1,0:T(8,128)(2,1)S(1)}, bf16[3,2,32,1280]{3,2,1,0:T(8,128)(2,1)S(1)}, u32[]{:S(2)}, u32[]{:S(2)}) %collective-permute-start.4) | collective-permute-done | bytes 491552 | tf_op jit(solution)/shard_map/ppermute | solution.py:95
  41.2 2.1 %collective-permute-start.10 = (bf16[3,2,32,1280]{3,2,1,0:T(8,128)(2,1)}, bf16[3,2,32,1280]{3,2,1,0:T(8,128)(2,1)S(1)}, u32[]{:S(2)}, u32[]{:S(2)}) collective-permute-start(bf16[3,2,32,1280]{3,2,1,0:T(8,128)(2,1)} %get-tuple-element.45), channel_id=1, source_target_pairs={{0,2},{1,6},{2,0},{3,4},{4,3},{5,7},{6,1},{7,5},{8,10},{9,14},{10,... | collective-permute-start | bytes 1474568 | tf_op jit(solution)/shard_map/ppermute | solution.py:95
  47.0 2.2 %broadcast_select_fusion.refs_3_ = bf16[9,80,640]{2,1,0:T(8,128)(2,1)} fusion(bf16[9,80,640]{2,1,0:T(8,128)(2,1)} %collective-permute-done.1, bf16[9,80,640]{2,1,0:T(8,128)(2,1)} %collective-permute-done, pred[]{:T(512)S(6)} %eq.54), kind=kLoop, calls=%fused_computation.1 | loop fusion | flops 460800 | bytes 2764801 | tf_op jit(solution)/shard_map/jit(_where)/select_n | solution.py:516
  49.2 5.3 %collective-permute-start.8 = (bf16[3,2,32,1280]{3,2,1,0:T(8,128)(2,1)}, bf16[3,2,32,1280]{3,2,1,0:T(8,128)(2,1)}, u32[]{:S(2)}, u32[]{:S(2)}) collective-permute-start(bf16[3,2,32,1280]{3,2,1,0:T(8,128)(2,1)} %get-tuple-element.45), channel_id=1, source_target_pairs={{0,0},{1,4},{2,2},{3,6},{4,1},{5,5},{6,3},{7,7},{8,8},{9,12},{10,1... | collective-permute-start | bytes 1474568 | tf_op jit(solution)/shard_map/ppermute | solution.py:95
  54.5 10.7 %collective-permute-done.10.refs_2_ = bf16[3,2,32,1280]{3,2,1,0:T(8,128)(2,1)S(1)} collective-permute-done((bf16[3,2,32,1280]{3,2,1,0:T(8,128)(2,1)}, bf16[3,2,32,1280]{3,2,1,0:T(8,128)(2,1)S(1)}, u32[]{:S(2)}, u32[]{:S(2)}) %collective-permute-start.10) | collective-permute-done | bytes 491552 | tf_op jit(solution)/shard_map/ppermute | solution.py:95
  71.9 5.0 %activation.2 = bf16[10,3,32,1280]{3,2,1,0:T(8,128)(2,1)S(1)} custom-call(s32[4]{0:T(128)S(1)} %pad_add_fusion.where, s32[6,2]{1,0:T(8,128)S(1)} %collective-permute-done.12.sizes, f32[1,1280]{1,0:T(1,128)S(1)} %broadcast_in_dim.14.gain, f32[1,1280]{1,0:T(1,128)S(1)} %broadcast_in_dim.15.shift, bf16[1280,128]{1,0:T(8,128)(2,1)S(1)} %fusion.group, ...), custom_call_target="tpu_custom_call" | custom-call | flops 1966080 | bytes 983040 | tf_op jit(solution)/shard_map/activation/pallas_call | solution.py:240
  76.9 2.6 %select_select_fusion.refs_5_ = bf16[9,80,640]{2,1,0:T(8,128)(2,1)} fusion(bf16[9,80,640]{2,1,0:T(8,128)(2,1)} %collective-permute-done.7, bf16[9,80,640]{2,1,0:T(8,128)(2,1)} %collective-permute-done.6, bf16[9,80,640]{2,1,0:T(8,128)(2,1)} %collective-permute-done.1, pred[]{:T(512)S(6)} %eq.55, pred[]{:T(512)S(6)} %eq.54), kind=kLoop, calls=%fused_computation | loop fusion | flops 921600 | bytes 3686402 | tf_op jit(solution)/shard_map/jit(_where)/select_n | solution.py:526
  79.5 2.0 %slice.26 = bf16[6,80,640]{2,1,0:T(8,128)(2,1)} slice(bf16[9,80,640]{2,1,0:T(8,128)(2,1)} %collective-permute-done.7), slice={[0:6], [0:80], [0:640]} | slice | bytes 1228800 | tf_op jit(solution)/shard_map/slice | solution.py:525
  81.4 2.0 %slice.27 = bf16[6,80,640]{2,1,0:T(8,128)(2,1)} slice(bf16[9,80,640]{2,1,0:T(8,128)(2,1)} %collective-permute-done.6), slice={[0:6], [0:80], [0:640]} | slice | bytes 1228800 | tf_op jit(solution)/shard_map/slice | solution.py:548
  88.3 5.7 %activation.3 = bf16[10,3,32,1280]{3,2,1,0:T(8,128)(2,1)S(1)} custom-call(s32[4]{0:T(128)S(1)} %pad_add_fusion.where, s32[6,2]{1,0:T(8,128)S(1)} %collective-permute-done.12.sizes, f32[1,1280]{1,0:T(1,128)S(1)} %broadcast_in_dim.14.gain, f32[1,1280]{1,0:T(1,128)S(1)} %broadcast_in_dim.15.shift, bf16[1280,128]{1,0:T(8,128)(2,1)S(1)} %fusion.group, ...), custom_call_target="tpu_custom_call" | custom-call | flops 1966080 | bytes 983040 | tf_op jit(solution)/shard_map/activation/pallas_call | solution.py:240
  94.0 12.8 %convolution.3 = (bf16[2,6,32,256]{3,2,1,0:T(8,128)(2,1)S(1)}, bf16[2,6,32,256]{3,2,1,0:T(8,128)(2,1)S(1)}, bf16[2,6,32,256]{3,2,1,0:T(8,128)(2,1)S(1)}, bf16[2,6,32,256]{3,2,1,0:T(8,128)(2,1)S(1)}) custom-call(s32[4]{0:T(128)S(1)} %pad_add_fusion.where, bf16[960,1280]{1,0:T(8,128)(2,1)S(1)} %bitcast.6, bf16[960,1280]{1,0:T(8,128)(2,1)S(1)} %bitcast.9, ...), custom_call_target="tpu_custom_call" | custom-call | flops 4529848320 | bytes 5529600 | tf_op jit(solution)/shard_map/convolution/pallas_call | solution.py:380
  112.8 10.2 %collective-permute-done.19 = bf16[3,80,640]{2,1,0:T(8,128)(2,1)S(1)} collective-permute-done((bf16[3,80,640]{2,1,0:T(8,128)(2,1)S(1)}, bf16[3,80,640]{2,1,0:T(8,128)(2,1)S(1)}, u32[]{:S(2)}, u32[]{:S(2)}) %collective-permute-start.19) | collective-permute-done | bytes 307232 | tf_op jit(solution)/shard_map/ppermute | solution.py:95
  126.4 2.0 %collective-permute-start.18 = (bf16[2,6,32,256]{3,2,1,0:T(8,128)(2,1)S(1)}, bf16[2,6,32,256]{3,2,1,0:T(8,128)(2,1)S(1)}, u32[]{:S(2)}, u32[]{:S(2)}) collective-permute-start(bf16[2,6,32,256]{3,2,1,0:T(8,128)(2,1)S(1)} %get-tuple-element.65), channel_id=1, source_target_pairs={{0,3},{1,7},{2,1},{3,5},{4,2},{5,6},{6,0},{7,4},{8,11},{9,15},{10,... | collective-permute-start | bytes 589832 | tf_op jit(solution)/shard_map/ppermute | solution.py:95
  128.4 7.4 %convolution.4 = (f32[768,80]{1,0:T(8,128)S(1)}, f32[768,80]{1,0:T(8,128)S(1)}) custom-call(s32[4]{0:T(128)S(1)} %pad_add_fusion.where, bf16[960,1280]{1,0:T(8,128)(2,1)S(1)} %bitcast.7, bf16[960,1280]{1,0:T(8,128)(2,1)S(1)} %bitcast.10, bf16[6,80,640]{2,1,0:T(8,128)(2,1)S(1)} %select_select_fusion.1.refs_2_, ...), custom_call_target="tpu_custom_call" | custom-call | flops 3019898880 | bytes 1228800 | tf_op jit(solution)/shard_map/convolution/pallas_call | solution.py:380
  135.9 4.4 %convolution.5 = (bf16[2,6,32,128]{3,2,1,0:T(8,128)(2,1)S(1)}, bf16[2,6,32,128]{3,2,1,0:T(8,128)(2,1)S(1)}, bf16[2,6,32,128]{3,2,1,0:T(8,128)(2,1)S(1)}, bf16[2,6,32,128]{3,2,1,0:T(8,128)(2,1)S(1)}) custom-call(s32[4]{0:T(128)S(1)} %pad_add_fusion.where, bf16[960,1280]{1,0:T(8,128)(2,1)S(1)} %bitcast.8, bf16[960,1280]{1,0:T(8,128)(2,1)S(1)} %bitcast.11, ...), custom_call_target="tpu_custom_call" | custom-call | flops 1509949440 | bytes 614400 | tf_op jit(solution)/shard_map/convolution/pallas_call | solution.py:380
  141.0 2.0 %collective-permute-start.26 = (bf16[2,6,32,128]{3,2,1,0:T(8,128)(2,1)S(1)}, bf16[2,6,32,128]{3,2,1,0:T(8,128)(2,1)S(1)}, u32[]{:S(2)}, u32[]{:S(2)}) collective-permute-start(bf16[2,6,32,128]{3,2,1,0:T(8,128)(2,1)S(1)} %get-tuple-element.78), channel_id=1, source_target_pairs={{0,1},{1,5},{2,3},{3,7},{4,0},{5,4},{6,2},{7,6},{8,9},{9,13},{10,1... | collective-permute-start | bytes 294920 | tf_op jit(solution)/shard_map/ppermute | solution.py:95
  145.3 2.3 %collective-permute-done.26.refs_5_ = bf16[2,6,32,128]{3,2,1,0:T(8,128)(2,1)S(1)} collective-permute-done((bf16[2,6,32,128]{3,2,1,0:T(8,128)(2,1)S(1)}, bf16[2,6,32,128]{3,2,1,0:T(8,128)(2,1)S(1)}, u32[]{:S(2)}, u32[]{:S(2)}) %collective-permute-start.26) | collective-permute-done | bytes 98336 | tf_op jit(solution)/shard_map/ppermute | solution.py:95
  147.6 2.5 %collective-permute-done.28.refs_7_ = bf16[2,6,32,128]{3,2,1,0:T(8,128)(2,1)S(1)} collective-permute-done((bf16[2,6,32,128]{3,2,1,0:T(8,128)(2,1)S(1)}, bf16[2,6,32,128]{3,2,1,0:T(8,128)(2,1)S(1)}, u32[]{:S(2)}, u32[]{:S(2)}) %collective-permute-start.28) | collective-permute-done | bytes 98336 | tf_op jit(solution)/shard_map/ppermute | solution.py:95
  150.1 4.1 %final_result.1 = bf16[6,2,32,1280]{3,2,1,0:T(8,128)(2,1)} custom-call(s32[4]{0:T(128)S(1)} %pad_add_fusion.where, s32[6,2]{1,0:T(8,128)S(1)} %copy.8.sizes, bf16[6,2,32,1280]{3,2,1,0:T(8,128)(2,1)S(1)} %copy-done, f32[6,1,1280]{2,1,0:T(1,128)S(1)} %broadcast_in_dim.6.bias, bf16[2,6,32,256]{3,2,1,0:T(8,128)(2,1)S(1)} %collective-permute-done.15.refs_0_, ...), custom_call_target="tpu_custom_call" | custom-call | flops 1966080 | bytes 3932160 | tf_op jit(solution)/shard_map/final_result/pallas_call | solution.py:454
  (96 shorter events, 35.1 us)
Async XLA Ops:
  2.1 15.1 %collective-permute-start.2 = (bf16[3,2,32,1280]{3,2,1,0:T(8,128)(2,1)S(1)}, bf16[3,2,32,1280]{3,2,1,0:T(8,128)(2,1)S(1)}, u32[]{:S(2)}, u32[]{:S(2)}) collective-permute-start(bf16[3,2,32,1280]{3,2,1,0:T(8,128)(2,1)S(1)} %get-tuple-element.82), channel_id=1, source_target_pairs={{0,0},{1,4},{2,2},{3,6},{4,1},{5,5},{6,3},{7,7},{8,8},{9,12},{10,1... | collective-permute-start | bytes 1474568 | tf_op jit(solution)/shard_map/ppermute | solution.py:95
  5.7 35.5 %collective-permute-start = (bf16[9,80,640]{2,1,0:T(8,128)(2,1)S(1)}, bf16[9,80,640]{2,1,0:T(8,128)(2,1)}, u32[]{:S(2)}, u32[]{:S(2)}) collective-permute-start(bf16[9,80,640]{2,1,0:T(8,128)(2,1)S(1)} %own_pieces.1), channel_id=1, source_target_pairs={{0,8},{1,9},{2,10},{3,11},{4,12},{5,13},{6,14},{7,15},{8,16},{9,17... | collective-permute-start | bytes 2764808 | tf_op jit(solution)/shard_map/ppermute | solution.py:95
  11.6 29.6 %collective-permute-start.1 = (bf16[9,80,640]{2,1,0:T(8,128)(2,1)S(1)}, bf16[9,80,640]{2,1,0:T(8,128)(2,1)}, u32[]{:S(2)}, u32[]{:S(2)}) collective-permute-start(bf16[9,80,640]{2,1,0:T(8,128)(2,1)S(1)} %own_pieces.1), channel_id=1, source_target_pairs={{8,0},{9,1},{10,2},{11,3},{12,4},{13,5},{14,6},{15,7},{16,8},{17,9... | collective-permute-start | bytes 2764808 | tf_op jit(solution)/shard_map/ppermute | solution.py:95
  12.9 14.0 %collective-permute-start.3 = (bf16[3,2,32,1280]{3,2,1,0:T(8,128)(2,1)S(1)}, bf16[3,2,32,1280]{3,2,1,0:T(8,128)(2,1)S(1)}, u32[]{:S(2)}, u32[]{:S(2)}) collective-permute-start(bf16[3,2,32,1280]{3,2,1,0:T(8,128)(2,1)S(1)} %get-tuple-element.82), channel_id=1, source_target_pairs={{0,4},{1,0},{2,6},{3,2},{4,5},{5,1},{6,7},{7,3},{8,12},{9,8},{10,1... | collective-permute-start | bytes 1474568 | tf_op jit(solution)/shard_map/ppermute | solution.py:95
  15.6 24.0 %collective-permute-start.4 = (bf16[3,2,32,1280]{3,2,1,0:T(8,128)(2,1)S(1)}, bf16[3,2,32,1280]{3,2,1,0:T(8,128)(2,1)S(1)}, u32[]{:S(2)}, u32[]{:S(2)}) collective-permute-start(bf16[3,2,32,1280]{3,2,1,0:T(8,128)(2,1)S(1)} %get-tuple-element.82), channel_id=1, source_target_pairs={{0,2},{1,6},{2,0},{3,4},{4,3},{5,7},{6,1},{7,5},{8,10},{9,14},{10,... | collective-permute-start | bytes 1474568 | tf_op jit(solution)/shard_map/ppermute | solution.py:95
  17.2 23.3 %collective-permute-start.5 = (bf16[3,2,32,1280]{3,2,1,0:T(8,128)(2,1)S(1)}, bf16[3,2,32,1280]{3,2,1,0:T(8,128)(2,1)S(1)}, u32[]{:S(2)}, u32[]{:S(2)}) collective-permute-start(bf16[3,2,32,1280]{3,2,1,0:T(8,128)(2,1)S(1)} %get-tuple-element.82), channel_id=1, source_target_pairs={{0,6},{1,2},{2,4},{3,0},{4,7},{5,3},{6,5},{7,1},{8,14},{9,10},{10,... | collective-permute-start | bytes 1474568 | tf_op jit(solution)/shard_map/ppermute | solution.py:95
  41.2 24.0 %collective-permute-start.10 = (bf16[3,2,32,1280]{3,2,1,0:T(8,128)(2,1)}, bf16[3,2,32,1280]{3,2,1,0:T(8,128)(2,1)S(1)}, u32[]{:S(2)}, u32[]{:S(2)}) collective-permute-start(bf16[3,2,32,1280]{3,2,1,0:T(8,128)(2,1)} %get-tuple-element.45), channel_id=1, source_target_pairs={{0,2},{1,6},{2,0},{3,4},{4,3},{5,7},{6,1},{7,5},{8,10},{9,14},{10,... | collective-permute-start | bytes 1474568 | tf_op jit(solution)/shard_map/ppermute | solution.py:95
  43.3 22.8 %collective-permute-start.11 = (bf16[3,2,32,1280]{3,2,1,0:T(8,128)(2,1)}, bf16[3,2,32,1280]{3,2,1,0:T(8,128)(2,1)S(1)}, u32[]{:S(2)}, u32[]{:S(2)}) collective-permute-start(bf16[3,2,32,1280]{3,2,1,0:T(8,128)(2,1)} %get-tuple-element.45), channel_id=1, source_target_pairs={{0,6},{1,2},{2,4},{3,0},{4,7},{5,3},{6,5},{7,1},{8,14},{9,10},{10,... | collective-permute-start | bytes 1474568 | tf_op jit(solution)/shard_map/ppermute | solution.py:95
  44.1 32.8 %collective-permute-start.6 = (bf16[9,80,640]{2,1,0:T(8,128)(2,1)}, bf16[9,80,640]{2,1,0:T(8,128)(2,1)}, u32[]{:S(2)}, u32[]{:S(2)}) collective-permute-start(bf16[9,80,640]{2,1,0:T(8,128)(2,1)} %collective-permute-done), channel_id=1, source_target_pairs={{8,16},{9,17},{10,18},{11,19},{12,20},{13,21},{14,22},{15,23},{16,... | collective-permute-start | bytes 2764808 | tf_op jit(solution)/shard_map/ppermute | solution.py:95
  45.7 31.2 %collective-permute-start.7 = (bf16[9,80,640]{2,1,0:T(8,128)(2,1)}, bf16[9,80,640]{2,1,0:T(8,128)(2,1)}, u32[]{:S(2)}, u32[]{:S(2)}) collective-permute-start(bf16[9,80,640]{2,1,0:T(8,128)(2,1)} %collective-permute-done.1), channel_id=1, source_target_pairs={{8,0},{9,1},{10,2},{11,3},{12,4},{13,5},{14,6},{15,7},{16,8},{17,9... | collective-permute-start | bytes 2764808 | tf_op jit(solution)/shard_map/ppermute | solution.py:95
  49.2 27.6 %collective-permute-start.8 = (bf16[3,2,32,1280]{3,2,1,0:T(8,128)(2,1)}, bf16[3,2,32,1280]{3,2,1,0:T(8,128)(2,1)}, u32[]{:S(2)}, u32[]{:S(2)}) collective-permute-start(bf16[3,2,32,1280]{3,2,1,0:T(8,128)(2,1)} %get-tuple-element.45), channel_id=1, source_target_pairs={{0,0},{1,4},{2,2},{3,6},{4,1},{5,5},{6,3},{7,7},{8,8},{9,12},{10,1... | collective-permute-start | bytes 1474568 | tf_op jit(solution)/shard_map/ppermute | solution.py:95
  66.1 10.8 %collective-permute-start.9 = (bf16[3,2,32,1280]{3,2,1,0:T(8,128)(2,1)}, bf16[3,2,32,1280]{3,2,1,0:T(8,128)(2,1)}, u32[]{:S(2)}, u32[]{:S(2)}) collective-permute-start(bf16[3,2,32,1280]{3,2,1,0:T(8,128)(2,1)} %get-tuple-element.45), channel_id=1, source_target_pairs={{0,4},{1,0},{2,6},{3,2},{4,5},{5,1},{6,7},{7,3},{8,12},{9,8},{10,1... | collective-permute-start | bytes 1474568 | tf_op jit(solution)/shard_map/ppermute | solution.py:95
  66.9 10.0 %collective-permute-start.13 = (bf16[9,80,640]{2,1,0:T(8,128)(2,1)}, bf16[9,80,640]{2,1,0:T(8,128)(2,1)}, u32[]{:S(2)}, u32[]{:S(2)}) collective-permute-start(bf16[9,80,640]{2,1,0:T(8,128)(2,1)} %broadcast_select_fusion.refs_3_), channel_id=1, source_target_pairs={{0,1},{1,0},{2,3},{3,2},{4,5},{5,4},{6,7},{7,6},{8,9},{9,8},{10,11... | collective-permute-start | bytes 2764808 | tf_op jit(solution)/shard_map/ppermute | solution.py:95
  79.5 14.5 %collective-permute-start.14 = (bf16[9,80,640]{2,1,0:T(8,128)(2,1)}, bf16[9,80,640]{2,1,0:T(8,128)(2,1)}, u32[]{:S(2)}, u32[]{:S(2)}) collective-permute-start(bf16[9,80,640]{2,1,0:T(8,128)(2,1)} %select_select_fusion.refs_5_), channel_id=1, source_target_pairs={{0,1},{1,0},{2,3},{3,2},{4,5},{5,4},{6,7},{7,6},{8,9},{9,8},{10,11... | collective-permute-start | bytes 2764808 | tf_op jit(solution)/shard_map/ppermute | solution.py:95
  83.4 23.4 %collective-permute-start.22 = (bf16[6,80,640]{2,1,0:T(8,128)(2,1)}, bf16[6,80,640]{2,1,0:T(8,128)(2,1)}, u32[]{:S(2)}, u32[]{:S(2)}) collective-permute-start(bf16[6,80,640]{2,1,0:T(8,128)(2,1)} %slice.26), channel_id=1, source_target_pairs={{8,0},{9,1},{10,2},{11,3},{12,4},{13,5},{14,6},{15,7}} | collective-permute-start | bytes 1843208 | tf_op jit(solution)/shard_map/ppermute | solution.py:95
  84.7 22.1 %collective-permute-start.23 = (bf16[6,80,640]{2,1,0:T(8,128)(2,1)}, bf16[6,80,640]{2,1,0:T(8,128)(2,1)}, u32[]{:S(2)}, u32[]{:S(2)}) collective-permute-start(bf16[6,80,640]{2,1,0:T(8,128)(2,1)} %slice.27), channel_id=1, source_target_pairs={{16,24},{17,25},{18,26},{19,27},{20,28},{21,29},{22,30},{23,31}} | collective-permute-start | bytes 1843208 | tf_op jit(solution)/shard_map/ppermute | solution.py:95
  108.2 18.2 %collective-permute-start.24 = (bf16[6,80,640]{2,1,0:T(8,128)(2,1)S(1)}, bf16[6,80,640]{2,1,0:T(8,128)(2,1)S(1)}, u32[]{:S(2)}, u32[]{:S(2)}) collective-permute-start(bf16[6,80,640]{2,1,0:T(8,128)(2,1)S(1)} %select_select_fusion.1.refs_2_), channel_id=1, source_target_pairs={{0,1},{1,0},{2,3},{3,2},{4,5},{5,4},{6,7},{7,6},{8,9},{9,8},{10,11... | collective-permute-start | bytes 1843208 | tf_op jit(solution)/shard_map/ppermute | solution.py:95
  110.8 12.1 %collective-permute-start.19 = (bf16[3,80,640]{2,1,0:T(8,128)(2,1)S(1)}, bf16[3,80,640]{2,1,0:T(8,128)(2,1)S(1)}, u32[]{:S(2)}, u32[]{:S(2)}) collective-permute-start(bf16[3,80,640]{2,1,0:T(8,128)(2,1)S(1)} %slice.24), channel_id=1, source_target_pairs={{8,0},{9,1},{10,2},{11,3},{12,4},{13,5},{14,6},{15,7}} | collective-permute-start | bytes 921608 | tf_op jit(solution)/shard_map/ppermute | solution.py:95
  112.1 10.9 %collective-permute-start.20 = (bf16[3,80,640]{2,1,0:T(8,128)(2,1)S(1)}, bf16[3,80,640]{2,1,0:T(8,128)(2,1)S(1)}, u32[]{:S(2)}, u32[]{:S(2)}) collective-permute-start(bf16[3,80,640]{2,1,0:T(8,128)(2,1)S(1)} %slice.25), channel_id=1, source_target_pairs={{16,24},{17,25},{18,26},{19,27},{20,28},{21,29},{22,30},{23,31}} | collective-permute-start | bytes 921608 | tf_op jit(solution)/shard_map/ppermute | solution.py:95
  123.0 12.8 %collective-permute-start.21 = (bf16[3,80,640]{2,1,0:T(8,128)(2,1)S(1)}, bf16[3,80,640]{2,1,0:T(8,128)(2,1)S(1)}, u32[]{:S(2)}, u32[]{:S(2)}) collective-permute-start(bf16[3,80,640]{2,1,0:T(8,128)(2,1)S(1)} %select_select_fusion.2.refs_2_), channel_id=1, source_target_pairs={{0,1},{1,0},{2,3},{3,2},{4,5},{5,4},{6,7},{7,6},{8,9},{9,8},{10,11... | collective-permute-start | bytes 921608 | tf_op jit(solution)/shard_map/ppermute | solution.py:95
  123.1 17.9 %collective-permute-start.15 = (bf16[2,6,32,256]{3,2,1,0:T(8,128)(2,1)S(1)}, bf16[2,6,32,256]{3,2,1,0:T(8,128)(2,1)S(1)}, u32[]{:S(2)}, u32[]{:S(2)}) collective-permute-start(bf16[2,6,32,256]{3,2,1,0:T(8,128)(2,1)S(1)} %get-tuple-element.74.refs_4_), channel_id=1, source_target_pairs={{0,0},{1,4},{2,2},{3,6},{4,1},{5,5},{6,3},{7,7},{8,8},{9,12},{10,1... | collective-permute-start | bytes 589832 | tf_op jit(solution)/shard_map/ppermute | solution.py:95
  123.8 19.2 %collective-permute-start.16 = (bf16[2,6,32,256]{3,2,1,0:T(8,128)(2,1)S(1)}, bf16[2,6,32,256]{3,2,1,0:T(8,128)(2,1)S(1)}, u32[]{:S(2)}, u32[]{:S(2)}) collective-permute-start(bf16[2,6,32,256]{3,2,1,0:T(8,128)(2,1)S(1)} %get-tuple-element.63), channel_id=1, source_target_pairs={{0,1},{1,5},{2,3},{3,7},{4,0},{5,4},{6,2},{7,6},{8,9},{9,13},{10,1... | collective-permute-start | bytes 589832 | tf_op jit(solution)/shard_map/ppermute | solution.py:95
  125.5 18.3 %collective-permute-start.17 = (bf16[2,6,32,256]{3,2,1,0:T(8,128)(2,1)S(1)}, bf16[2,6,32,256]{3,2,1,0:T(8,128)(2,1)S(1)}, u32[]{:S(2)}, u32[]{:S(2)}) collective-permute-start(bf16[2,6,32,256]{3,2,1,0:T(8,128)(2,1)S(1)} %get-tuple-element.64), channel_id=1, source_target_pairs={{0,2},{1,6},{2,0},{3,4},{4,3},{5,7},{6,1},{7,5},{8,10},{9,14},{10,... | collective-permute-start | bytes 589832 | tf_op jit(solution)/shard_map/ppermute | solution.py:95
  126.4 18.9 %collective-permute-start.18 = (bf16[2,6,32,256]{3,2,1,0:T(8,128)(2,1)S(1)}, bf16[2,6,32,256]{3,2,1,0:T(8,128)(2,1)S(1)}, u32[]{:S(2)}, u32[]{:S(2)}) collective-permute-start(bf16[2,6,32,256]{3,2,1,0:T(8,128)(2,1)S(1)} %get-tuple-element.65), channel_id=1, source_target_pairs={{0,3},{1,7},{2,1},{3,5},{4,2},{5,6},{6,0},{7,4},{8,11},{9,15},{10,... | collective-permute-start | bytes 589832 | tf_op jit(solution)/shard_map/ppermute | solution.py:95
  (24 other events, 285.4 us)

commit v3 on v0

--- a/solution.py
+++ b/solution.py
@@ -1,12 +1,15 @@
+import functools
+
 import jax
 import jax.numpy as jnp
 from jax import lax
+from jax.experimental import pallas as pl
+from jax.experimental.pallas import tpu as pltpu
 from jax.sharding import PartitionSpec as P
 
 GROUPS = 32
-
-
-eps = 1e-05
+EPS = 1e-05
+FRAME_BYTES = 8 << 20
 
 
 def with_halo(x, sides, width):
@@ -28,7 +31,7 @@
     )
 
 
-def on_device(latents, buckets, gn_gain, gn_shift, conv_weight, time_bias):
+def row_plan(latents, buckets, gn_gain, gn_shift, conv_weight, time_bias):
     frames, rows, cols, chans = latents.shape
     members = chans // GROUPS
     row_ids = lax.axis_index("space") * rows + jnp.arange(rows, dtype=jnp.int32)
@@ -44,7 +47,7 @@
     mean = total / count
     centered = values - mean[:, None, None, :, None]
     spread = lax.psum(jnp.sum(centered * centered * weight_mask, axis=(1, 2, 4)), "space") / count
-    normed = (centered / jnp.sqrt(spread[:, None, None, :, None] + eps)).reshape(
+    normed = (centered / jnp.sqrt(spread[:, None, None, :, None] + EPS)).reshape(
         frames, rows, cols, chans
     )
     normed = normed * gn_gain + gn_shift
@@ -65,6 +68,535 @@
         conv_out.astype(jnp.float32) + time_bias[:, None, None, :]
     )
     return summed.astype(jnp.bfloat16)
+
+
+class Grid:
+    def __init__(self, mesh):
+        dp, space = mesh.shape["dp"], mesh.shape["space"]
+        self.X = self.C = 2
+        self.Z, self.Y = dp // 2, space // 2
+        self.places = [
+            (z, x, y, c)
+            for z in range(self.Z)
+            for x in range(2)
+            for y in range(self.Y)
+            for c in range(2)
+        ]
+
+    def linear(self, z, x, y, c):
+        return ((z * 2 + x) * self.Y + y) * 2 + c
+
+    def permute(self, value, target):
+        pairs = []
+        for place in self.places:
+            goal = target(*place)
+            if goal is not None:
+                pairs.append((self.linear(*place), self.linear(*goal)))
+        return lax.ppermute(value, ("dp", "space"), pairs)
+
+
+LANES = 128
+ANY = pl.BlockSpec(memory_space=pl.ANY)
+VMEM = pl.BlockSpec(memory_space=pltpu.VMEM)
+SMEM = pl.BlockSpec(memory_space=pltpu.SMEM)
+
+
+def params(mib):
+    return pltpu.CompilerParams(vmem_limit_bytes=mib << 20)
+
+
+def start_all(pairs, sems):
+    copies = [pltpu.make_async_copy(src, dst, sems.at[n]) for n, (src, dst) in enumerate(pairs)]
+    for copy in copies:
+        copy.start()
+    return copies
+
+
+def piece_kernel(part, where, weight, out, sem):
+    rows = pl.ds(pl.multiple_of(where[2] * part, part), part)
+    copy = pltpu.make_async_copy(weight.at[:, rows, :], out, sem.at[0])
+    copy.start()
+    copy.wait()
+
+
+def own_piece(where, weight, part):
+    taps, _, chans = weight.shape
+    return pl.pallas_call(
+        functools.partial(piece_kernel, part),
+        out_shape=jax.ShapeDtypeStruct((taps, part, chans), weight.dtype),
+        in_specs=[SMEM, ANY],
+        out_specs=ANY,
+        scratch_shapes=[pltpu.SemaphoreType.DMA((1,))],
+        compiler_params=params(56),
+        cost_estimate=pl.CostEstimate(flops=0, transcendentals=0, bytes_accessed=4 << 20),
+        name="own_piece",
+    )(where, weight)
+
+
+def choose(index, sources, target, sem, wait):
+    for value, source in enumerate(sources):
+
+        @pl.when(index == value)
+        def _(source=source):
+            copy = pltpu.make_async_copy(source, target, sem)
+            copy.wait() if wait else copy.start()
+
+
+def exact_dot(value, ones):
+    total = None
+    for _ in range(3):
+        top = value.astype(jnp.bfloat16)
+        term = jnp.dot(top, ones, preferred_element_type=jnp.float32)
+        total = term if total is None else total + term
+        value = value - top.astype(jnp.float32)
+    return total
+
+
+def act_kernel(begin, where, sizes, gain, shift, group, group_t, *refs):
+    given, act, blocks, sums, scale, sems = refs[:6], *refs[6:]
+    frames, rows, cols, chans = blocks.shape[1:]
+    members = chans // GROUPS
+    x, y, c = where[1], where[2], where[3]
+    span = pl.ds(begin, frames)
+    away = jnp.where(c == x, 0, 1)
+    same0, same1, other0, other1, relay0, relay1 = (ref.at[span] for ref in given)
+    choices = [(same0, same0), (same1, same1), (other0, relay0), (other1, relay1)]
+    for wait in (False, True):
+        for k, pair in enumerate(choices):
+            choose(away, pair, blocks.at[k], sems.at[k], wait)
+    tiles = chans // LANES
+    first_row = [rows * (2 * (y ^ (k // 2)) + (x ^ (k % 2))) for k in range(4)]
+    col_ids = lax.broadcasted_iota(jnp.int32, (cols, LANES), 0)
+
+    def limit(f, k, r):
+        return jnp.where(first_row[k] + r < sizes[begin + f, 0], sizes[begin + f, 1], 0)
+
+    def fold(v):
+        return jnp.sum(v.reshape(cols // 8, 8, LANES), axis=0)
+
+    def keep(kind, value):
+        for f in range(frames):
+            scale[8 * kind + f] = value[f : f + 1]
+
+    sums[...] = jnp.zeros_like(sums)
+
+    def add_sums(f, _):
+        masks = [[col_ids < limit(f, k, r) for r in range(rows)] for k in range(4)]
+        for t in range(tiles):
+            lanes = slice(t * LANES, (t + 1) * LANES)
+            total = jnp.zeros((8, LANES), jnp.float32)
+            for k in range(4):
+                for r in range(rows):
+                    v = blocks[k, f, r, :, lanes].astype(jnp.float32)
+                    total += fold(jnp.where(masks[k][r], v, 0.0))
+            sums[f, :, lanes] = total
+        return 0
+
+    lax.fori_loop(0, frames, add_sums, 0)
+    ids = lax.broadcasted_iota(jnp.int32, (8, LANES), 0)
+    count = jnp.ones((8, LANES), jnp.float32)
+    for f in range(frames):
+        cells = (sizes[begin + f, 0] * sizes[begin + f, 1] * members).astype(jnp.float32)
+        count = jnp.where(ids == f, cells, count)
+    mean = exact_dot(jnp.sum(sums[...], axis=1), group[...]) / count
+    keep(0, exact_dot(mean, group_t[...]))
+
+    def add_squares(f, _):
+        masks = [[col_ids < limit(f, k, r) for r in range(rows)] for k in range(4)]
+        for t in range(tiles):
+            lanes = slice(t * LANES, (t + 1) * LANES)
+            middle = scale[f, :, lanes]
+            total = jnp.zeros((8, LANES), jnp.float32)
+            for k in range(4):
+                for r in range(rows):
+                    v = blocks[k, f, r, :, lanes].astype(jnp.float32) - middle
+                    total += fold(jnp.where(masks[k][r], v * v, 0.0))
+            sums[f, :, lanes] = total
+        return 0
+
+    lax.fori_loop(0, frames, add_squares, 0)
+    spread = exact_dot(jnp.sum(sums[...], axis=1), group[...]) / count
+    keep(1, exact_dot(1.0 / jnp.sqrt(spread + EPS), group_t[...]) * gain[...])
+
+    def activate(f, _):
+        for t in range(tiles):
+            lanes = slice(t * LANES, (t + 1) * LANES)
+            middle = scale[f, :, lanes]
+            factor = scale[8 + f, :, lanes]
+            offset = shift[:, lanes]
+            for k in range(4):
+                for r in range(rows):
+                    v = blocks[k, f, r, :, lanes].astype(jnp.float32)
+                    v = (v - middle) * factor + offset
+                    v = v / (1.0 + jnp.exp(-v))
+                    v = jnp.where(col_ids < limit(f, k, r), v, 0.0)
+                    act[first_row[k] + r + 1, f, :, lanes] = v.astype(jnp.bfloat16)
+        return 0
+
+    lax.fori_loop(0, frames, activate, 0)
+    edge = jnp.zeros((frames, cols, chans), jnp.bfloat16)
+    act[0] = edge
+    act[act.shape[0] - 1] = edge
+
+
+def group_matrix(chans):
+    member = jnp.arange(chans, dtype=jnp.int32)[:, None] // (chans // GROUPS)
+    return (member == jnp.arange(LANES, dtype=jnp.int32)[None, :]).astype(jnp.bfloat16)
+
+
+def activation(where, sizes, gain, shift, group, blocks, begin, frames):
+    _, rows, cols, chans = blocks[0].shape
+    elements = 4 * frames * rows * cols * chans
+    return pl.pallas_call(
+        functools.partial(act_kernel, begin),
+        out_shape=jax.ShapeDtypeStruct((4 * rows + 2, frames, cols, chans), jnp.bfloat16),
+        in_specs=[SMEM, SMEM] + [VMEM] * 4 + [ANY] * 6,
+        out_specs=VMEM,
+        scratch_shapes=[
+            pltpu.VMEM((4, frames, rows, cols, chans), jnp.bfloat16),
+            pltpu.VMEM((8, 8, chans), jnp.float32),
+            pltpu.VMEM((16, 1, chans), jnp.float32),
+            pltpu.SemaphoreType.DMA((4,)),
+        ],
+        compiler_params=params(12),
+        cost_estimate=pl.CostEstimate(
+            flops=2 * elements, transcendentals=0, bytes_accessed=elements
+        ),
+        name="activation",
+    )(where, sizes, gain[None, :], shift[None, :], *group, *blocks)
+
+
+def shifted_sum(left, middle, right, cols):
+    size = middle.shape[0]
+    col = lax.broadcasted_iota(jnp.int32, middle.shape, 0) % cols
+    left = jnp.where(col == 0, 0.0, pltpu.roll(left, 1, 0))
+    right = jnp.where(col == cols - 1, 0.0, pltpu.roll(right, size - 1, 0))
+    return middle + left + right
+
+
+def window(act, base, dr, chunk, line, cols):
+    return act[pl.ds(pl.multiple_of(base + dr * line, cols), chunk), :]
+
+
+def product(rows, weight):
+    return lax.dot_general(
+        rows, weight, (((1,), (1,)), ((), ())), preferred_element_type=jnp.float32
+    )
+
+
+def give_rows(where, results, outs, rows):
+    x, y = where[1], where[2]
+    for k, out in enumerate(outs):
+        first = rows * (2 * (y ^ (k // 2)) + (x ^ (k % 2)))
+        width = results[0].shape[3]
+        for n, result in enumerate(results):
+            frames = result.shape[1]
+            out[:, n * frames : (n + 1) * frames, :, 0:width] = result[pl.ds(first, rows)]
+        if out.shape[3] > width:
+            blank = out.shape[:3] + (out.shape[3] - width,)
+            out[:, :, :, width:] = jnp.zeros(blank, out.dtype)
+
+
+def all_rows(acts, results, cols, compute):
+    for act, result in zip(acts, results):
+        frames = result.shape[1]
+        line = frames * cols
+        chunk = result.shape[0] * line // 2
+        lines = chunk // line
+
+        def body(m, _, act=act, result=result, frames=frames, line=line, chunk=chunk, lines=lines):
+            base = pl.multiple_of(m * chunk, chunk)
+            value = compute(act, base, chunk, line).astype(jnp.bfloat16)
+            result[pl.ds(m * lines, lines)] = value.reshape(lines, frames, cols, value.shape[1])
+            return 0
+
+        lax.fori_loop(0, 2, body, 0)
+
+
+def from_below(hop, c):
+    return 2 * hop + c
+
+
+def from_above(hop, c):
+    return 2 * hop + 1 - c
+
+
+def main_kernel(rows, cols, part, where, act0, act1, own, *refs):
+    z, y, c = where[0], where[2], where[3]
+    hops, refs = refs[:4], refs[4:]
+    outs, weight, results, sems = refs[:4], refs[4], refs[5:7], refs[7]
+    low = jnp.where(z < 2, 0, 1)
+
+    def rows_of(place):
+        return pl.ds(pl.multiple_of(place * part, part), part)
+
+    mine = pltpu.make_async_copy(own, weight.at[:, rows_of(z - low), :], sems.at[2])
+    mine.start()
+    first = jnp.where(z == 0, from_above(0, c), from_below(0, c))
+    second = jnp.where(
+        z == 0, from_above(1, c), jnp.where(z == 3, from_below(1, c), from_above(0, c))
+    )
+    first_rows = rows_of(jnp.where(z == 0, 1, z - 1) - low)
+    second_rows = rows_of(jnp.where(z < 3, 2, 0))
+    for wait in (False, True):
+        choose(first, hops[:2], weight.at[:, first_rows, :], sems.at[0], wait)
+        choose(second, hops, weight.at[:, second_rows, :], sems.at[1], wait)
+    mine.wait()
+
+    def compute(act, base, chunk, line):
+        columns = []
+        for dc in range(3):
+            total = None
+            for dr in range(3):
+                term = product(window(act, base, dr, chunk, line, cols), weight[3 * dr + dc])
+                total = term if total is None else total + term
+            columns.append(total)
+        return shifted_sum(*columns, cols)
+
+    all_rows((act0, act1), results, cols, compute)
+    give_rows(where, results, outs, rows)
+
+
+def last_kernel(rows, cols, part, where, act0, act1, *refs):
+    z, c = where[0], where[3]
+    hops, refs = refs[:4], refs[4:]
+    outs, weight, results, sems = refs[:4], refs[4], refs[5:7], refs[7]
+    index = jnp.where(
+        z < 2,
+        jnp.where(z == 0, from_above(1, c), from_above(0, c)),
+        jnp.where(z == 2, from_below(0, c), from_below(1, c)),
+    )
+    for wait in (False, True):
+        choose(index, hops, weight, sems.at[0], wait)
+
+    def compute(act, base, chunk, line):
+        total = None
+        for dr in range(3):
+            taps = weight[3 * dr : 3 * dr + 3].reshape(3 * part, weight.shape[2])
+            term = product(window(act, base, dr, chunk, line, cols), taps)
+            total = term if total is None else total + term
+        columns = [total[:, dc * part : (dc + 1) * part] for dc in range(3)]
+        return shifted_sum(*columns, cols)
+
+    all_rows((act0, act1), results, cols, compute)
+    give_rows(where, results, outs, rows)
+
+
+def convolution(kernel, where, acts, weights, part, rows, shards):
+    padded, frames, cols, chans = acts[0].shape
+    height = padded - 2
+    width = part * shards
+    lanes = -(-width // LANES) * LANES
+    out = jax.ShapeDtypeStruct((rows, 2 * frames, cols, lanes), jnp.bfloat16)
+    return pl.pallas_call(
+        functools.partial(kernel, rows, cols, part),
+        out_shape=[out] * 4,
+        in_specs=[SMEM, VMEM, VMEM] + [ANY] * len(weights),
+        out_specs=[VMEM] * 4,
+        scratch_shapes=[
+            pltpu.VMEM((9, width, chans), jnp.bfloat16),
+            pltpu.VMEM((height, frames, cols, width), jnp.bfloat16),
+            pltpu.VMEM((height, frames, cols, width), jnp.bfloat16),
+            pltpu.SemaphoreType.DMA((3,)),
+        ],
+        compiler_params=params(24),
+        cost_estimate=pl.CostEstimate(
+            flops=4 * height * frames * cols * 9 * chans * width,
+            transcendentals=0,
+            bytes_accessed=9 * width * chans * 2,
+        ),
+        name="convolution",
+    )(where, *[act.reshape(padded * frames * cols, chans) for act in acts], *weights)
+
+
+def place_of(where, k):
+    return 2 * (where[3] ^ (k % 2)) + (where[2] ^ (k // 2))
+
+
+def bring(where, parts, buffer, sems):
+    copies = [
+        pltpu.make_async_copy(part, buffer.at[place_of(where, k)], sems.at[k])
+        for k, part in enumerate(parts)
+    ]
+    for copy in copies:
+        copy.start()
+    for copy in copies:
+        copy.wait()
+
+
+def main_result_kernel(where, sizes, latents, bias, *refs):
+    parts, out, buffer, sems = refs[:4], *refs[4:]
+    frames, rows, cols, chans = latents.shape
+    part = chans // 16
+    bring(where, parts, buffer, sems)
+    first_row = rows * (2 * where[2] + where[3])
+    col_ids = lax.broadcasted_iota(jnp.int32, (cols, 12 * part), 0)
+
+    def finish(low):
+        lanes = slice(low * 4 * part, (low + 3) * 4 * part)
+        rest = slice(12 * part, chans) if low == 0 else slice(0, 4 * part)
+
+        def body(f, _):
+            for r in range(rows):
+                chunks = [
+                    buffer[q, r, f, :, n * part : (n + 1) * part].astype(jnp.float32)
+                    for n in range(3)
+                    for q in range(4)
+                ]
+                value = jnp.concatenate(chunks, axis=1) + bias[f, :, lanes]
+                limit = jnp.where(first_row + r < sizes[f, 0], sizes[f, 1], 0)
+                value = jnp.where(col_ids < limit, value, 0.0)
+                value += latents[f, r, :, lanes].astype(jnp.float32)
+                out[f, r, :, lanes] = value.astype(jnp.bfloat16)
+                out[f, r, :, rest] = latents[f, r, :, rest]
+            return 0
+
+        lax.fori_loop(0, frames, body, 0)
+
+    for low in (0, 1):
+        pl.when((where[0] >= 2) == bool(low))(functools.partial(finish, low))
+
+
+def main_result(where, sizes, latents, bias, parts):
+    return pl.pallas_call(
+        main_result_kernel,
+        out_shape=jax.ShapeDtypeStruct(latents.shape, latents.dtype),
+        in_specs=[SMEM, SMEM, VMEM, VMEM] + [ANY] * 4,
+        out_specs=VMEM,
+        scratch_shapes=[
+            pltpu.VMEM((4,) + parts[0].shape, jnp.bfloat16),
+            pltpu.SemaphoreType.DMA((4,)),
+        ],
+        compiler_params=params(12),
+        cost_estimate=pl.CostEstimate(
+            flops=4 * latents.size, transcendentals=0, bytes_accessed=4 * latents.size
+        ),
+        name="main_result",
+    )(where, sizes, latents, bias, *parts)
+
+
+def last_result_kernel(where, sizes, bias, given, *refs):
+    parts, out, buffer, slab, sems = refs[:4], *refs[4:]
+    del given
+    frames, rows, cols, wide = slab.shape
+    chans = out.shape[3]
+    part = chans // 16
+    first_row = rows * (2 * where[2] + where[3])
+    col_ids = lax.broadcasted_iota(jnp.int32, (cols, 4 * part), 0)
+
+    def finish(low):
+        begin = 0 if low else chans - wide
+        inner = slice(0, 4 * part) if low else slice(wide - 4 * part, wide)
+        lanes = slice(0, 4 * part) if low else slice(chans - 4 * part, chans)
+        home = out.at[:, :, :, begin : begin + wide]
+        copy = pltpu.make_async_copy(home, slab, sems.at[4])
+        copy.start()
+        bring(where, parts, buffer, sems)
+        copy.wait()
+
+        def body(f, _):
+            for r in range(rows):
+                chunks = [buffer[q, r, f, :, 0:part].astype(jnp.float32) for q in range(4)]
+                value = jnp.concatenate(chunks, axis=1) + bias[f, :, lanes]
+                limit = jnp.where(first_row + r < sizes[f, 0], sizes[f, 1], 0)
+                value = jnp.where(col_ids < limit, value, 0.0)
+                value += slab[f, r, :, inner].astype(jnp.float32)
+                slab[f, r, :, inner] = value.astype(jnp.bfloat16)
+            return 0
+
+        lax.fori_loop(0, frames, body, 0)
+        copy = pltpu.make_async_copy(slab, home, sems.at[4])
+        copy.start()
+        copy.wait()
+
+    for low in (0, 1):
+        pl.when((where[0] >= 2) == bool(low))(functools.partial(finish, low))
+
+
+def last_result(where, sizes, bias, given, parts):
+    frames, rows, cols, chans = given.shape
+    wide = -(-(chans // 4) // LANES) * LANES
+    return pl.pallas_call(
+        last_result_kernel,
+        out_shape=jax.ShapeDtypeStruct(given.shape, given.dtype),
+        in_specs=[SMEM, SMEM, VMEM, ANY] + [ANY] * 4,
+        out_specs=ANY,
+        scratch_shapes=[
+            pltpu.VMEM((4,) + parts[0].shape, jnp.bfloat16),
+            pltpu.VMEM((frames, rows, cols, wide), jnp.bfloat16),
+            pltpu.SemaphoreType.DMA((5,)),
+        ],
+        input_output_aliases={3: 0},
+        compiler_params=params(8),
+        cost_estimate=pl.CostEstimate(
+            flops=given.size, transcendentals=0, bytes_accessed=given.size
+        ),
+        name="last_result",
+    )(where, sizes, bias, given, *parts)
+
+
+def frame_plan(grid, latents, buckets, gn_gain, gn_shift, conv_weight, time_bias):
+    frames, rows, cols, chans = latents.shape
+    part = conv_weight.shape[1] // 2
+    dp_index, space_index = lax.axis_index("dp"), lax.axis_index("space")
+    z, x = dp_index // 2, dp_index % 2
+    y, c = space_index // 2, space_index % 2
+    where = jnp.stack([z, x, y, c]).astype(jnp.int32)
+
+    def spread(values):
+        return [
+            grid.permute(v, lambda z, x, y, c, k=k: (z, c, y ^ (k // 2), x ^ (k % 2)))
+            for k, v in enumerate(values)
+        ]
+
+    def hop(value, step):
+        def target(z, x, y, c):
+            if c == 0:
+                return (z + 1, x, y, c) if step - 1 <= z < 3 else None
+            return (z - 1, x, y, c) if 1 <= z <= 4 - step else None
+
+        return grid.permute(value, target)
+
+    def swap(value):
+        return grid.permute(value, lambda z, x, y, c: (z, x, y, 1 - c))
+
+    def same_y(j):
+        return grid.permute(latents, lambda z, x, y, c: (z, c ^ j, y, x))
+
+    def other_y(j):
+        return grid.permute(latents, lambda z, x, y, c: (z, x, 1 - y, x) if c == x ^ j else None)
+
+    group = group_matrix(chans)
+    group = (group, group.T)
+    half = frames // 2
+
+    piece = own_piece(where, conv_weight, part)
+    hop1 = hop(piece, 1)
+    blocks = [same_y(0), same_y(1), other_y(0), other_y(1)]
+    hop1, blocks, buckets = lax.optimization_barrier((hop1, blocks, buckets))
+
+    hop2 = hop(hop1, 2)
+    relay0 = grid.permute(blocks[0], lambda z, x, y, c: (z, x, 1 - y, c) if c != x else None)
+    relay1 = grid.permute(blocks[2], lambda z, x, y, c: (z, 1 - x, y, c) if c == x else None)
+    sizes = grid.permute(buckets, lambda z, x, y, c: (z, c, y, x))
+    blocks += [relay0, relay1]
+    swap1 = swap(hop1)
+    act0 = activation(where, sizes, gn_gain, gn_shift, group, blocks, 0, half)
+    hop2, blocks, act0, swap1 = lax.optimization_barrier((hop2, blocks, act0, swap1))
+
+    hop3 = hop(hop2, 3)
+    swap2 = swap(hop2)
+    act1 = activation(where, sizes, gn_gain, gn_shift, group, blocks, half, half)
+    acts = [act0, act1]
+    weights = [piece, hop1, swap1, hop2, swap2]
+    main = convolution(main_kernel, where, acts, weights, part, rows, 3)
+
+    hop3, main = lax.optimization_barrier((hop3, main))
+    weights = [hop2, swap2, hop3, swap(hop3)]
+    last = convolution(last_kernel, where, acts, weights, part, rows, 1)
+    bias = time_bias[:, None, :]
+    result = main_result(where, buckets, latents, bias, spread(main))
+    return last_result(where, buckets, bias, result, spread(last))
 
 
 def solution(mesh):
@@ -76,7 +608,13 @@
         P(None, "dp", None),
         P("dp", None),
     )
-    out_specs = P("dp", "space", None, None)
+    grid = Grid(mesh)
+
+    def body(latents, *rest):
+        if (grid.Z, grid.Y) == (4, 2) and latents.shape[1] == 2:
+            return frame_plan(grid, latents, *rest)
+        return row_plan(latents, *rest)
+
     return jax.shard_map(
-        on_device, mesh=mesh, in_specs=in_specs, out_specs=out_specs, check_vma=False
-    )
+        body, mesh=mesh, in_specs=in_specs, out_specs=P("dp", "space", None, None), check_vma=False
+    )

time: 675 us -> 175 us (0.26)
  waiting for transfers between devices: 566 us -> 32 us
  Pallas kernels: 0 us -> 95.1 us
  matrix products: 50.9 us -> 0 us
  starting transfers between devices: 3 us -> 42.1 us
  local copies, waits for them, and re-layouts: 18.2 us -> 3.28 us
  blocking collectives: 14.1 us -> 0 us
  between operations: 13.2 us -> 0.29 us
  other arithmetic: 9.07 us -> 1.65 us
    all_gather x9 -> x0, waiting for transfers between devices: 563 us -> none  [add_tap(): lax.all_gather(panel, 'dp', axis=0, tiled=True)]
    pallas_call x0 -> x7, Pallas kernels: none -> 95.1 us  [the longest x1 57.7 us: own_piece(): pl.pallas_call(functools.partial(piece_kernel, part), out_shape=jax.Shape...]
    dot_general x9 -> x0, matrix products: 50.9 us -> none  [tap_product(): lax.dot_general(window, panel, (((3,), (1,)), ((), ())), preferred_elemen...]
    ppermute x2 -> x21, starting transfers between devices: 2.98 us -> 42.1 us  [permute(): return lax.ppermute(value, ('dp', 'space'), pairs)]
    ppermute x2 -> x21, waiting for transfers between devices: 2.55 us -> 32 us  [permute(): return lax.ppermute(value, ('dp', 'space'), pairs)]
    dynamic_slice x9 -> x0, local copies, waits for them, and re-layouts: 16 us -> none  [add_tap(): panel = lax.dynamic_index_in_dim(conv_weight, index, 0, keepdims=False)]
    psum x2 -> x0, blocking collectives: 14.1 us -> none  [the longest x1 8.38 us: on_device(): total = lax.psum(jnp.sum(values * weight_mask, axis=(1, 2, 4)), 'space')]
  transfers between devices with their start and end apart: 11 -> 21, of which waited for: 11 -> 5; matrix products, arithmetic and copies ran while one was open for 0% -> 1% of each run, Pallas kernels for 0% -> 19%
where the time goes in v3:
time: 175 us; the launch traced here: 174 us
  Pallas kernels  95.1 us (54%)
  starting transfers between devices  42.1 us (24%)
  waiting for transfers between devices  32 us (18%)
  local copies, waits for them, and re-layouts  3.28 us (2%)
    pallas_call x1, Pallas kernels, own_piece(): pl.pallas_call(functools.partial(piece_kernel, part), out_shape=jax.Shape...  57.7 us
    ppermute x21, starting transfers between devices, permute(): return lax.ppermute(value, ('dp', 'space'), pairs)  42.1 us
    ppermute x21, waiting for transfers between devices, permute(): return lax.ppermute(value, ('dp', 'space'), pairs)  32 us
    pallas_call x2, Pallas kernels, convolution(): pl.pallas_call(functools.partial(kernel, rows, cols, part), out_shape=[ou...  17.9 us
    pallas_call x2, Pallas kernels, activation(): pl.pallas_call(functools.partial(act_kernel, begin), out_shape=jax.ShapeD...  12.5 us
  transfers between devices with their start and end apart: 21, of which 5 were waited for; matrix products, arithmetic and copies ran while one was open for 1% of the time, Pallas kernels for 19%

profile of v3, /device:TPU:0, one launch (start us, length us, event | category | flops | bytes accessed | tf_op | source)
XLA Modules:
  0.0 174.4 jit_solution(2313443697730196859)
XLA Ops:
  0.6 57.7 %own_piece.1.own = bf16[9,80,1280]{2,1,0:T(8,128)(2,1)} custom-call(s32[4]{0:T(128)} %pad_add_fusion.where, bf16[9,160,1280]{2,1,0:T(8,128)(2,1)} %weight.1), custom_call_target="tpu_custom_call" | custom-call | bytes 4194304 | tf_op jit(solution)/shard_map/own_piece/pallas_call | solution.py:124
  58.4 6.2 %collective-permute-start = (bf16[9,80,1280]{2,1,0:T(8,128)(2,1)}, bf16[9,80,1280]{2,1,0:T(8,128)(2,1)}, u32[]{:S(2)}, u32[]{:S(2)}) collective-permute-start(bf16[9,80,1280]{2,1,0:T(8,128)(2,1)} %own_piece.1.own), channel_id=1, source_target_pairs={{0,8},{2,10},{4,12},{6,14},{8,16},{9,1},{10,18},{11,3},{12,20},{13... | collective-permute-start | bytes 5529608 | tf_op jit(solution)/shard_map/ppermute | solution.py:95
  65.3 2.7 %collective-permute-start.2 = (bf16[6,2,32,1280]{3,2,1,0:T(8,128)(2,1)S(1)}, bf16[6,2,32,1280]{3,2,1,0:T(8,128)(2,1)S(1)}, u32[]{:S(2)}, u32[]{:S(2)}) collective-permute-start(bf16[6,2,32,1280]{3,2,1,0:T(8,128)(2,1)S(1)} %copy-done.4), channel_id=1, source_target_pairs={{0,4},{1,0},{2,6},{3,2},{4,5},{5,1},{6,7},{7,3},{8,12},{9,8},{10,1... | collective-permute-start | bytes 2949128 | tf_op jit(solution)/shard_map/ppermute | solution.py:95
  68.0 3.4 %collective-permute-start.3 = (bf16[6,2,32,1280]{3,2,1,0:T(8,128)(2,1)S(1)}, bf16[6,2,32,1280]{3,2,1,0:T(8,128)(2,1)S(1)}, u32[]{:S(2)}, u32[]{:S(2)}) collective-permute-start(bf16[6,2,32,1280]{3,2,1,0:T(8,128)(2,1)S(1)} %copy-done.4), channel_id=1, source_target_pairs={{0,2},{2,0},{5,7},{7,5},{8,10},{10,8},{13,15},{15,13},{16,18},{18,... | collective-permute-start | bytes 2949128 | tf_op jit(solution)/shard_map/ppermute | solution.py:95
  71.4 1.3 collective-permute-start.4
  72.8 16.8 %collective-permute-done.2.refs_1_ = bf16[6,2,32,1280]{3,2,1,0:T(8,128)(2,1)S(1)} collective-permute-done((bf16[6,2,32,1280]{3,2,1,0:T(8,128)(2,1)S(1)}, bf16[6,2,32,1280]{3,2,1,0:T(8,128)(2,1)S(1)}, u32[]{:S(2)}, u32[]{:S(2)}) %collective-permute-start.2) | collective-permute-done | bytes 983072 | tf_op jit(solution)/shard_map/ppermute | solution.py:95
  89.5 2.1 %collective-permute-done.3.refs_2_ = bf16[6,2,32,1280]{3,2,1,0:T(8,128)(2,1)S(1)} collective-permute-done((bf16[6,2,32,1280]{3,2,1,0:T(8,128)(2,1)S(1)}, bf16[6,2,32,1280]{3,2,1,0:T(8,128)(2,1)S(1)}, u32[]{:S(2)}, u32[]{:S(2)}) %collective-permute-start.3) | collective-permute-done | bytes 983072 | tf_op jit(solution)/shard_map/ppermute | solution.py:95
  91.7 2.9 %collective-permute-done.4.refs_3_ = bf16[6,2,32,1280]{3,2,1,0:T(8,128)(2,1)S(1)} collective-permute-done((bf16[6,2,32,1280]{3,2,1,0:T(8,128)(2,1)S(1)}, bf16[6,2,32,1280]{3,2,1,0:T(8,128)(2,1)S(1)}, u32[]{:S(2)}, u32[]{:S(2)}) %collective-permute-start.4) | collective-permute-done | bytes 983072 | tf_op jit(solution)/shard_map/ppermute | solution.py:95
  95.5 1.9 %collective-permute-start.5 = (bf16[9,80,1280]{2,1,0:T(8,128)(2,1)}, bf16[9,80,1280]{2,1,0:T(8,128)(2,1)}, u32[]{:S(2)}, u32[]{:S(2)}) collective-permute-start(bf16[9,80,1280]{2,1,0:T(8,128)(2,1)} %collective-permute-done.refs_0_), channel_id=1, source_target_pairs={{8,16},{9,1},{10,18},{11,3},{12,20},{13,5},{14,22},{15,7},{16,24},... | collective-permute-start | bytes 5529608 | tf_op jit(solution)/shard_map/ppermute | solution.py:95
  97.4 1.7 collective-permute-start.6
  99.2 4.7 %collective-permute-start.7 = (bf16[6,2,32,1280]{3,2,1,0:T(8,128)(2,1)S(1)}, bf16[6,2,32,1280]{3,2,1,0:T(8,128)(2,1)}, u32[]{:S(2)}, u32[]{:S(2)}) collective-permute-start(bf16[6,2,32,1280]{3,2,1,0:T(8,128)(2,1)S(1)} %collective-permute-done.3.refs_2_), channel_id=1, source_target_pairs={{0,4},{2,6},{5,1},{7,3},{8,12},{10,14},{13,9},{15,11},{16,20},{18,... | collective-permute-start | bytes 2949128 | tf_op jit(solution)/shard_map/ppermute | solution.py:95
  105.8 8.8 %collective-permute-done.7.refs_5_ = bf16[6,2,32,1280]{3,2,1,0:T(8,128)(2,1)} collective-permute-done((bf16[6,2,32,1280]{3,2,1,0:T(8,128)(2,1)S(1)}, bf16[6,2,32,1280]{3,2,1,0:T(8,128)(2,1)}, u32[]{:S(2)}, u32[]{:S(2)}) %collective-permute-start.7) | collective-permute-done | bytes 983072 | tf_op jit(solution)/shard_map/ppermute | solution.py:95
  116.7 6.3 %activation.2 = bf16[10,3,32,1280]{3,2,1,0:T(8,128)(2,1)S(1)} custom-call(s32[4]{0:T(128)S(1)} %copy-done.6, s32[6,2]{1,0:T(8,128)S(1)} %collective-permute-done.8.sizes, f32[1,1280]{1,0:T(1,128)S(1)} %broadcast_in_dim.14.gain, f32[1,1280]{1,0:T(1,128)S(1)} %broadcast_in_dim.15.shift, bf16[1280,128]{1,0:T(8,128)(2,1)S(1)} %fusion.group, ...), custom_call_target="tpu_custom_call" | custom-call | flops 1966080 | bytes 983040 | tf_op jit(solution)/shard_map/activation/pallas_call | solution.py:250
  123.0 2.1 %collective-permute-start.11 = (bf16[9,80,1280]{2,1,0:T(8,128)(2,1)}, bf16[9,80,1280]{2,1,0:T(8,128)(2,1)S(1)}, u32[]{:S(2)}, u32[]{:S(2)}) collective-permute-start(bf16[9,80,1280]{2,1,0:T(8,128)(2,1)} %collective-permute-done.5.refs_2_.refs_0_), channel_id=1, source_target_pairs={{0,1},{1,0},{2,3},{3,2},{4,5},{5,4},{6,7},{7,6},{8,9},{9,8},{10,11... | collective-permute-start | bytes 5529608 | tf_op jit(solution)/shard_map/ppermute | solution.py:95
  126.0 6.3 %activation.3 = bf16[10,3,32,1280]{3,2,1,0:T(8,128)(2,1)S(1)} custom-call(s32[4]{0:T(128)S(1)} %copy-done.6, s32[6,2]{1,0:T(8,128)S(1)} %collective-permute-done.8.sizes, f32[1,1280]{1,0:T(1,128)S(1)} %broadcast_in_dim.14.gain, f32[1,1280]{1,0:T(1,128)S(1)} %broadcast_in_dim.15.shift, bf16[1280,128]{1,0:T(8,128)(2,1)S(1)} %fusion.group, ...), custom_call_target="tpu_custom_call" | custom-call | flops 1966080 | bytes 983040 | tf_op jit(solution)/shard_map/activation/pallas_call | solution.py:250
  132.3 12.2 %convolution.2 = (bf16[2,6,32,256]{3,2,1,0:T(8,128)(2,1)S(1)}, bf16[2,6,32,256]{3,2,1,0:T(8,128)(2,1)S(1)}, bf16[2,6,32,256]{3,2,1,0:T(8,128)(2,1)S(1)}, bf16[2,6,32,256]{3,2,1,0:T(8,128)(2,1)S(1)}) custom-call(s32[4]{0:T(128)S(1)} %copy-done.6, bf16[960,1280]{1,0:T(8,128)(2,1)S(1)} %bitcast.6, bf16[960,1280]{1,0:T(8,128)(2,1)S(1)} %bitcast.8, ...), custom_call_target="tpu_custom_call" | custom-call | flops 8493465600 | bytes 5529600 | tf_op jit(solution)/shard_map/convolution/pallas_call | solution.py:391
  144.5 5.8 %collective-permute-start.16 = (bf16[9,80,1280]{2,1,0:T(8,128)(2,1)S(1)}, bf16[9,80,1280]{2,1,0:T(8,128)(2,1)S(1)}, u32[]{:S(2)}, u32[]{:S(2)}) collective-permute-start(bf16[9,80,1280]{2,1,0:T(8,128)(2,1)S(1)} %collective-permute-done.10.refs_2_), channel_id=1, source_target_pairs={{0,1},{1,0},{2,3},{3,2},{4,5},{5,4},{6,7},{7,6},{8,9},{9,8},{10,11... | collective-permute-start | bytes 5529608 | tf_op jit(solution)/shard_map/ppermute | solution.py:95
  151.0 2.0 %collective-permute-start.13 = (bf16[2,6,32,256]{3,2,1,0:T(8,128)(2,1)S(1)}, bf16[2,6,32,256]{3,2,1,0:T(8,128)(2,1)S(1)}, u32[]{:S(2)}, u32[]{:S(2)}) collective-permute-start(bf16[2,6,32,256]{3,2,1,0:T(8,128)(2,1)S(1)} %get-tuple-element.53), channel_id=1, source_target_pairs={{0,1},{1,5},{2,3},{3,7},{4,0},{5,4},{6,2},{7,6},{8,9},{9,13},{10,1... | collective-permute-start | bytes 589832 | tf_op jit(solution)/shard_map/ppermute | solution.py:95
  154.1 1.2 collective-permute-start.15
  155.3 5.7 %convolution.3 = (bf16[2,6,32,128]{3,2,1,0:T(8,128)(2,1)S(1)}, bf16[2,6,32,128]{3,2,1,0:T(8,128)(2,1)S(1)}, bf16[2,6,32,128]{3,2,1,0:T(8,128)(2,1)S(1)}, bf16[2,6,32,128]{3,2,1,0:T(8,128)(2,1)S(1)}) custom-call(s32[4]{0:T(128)S(1)} %copy-done.6, bf16[960,1280]{1,0:T(8,128)(2,1)S(1)} %bitcast.7, bf16[960,1280]{1,0:T(8,128)(2,1)S(1)} %bitcast.9, ...), custom_call_target="tpu_custom_call" | custom-call | flops 2831155200 | bytes 1843200 | tf_op jit(solution)/shard_map/convolution/pallas_call | solution.py:391
  161.7 2.6 %collective-permute-start.18 = (bf16[2,6,32,128]{3,2,1,0:T(8,128)(2,1)S(1)}, bf16[2,6,32,128]{3,2,1,0:T(8,128)(2,1)S(1)}, u32[]{:S(2)}, u32[]{:S(2)}) collective-permute-start(bf16[2,6,32,128]{3,2,1,0:T(8,128)(2,1)S(1)} %get-tuple-element.58), channel_id=1, source_target_pairs={{0,1},{1,5},{2,3},{3,7},{4,0},{5,4},{6,2},{7,6},{8,9},{9,13},{10,1... | collective-permute-start | bytes 294920 | tf_op jit(solution)/shard_map/ppermute | solution.py:95
  166.0 3.5 %main_result.1.given = bf16[6,2,32,1280]{3,2,1,0:T(8,128)(2,1)} custom-call(s32[4]{0:T(128)S(1)} %copy-done.6, s32[6,2]{1,0:T(8,128)S(1)} %copy.10.sizes, bf16[6,2,32,1280]{3,2,1,0:T(8,128)(2,1)S(1)} %copy-done.5, f32[6,1,1280]{2,1,0:T(1,128)S(1)} %broadcast_in_dim.6.bias, bf16[2,6,32,256]{3,2,1,0:T(8,128)(2,1)S(1)} %collective-permute-done.12.refs_0_, ...), custom_call_target="tpu_custom_call" | custom-call | flops 1966080 | bytes 1966080 | tf_op jit(solution)/shard_map/main_result/pallas_call | solution.py:461
  169.6 1.4 collective-permute-done.19.refs_2_
  171.0 3.4 %last_result.1 = bf16[6,2,32,1280]{3,2,1,0:T(8,128)(2,1)} custom-call(s32[4]{0:T(128)S(1)} %copy-done.6, s32[6,2]{1,0:T(8,128)S(1)} %copy.10.sizes, f32[6,1,1280]{2,1,0:T(1,128)S(1)} %broadcast_in_dim.6.bias, bf16[6,2,32,1280]{3,2,1,0:T(8,128)(2,1)} %main_result.1.given, ...), custom_call_target="tpu_custom_call", output_to_operand_aliasing={{}: (3, {})} | custom-call | flops 491520 | bytes 491520 | tf_op jit(solution)/shard_map/last_result/pallas_call | solution.py:519
  (55 shorter events, 11.2 us)
Async XLA Ops:
  0.6 96.8 %copy-start.9 = (f32[1280]{0:T(1024)S(1)}, f32[1280]{0:T(1024)}, u32[]{:S(2)}) copy-start(f32[1280]{0:T(1024)} %param.9) | copy-start | bytes 15364
  0.6 104.4 %copy-start.10 = (s32[6,2]{0,1:T(2,128)S(1)}, s32[6,2]{0,1:T(2,128)}, u32[]{:S(2)}) copy-start(s32[6,2]{0,1:T(2,128)} %param.7) | copy-start | bytes 148
  0.6 113.9 %copy-start.6 = (s32[4]{0:T(128)S(1)}, s32[4]{0:T(128)}, u32[]{:S(2)}) copy-start(s32[4]{0:T(128)} %pad_add_fusion.where) | copy-start | bytes 52
  58.4 37.1 %collective-permute-start = (bf16[9,80,1280]{2,1,0:T(8,128)(2,1)}, bf16[9,80,1280]{2,1,0:T(8,128)(2,1)}, u32[]{:S(2)}, u32[]{:S(2)}) collective-permute-start(bf16[9,80,1280]{2,1,0:T(8,128)(2,1)} %own_piece.1.own), channel_id=1, source_target_pairs={{0,8},{2,10},{4,12},{6,14},{8,16},{9,1},{10,18},{11,3},{12,20},{13... | collective-permute-start | bytes 5529608 | tf_op jit(solution)/shard_map/ppermute | solution.py:95
  64.6 8.1 %collective-permute-start.1 = (bf16[6,2,32,1280]{3,2,1,0:T(8,128)(2,1)S(1)}, bf16[6,2,32,1280]{3,2,1,0:T(8,128)(2,1)S(1)}, u32[]{:S(2)}, u32[]{:S(2)}) collective-permute-start(bf16[6,2,32,1280]{3,2,1,0:T(8,128)(2,1)S(1)} %copy-done.4), channel_id=1, source_target_pairs={{0,0},{1,4},{2,2},{3,6},{4,1},{5,5},{6,3},{7,7},{8,8},{9,12},{10,1... | collective-permute-start | bytes 2949128 | tf_op jit(solution)/shard_map/ppermute | solution.py:95
  65.3 24.2 %collective-permute-start.2 = (bf16[6,2,32,1280]{3,2,1,0:T(8,128)(2,1)S(1)}, bf16[6,2,32,1280]{3,2,1,0:T(8,128)(2,1)S(1)}, u32[]{:S(2)}, u32[]{:S(2)}) collective-permute-start(bf16[6,2,32,1280]{3,2,1,0:T(8,128)(2,1)S(1)} %copy-done.4), channel_id=1, source_target_pairs={{0,4},{1,0},{2,6},{3,2},{4,5},{5,1},{6,7},{7,3},{8,12},{9,8},{10,1... | collective-permute-start | bytes 2949128 | tf_op jit(solution)/shard_map/ppermute | solution.py:95
  68.0 23.6 %collective-permute-start.3 = (bf16[6,2,32,1280]{3,2,1,0:T(8,128)(2,1)S(1)}, bf16[6,2,32,1280]{3,2,1,0:T(8,128)(2,1)S(1)}, u32[]{:S(2)}, u32[]{:S(2)}) collective-permute-start(bf16[6,2,32,1280]{3,2,1,0:T(8,128)(2,1)S(1)} %copy-done.4), channel_id=1, source_target_pairs={{0,2},{2,0},{5,7},{7,5},{8,10},{10,8},{13,15},{15,13},{16,18},{18,... | collective-permute-start | bytes 2949128 | tf_op jit(solution)/shard_map/ppermute | solution.py:95
  71.4 23.1 %collective-permute-start.4 = (bf16[6,2,32,1280]{3,2,1,0:T(8,128)(2,1)S(1)}, bf16[6,2,32,1280]{3,2,1,0:T(8,128)(2,1)S(1)}, u32[]{:S(2)}, u32[]{:S(2)}) collective-permute-start(bf16[6,2,32,1280]{3,2,1,0:T(8,128)(2,1)S(1)} %copy-done.4), channel_id=1, source_target_pairs={{1,2},{3,0},{4,7},{6,5},{9,10},{11,8},{12,15},{14,13},{17,18},{19,... | collective-permute-start | bytes 2949128 | tf_op jit(solution)/shard_map/ppermute | solution.py:95
  95.5 27.5 %collective-permute-start.5 = (bf16[9,80,1280]{2,1,0:T(8,128)(2,1)}, bf16[9,80,1280]{2,1,0:T(8,128)(2,1)}, u32[]{:S(2)}, u32[]{:S(2)}) collective-permute-start(bf16[9,80,1280]{2,1,0:T(8,128)(2,1)} %collective-permute-done.refs_0_), channel_id=1, source_target_pairs={{8,16},{9,1},{10,18},{11,3},{12,20},{13,5},{14,22},{15,7},{16,24},... | collective-permute-start | bytes 5529608 | tf_op jit(solution)/shard_map/ppermute | solution.py:95
  97.4 25.6 %collective-permute-start.9 = (bf16[9,80,1280]{2,1,0:T(8,128)(2,1)}, bf16[9,80,1280]{2,1,0:T(8,128)(2,1)}, u32[]{:S(2)}, u32[]{:S(2)}) collective-permute-start(bf16[9,80,1280]{2,1,0:T(8,128)(2,1)} %collective-permute-done.refs_0_), channel_id=1, source_target_pairs={{0,1},{1,0},{2,3},{3,2},{4,5},{5,4},{6,7},{7,6},{8,9},{9,8},{10,11... | collective-permute-start | bytes 5529608 | tf_op jit(solution)/shard_map/ppermute | solution.py:95
  97.4 8.3 %collective-permute-start.6 = (bf16[6,2,32,1280]{3,2,1,0:T(8,128)(2,1)S(1)}, bf16[6,2,32,1280]{3,2,1,0:T(8,128)(2,1)}, u32[]{:S(2)}, u32[]{:S(2)}) collective-permute-start(bf16[6,2,32,1280]{3,2,1,0:T(8,128)(2,1)S(1)} %collective-permute-done.1.refs_0_), channel_id=1, source_target_pairs={{1,3},{3,1},{4,6},{6,4},{9,11},{11,9},{12,14},{14,12},{17,19},{19,... | collective-permute-start | bytes 2949128 | tf_op jit(solution)/shard_map/ppermute | solution.py:95
  99.2 15.4 %collective-permute-start.7 = (bf16[6,2,32,1280]{3,2,1,0:T(8,128)(2,1)S(1)}, bf16[6,2,32,1280]{3,2,1,0:T(8,128)(2,1)}, u32[]{:S(2)}, u32[]{:S(2)}) collective-permute-start(bf16[6,2,32,1280]{3,2,1,0:T(8,128)(2,1)S(1)} %collective-permute-done.3.refs_2_), channel_id=1, source_target_pairs={{0,4},{2,6},{5,1},{7,3},{8,12},{10,14},{13,9},{15,11},{16,20},{18,... | collective-permute-start | bytes 2949128 | tf_op jit(solution)/shard_map/ppermute | solution.py:95
  105.1 0.7 collective-permute-start.8
  123.0 9.2 %collective-permute-start.11 = (bf16[9,80,1280]{2,1,0:T(8,128)(2,1)}, bf16[9,80,1280]{2,1,0:T(8,128)(2,1)S(1)}, u32[]{:S(2)}, u32[]{:S(2)}) collective-permute-start(bf16[9,80,1280]{2,1,0:T(8,128)(2,1)} %collective-permute-done.5.refs_2_.refs_0_), channel_id=1, source_target_pairs={{0,1},{1,0},{2,3},{3,2},{4,5},{5,4},{6,7},{7,6},{8,9},{9,8},{10,11... | collective-permute-start | bytes 5529608 | tf_op jit(solution)/shard_map/ppermute | solution.py:95
  125.2 19.3 %collective-permute-start.10 = (bf16[9,80,1280]{2,1,0:T(8,128)(2,1)}, bf16[9,80,1280]{2,1,0:T(8,128)(2,1)S(1)}, u32[]{:S(2)}, u32[]{:S(2)}) collective-permute-start(bf16[9,80,1280]{2,1,0:T(8,128)(2,1)} %collective-permute-done.5.refs_2_.refs_0_), channel_id=1, source_target_pairs={{9,1},{11,3},{13,5},{15,7},{16,24},{18,26},{20,28},{22,30}} | collective-permute-start | bytes 5529608 | tf_op jit(solution)/shard_map/ppermute | solution.py:95
  144.5 10.8 %collective-permute-start.16 = (bf16[9,80,1280]{2,1,0:T(8,128)(2,1)S(1)}, bf16[9,80,1280]{2,1,0:T(8,128)(2,1)S(1)}, u32[]{:S(2)}, u32[]{:S(2)}) collective-permute-start(bf16[9,80,1280]{2,1,0:T(8,128)(2,1)S(1)} %collective-permute-done.10.refs_2_), channel_id=1, source_target_pairs={{0,1},{1,0},{2,3},{3,2},{4,5},{5,4},{6,7},{7,6},{8,9},{9,8},{10,11... | collective-permute-start | bytes 5529608 | tf_op jit(solution)/shard_map/ppermute | solution.py:95
  150.4 11.3 %collective-permute-start.12 = (bf16[2,6,32,256]{3,2,1,0:T(8,128)(2,1)S(1)}, bf16[2,6,32,256]{3,2,1,0:T(8,128)(2,1)S(1)}, u32[]{:S(2)}, u32[]{:S(2)}) collective-permute-start(bf16[2,6,32,256]{3,2,1,0:T(8,128)(2,1)S(1)} %get-tuple-element.52), channel_id=1, source_target_pairs={{0,0},{1,4},{2,2},{3,6},{4,1},{5,5},{6,3},{7,7},{8,8},{9,12},{10,1... | collective-permute-start | bytes 589832 | tf_op jit(solution)/shard_map/ppermute | solution.py:95
  151.0 13.2 %collective-permute-start.13 = (bf16[2,6,32,256]{3,2,1,0:T(8,128)(2,1)S(1)}, bf16[2,6,32,256]{3,2,1,0:T(8,128)(2,1)S(1)}, u32[]{:S(2)}, u32[]{:S(2)}) collective-permute-start(bf16[2,6,32,256]{3,2,1,0:T(8,128)(2,1)S(1)} %get-tuple-element.53), channel_id=1, source_target_pairs={{0,1},{1,5},{2,3},{3,7},{4,0},{5,4},{6,2},{7,6},{8,9},{9,13},{10,1... | collective-permute-start | bytes 589832 | tf_op jit(solution)/shard_map/ppermute | solution.py:95
  153.0 12.3 %collective-permute-start.14 = (bf16[2,6,32,256]{3,2,1,0:T(8,128)(2,1)S(1)}, bf16[2,6,32,256]{3,2,1,0:T(8,128)(2,1)S(1)}, u32[]{:S(2)}, u32[]{:S(2)}) collective-permute-start(bf16[2,6,32,256]{3,2,1,0:T(8,128)(2,1)S(1)} %get-tuple-element.54), channel_id=1, source_target_pairs={{0,2},{1,6},{2,0},{3,4},{4,3},{5,7},{6,1},{7,5},{8,10},{9,14},{10,... | collective-permute-start | bytes 589832 | tf_op jit(solution)/shard_map/ppermute | solution.py:95
  154.1 11.9 %collective-permute-start.15 = (bf16[2,6,32,256]{3,2,1,0:T(8,128)(2,1)S(1)}, bf16[2,6,32,256]{3,2,1,0:T(8,128)(2,1)S(1)}, u32[]{:S(2)}, u32[]{:S(2)}) collective-permute-start(bf16[2,6,32,256]{3,2,1,0:T(8,128)(2,1)S(1)} %get-tuple-element.55), channel_id=1, source_target_pairs={{0,3},{1,7},{2,1},{3,5},{4,2},{5,6},{6,0},{7,4},{8,11},{9,15},{10,... | collective-permute-start | bytes 589832 | tf_op jit(solution)/shard_map/ppermute | solution.py:95
  161.0 8.5 %collective-permute-start.17 = (bf16[2,6,32,128]{3,2,1,0:T(8,128)(2,1)S(1)}, bf16[2,6,32,128]{3,2,1,0:T(8,128)(2,1)S(1)}, u32[]{:S(2)}, u32[]{:S(2)}) collective-permute-start(bf16[2,6,32,128]{3,2,1,0:T(8,128)(2,1)S(1)} %get-tuple-element.57), channel_id=1, source_target_pairs={{0,0},{1,4},{2,2},{3,6},{4,1},{5,5},{6,3},{7,7},{8,8},{9,12},{10,1... | collective-permute-start | bytes 294920 | tf_op jit(solution)/shard_map/ppermute | solution.py:95
  161.7 7.9 %collective-permute-start.18 = (bf16[2,6,32,128]{3,2,1,0:T(8,128)(2,1)S(1)}, bf16[2,6,32,128]{3,2,1,0:T(8,128)(2,1)S(1)}, u32[]{:S(2)}, u32[]{:S(2)}) collective-permute-start(bf16[2,6,32,128]{3,2,1,0:T(8,128)(2,1)S(1)} %get-tuple-element.58), channel_id=1, source_target_pairs={{0,1},{1,5},{2,3},{3,7},{4,0},{5,4},{6,2},{7,6},{8,9},{9,13},{10,1... | collective-permute-start | bytes 294920 | tf_op jit(solution)/shard_map/ppermute | solution.py:95
  164.2 6.7 %collective-permute-start.19 = (bf16[2,6,32,128]{3,2,1,0:T(8,128)(2,1)S(1)}, bf16[2,6,32,128]{3,2,1,0:T(8,128)(2,1)S(1)}, u32[]{:S(2)}, u32[]{:S(2)}) collective-permute-start(bf16[2,6,32,128]{3,2,1,0:T(8,128)(2,1)S(1)} %get-tuple-element.59), channel_id=1, source_target_pairs={{0,2},{1,6},{2,0},{3,4},{4,3},{5,7},{6,1},{7,5},{8,10},{9,14},{10,... | collective-permute-start | bytes 294920 | tf_op jit(solution)/shard_map/ppermute | solution.py:95
  165.3 5.6 %collective-permute-start.20 = (bf16[2,6,32,128]{3,2,1,0:T(8,128)(2,1)S(1)}, bf16[2,6,32,128]{3,2,1,0:T(8,128)(2,1)S(1)}, u32[]{:S(2)}, u32[]{:S(2)}) collective-permute-start(bf16[2,6,32,128]{3,2,1,0:T(8,128)(2,1)S(1)} %get-tuple-element.60), channel_id=1, source_target_pairs={{0,3},{1,7},{2,1},{3,5},{4,2},{5,6},{6,0},{7,4},{8,11},{9,15},{10,... | collective-permute-start | bytes 294920 | tf_op jit(solution)/shard_map/ppermute | solution.py:95
  (8 other events, 216.1 us)

commit v4 on v3

--- a/solution.py
+++ b/solution.py
@@ -112,24 +112,31 @@
     return copies
 
 
-def piece_kernel(part, where, weight, out, sem):
+def piece_kernel(part, where, weight, *refs):
+    outs, sems = refs[:-1], refs[-1]
     rows = pl.ds(pl.multiple_of(where[2] * part, part), part)
-    copy = pltpu.make_async_copy(weight.at[:, rows, :], out, sem.at[0])
-    copy.start()
-    copy.wait()
-
-
-def own_piece(where, weight, part):
-    taps, _, chans = weight.shape
+    first, copies = 0, []
+    for n, out in enumerate(outs):
+        taps = pl.ds(first, out.shape[0])
+        copies.append(pltpu.make_async_copy(weight.at[taps, rows, :], out, sems.at[n]))
+        first += out.shape[0]
+    for copy in copies:
+        copy.start()
+    for copy in copies:
+        copy.wait()
+
+
+def own_pieces(where, weight, part, cuts):
+    chans = weight.shape[2]
     return pl.pallas_call(
         functools.partial(piece_kernel, part),
-        out_shape=jax.ShapeDtypeStruct((taps, part, chans), weight.dtype),
+        out_shape=[jax.ShapeDtypeStruct((n, part, chans), weight.dtype) for n in cuts],
         in_specs=[SMEM, ANY],
-        out_specs=ANY,
-        scratch_shapes=[pltpu.SemaphoreType.DMA((1,))],
+        out_specs=[VMEM] * len(cuts),
+        scratch_shapes=[pltpu.SemaphoreType.DMA((len(cuts),))],
         compiler_params=params(56),
         cost_estimate=pl.CostEstimate(flops=0, transcendentals=0, bytes_accessed=4 << 20),
-        name="own_piece",
+        name="own_pieces",
     )(where, weight)
 
 
@@ -321,17 +328,15 @@
     return 2 * hop + 1 - c
 
 
-def main_kernel(rows, cols, part, where, act0, act1, own, *refs):
-    z, y, c = where[0], where[2], where[3]
-    hops, refs = refs[:4], refs[4:]
+def main_kernel(rows, cols, part, where, act0, act1, *refs):
+    z, c = where[0], where[3]
+    own, hops, refs = refs[:2], (refs[2:6], refs[6:10]), refs[10:]
     outs, weight, results, sems = refs[:4], refs[4], refs[5:7], refs[7]
     low = jnp.where(z < 2, 0, 1)
 
     def rows_of(place):
         return pl.ds(pl.multiple_of(place * part, part), part)
 
-    mine = pltpu.make_async_copy(own, weight.at[:, rows_of(z - low), :], sems.at[2])
-    mine.start()
     first = jnp.where(z == 0, from_above(0, c), from_below(0, c))
     second = jnp.where(
         z == 0, from_above(1, c), jnp.where(z == 3, from_below(1, c), from_above(0, c))
@@ -339,9 +344,14 @@
     first_rows = rows_of(jnp.where(z == 0, 1, z - 1) - low)
     second_rows = rows_of(jnp.where(z < 3, 2, 0))
     for wait in (False, True):
-        choose(first, hops[:2], weight.at[:, first_rows, :], sems.at[0], wait)
-        choose(second, hops, weight.at[:, second_rows, :], sems.at[1], wait)
-    mine.wait()
+        tap = 0
+        for n in range(2):
+            taps = pl.ds(tap, own[n].shape[0])
+            tap += own[n].shape[0]
+            mine = weight.at[taps, rows_of(z - low), :]
+            choose(0, own[n : n + 1], mine, sems.at[3 * n], wait)
+            choose(first, hops[n][:2], weight.at[taps, first_rows, :], sems.at[3 * n + 1], wait)
+            choose(second, hops[n], weight.at[taps, second_rows, :], sems.at[3 * n + 2], wait)
 
     def compute(act, base, chunk, line):
         columns = []
@@ -357,24 +367,36 @@
     give_rows(where, results, outs, rows)
 
 
-def last_kernel(rows, cols, part, where, act0, act1, *refs):
+def farthest(where):
     z, c = where[0], where[3]
-    hops, refs = refs[:4], refs[4:]
-    outs, weight, results, sems = refs[:4], refs[4], refs[5:7], refs[7]
-    index = jnp.where(
+    return jnp.where(
         z < 2,
         jnp.where(z == 0, from_above(1, c), from_above(0, c)),
         jnp.where(z == 2, from_below(0, c), from_below(1, c)),
     )
+
+
+def tap_rows(act, weight, part, base, chunk, line, cols, first):
+    total = None
+    for n in range(weight.shape[0] // 3):
+        taps = weight[3 * n : 3 * n + 3].reshape(3 * part, weight.shape[2])
+        term = product(window(act, base, first + n, chunk, line, cols), taps)
+        total = term if total is None else total + term
+    return total
+
+
+def last_kernel(rows, cols, part, where, act0, act1, *refs):
+    hops, refs = (refs[:4], refs[4:8]), refs[8:]
+    outs, weight, results, sems = refs[:4], refs[4], refs[5:7], refs[7]
     for wait in (False, True):
-        choose(index, hops, weight, sems.at[0], wait)
+        tap = 0
+        for n in range(2):
+            taps = pl.ds(tap, hops[n][0].shape[0])
+            tap += hops[n][0].shape[0]
+            choose(farthest(where), hops[n], weight.at[taps], sems.at[n], wait)
 
     def compute(act, base, chunk, line):
-        total = None
-        for dr in range(3):
-            taps = weight[3 * dr : 3 * dr + 3].reshape(3 * part, weight.shape[2])
-            term = product(window(act, base, dr, chunk, line, cols), taps)
-            total = term if total is None else total + term
+        total = tap_rows(act, weight, part, base, chunk, line, cols, 0)
         columns = [total[:, dc * part : (dc + 1) * part] for dc in range(3)]
         return shifted_sum(*columns, cols)
 
@@ -385,7 +407,7 @@
 def convolution(kernel, where, acts, weights, part, rows, shards):
     padded, frames, cols, chans = acts[0].shape
     height = padded - 2
-    width = part * shards
+    taps, width = 9, part * shards
     lanes = -(-width // LANES) * LANES
     out = jax.ShapeDtypeStruct((rows, 2 * frames, cols, lanes), jnp.bfloat16)
     return pl.pallas_call(
@@ -394,16 +416,16 @@
         in_specs=[SMEM, VMEM, VMEM] + [ANY] * len(weights),
         out_specs=[VMEM] * 4,
         scratch_shapes=[
-            pltpu.VMEM((9, width, chans), jnp.bfloat16),
+            pltpu.VMEM((taps, width, chans), jnp.bfloat16),
             pltpu.VMEM((height, frames, cols, width), jnp.bfloat16),
             pltpu.VMEM((height, frames, cols, width), jnp.bfloat16),
-            pltpu.SemaphoreType.DMA((3,)),
+            pltpu.SemaphoreType.DMA((6,)),
         ],
-        compiler_params=params(24),
+        compiler_params=params(6 + 2 * taps),
         cost_estimate=pl.CostEstimate(
-            flops=4 * height * frames * cols * 9 * chans * width,
+            flops=4 * height * frames * cols * taps * chans * width,
             transcendentals=0,
-            bytes_accessed=9 * width * chans * 2,
+            bytes_accessed=taps * width * chans * 2,
         ),
         name="convolution",
     )(where, *[act.reshape(padded * frames * cols, chans) for act in acts], *weights)
@@ -570,30 +592,45 @@
     group = (group, group.T)
     half = frames // 2
 
-    piece = own_piece(where, conv_weight, part)
-    hop1 = hop(piece, 1)
+    cuts = (6, conv_weight.shape[0] - 6)
+    pieces = own_pieces(where, conv_weight, part, cuts)
+    hop1 = [hop(pieces[0], 1), None]
     blocks = [same_y(0), same_y(1), other_y(0), other_y(1)]
-    hop1, blocks, buckets = lax.optimization_barrier((hop1, blocks, buckets))
-
-    hop2 = hop(hop1, 2)
+    hop1[0], later = lax.optimization_barrier((hop1[0], pieces[1]))
+    hop1[1] = hop(later, 1)
+    swap1 = [swap(hop1[0]), None]
+    hop2 = [hop(hop1[0], 2), None]
+    hop1[1], blocks, buckets = lax.optimization_barrier((hop1[1], blocks, buckets))
+
+    hop2[1] = hop(hop1[1], 2)
+    swap1[1] = swap(hop1[1])
     relay0 = grid.permute(blocks[0], lambda z, x, y, c: (z, x, 1 - y, c) if c != x else None)
     relay1 = grid.permute(blocks[2], lambda z, x, y, c: (z, 1 - x, y, c) if c == x else None)
     sizes = grid.permute(buckets, lambda z, x, y, c: (z, c, y, x))
     blocks += [relay0, relay1]
-    swap1 = swap(hop1)
+    hop3 = [hop(hop2[0], 3), None]
+    swap2 = [swap(hop2[0]), None]
+    hop2[1], blocks, sizes = lax.optimization_barrier((hop2[1], blocks, sizes))
+
+    hop3[1] = hop(hop2[1], 3)
+    swap2[1] = swap(hop2[1])
     act0 = activation(where, sizes, gn_gain, gn_shift, group, blocks, 0, half)
-    hop2, blocks, act0, swap1 = lax.optimization_barrier((hop2, blocks, act0, swap1))
-
-    hop3 = hop(hop2, 3)
-    swap2 = swap(hop2)
     act1 = activation(where, sizes, gn_gain, gn_shift, group, blocks, half, half)
     acts = [act0, act1]
-    weights = [piece, hop1, swap1, hop2, swap2]
+
+    def arrived(n, *hops):
+        return [value[n] for one in hops for value in one]
+
+    near = (hop1, swap1, hop2, swap2)
+    weights = list(pieces) + arrived(0, near) + arrived(1, near)
     main = convolution(main_kernel, where, acts, weights, part, rows, 3)
 
     hop3, main = lax.optimization_barrier((hop3, main))
-    weights = [hop2, swap2, hop3, swap(hop3)]
-    last = convolution(last_kernel, where, acts, weights, part, rows, 1)
+    swap3 = [swap(value) for value in hop3]
+    far = (hop2, swap2, hop3, swap3)
+    last = convolution(
+        last_kernel, where, acts, arrived(0, far) + arrived(1, far), part, rows, 1
+    )
     bias = time_bias[:, None, :]
     result = main_result(where, buckets, latents, bias, spread(main))
     return last_result(where, buckets, bias, result, spread(last))

time: 175 us -> 118 us (0.67)
  Pallas kernels: 95.1 us -> 40.4 us
  waiting for transfers between devices: 32 us -> 16.8 us
  starting transfers between devices: 42.1 us -> 55.4 us
    pallas_call x1, Pallas kernels: 57.7 us -> 3.51 us  [own_pieces(): pl.pallas_call(functools.partial(piece_kernel, part), out_shape=[jax.Shap...]
    ppermute x21 -> x27, waiting for transfers between devices: 32 us -> 16.8 us  [permute(): return lax.ppermute(value, ('dp', 'space'), pairs)]
    ppermute x21 -> x27, starting transfers between devices: 42.1 us -> 55.4 us  [permute(): return lax.ppermute(value, ('dp', 'space'), pairs)]
  transfers between devices with their start and end apart: 21 -> 27, of which waited for: 5 -> 5; matrix products, arithmetic and copies ran while one was open for 1% -> 0% of each run, Pallas kernels for 19% -> 29%
where the time goes in v4:
time: 118 us; the launch traced here: 116 us
  starting transfers between devices  55.4 us (47%)
  Pallas kernels  40.4 us (34%)
  waiting for transfers between devices  16.8 us (14%)
  local copies, waits for them, and re-layouts  2.31 us (2%)
    ppermute x27, starting transfers between devices, permute(): return lax.ppermute(value, ('dp', 'space'), pairs)  55.4 us
    pallas_call x2, Pallas kernels, convolution(): pl.pallas_call(functools.partial(kernel, rows, cols, part), out_shape=[ou...  17.4 us
    ppermute x27, waiting for transfers between devices, permute(): return lax.ppermute(value, ('dp', 'space'), pairs)  16.8 us
    pallas_call x2, Pallas kernels, activation(): pl.pallas_call(functools.partial(act_kernel, begin), out_shape=jax.ShapeD...  12.6 us
    pallas_call x1, Pallas kernels, own_pieces(): pl.pallas_call(functools.partial(piece_kernel, part), out_shape=[jax.Shap...  3.51 us
    pallas_call x1, Pallas kernels, main_result(): pl.pallas_call(main_result_kernel, out_shape=jax.ShapeDtypeStruct(latents...  3.49 us
    pallas_call x1, Pallas kernels, last_result(): pl.pallas_call(last_result_kernel, out_shape=jax.ShapeDtypeStruct(given.s...  3.42 us
  transfers between devices with their start and end apart: 27, of which 5 were waited for; matrix products, arithmetic and copies ran while one was open for 0% of the time, Pallas kernels for 29%

profile of v4, /device:TPU:0, one launch (start us, length us, event | category | flops | bytes accessed | tf_op | source)
XLA Modules:
  0.0 116.4 jit_solution(13976607813071638930)
XLA Ops:
  0.6 3.5 %own_pieces.1 = (bf16[6,80,1280]{2,1,0:T(8,128)(2,1)}, bf16[3,80,1280]{2,1,0:T(8,128)(2,1)}) custom-call(s32[4]{0:T(128)} %pad_add_fusion.where, bf16[9,160,1280]{2,1,0:T(8,128)(2,1)} %weight.1), custom_call_target="tpu_custom_call" | custom-call | bytes 4194304 | tf_op jit(solution)/shard_map/own_pieces/pallas_call | solution.py:131
  4.1 6.0 %collective-permute-start = (bf16[6,80,1280]{2,1,0:T(8,128)(2,1)}, bf16[6,80,1280]{2,1,0:T(8,128)(2,1)}, u32[]{:S(2)}, u32[]{:S(2)}) collective-permute-start(bf16[6,80,1280]{2,1,0:T(8,128)(2,1)} %get-tuple-element.37.refs_0_), channel_id=1, source_target_pairs={{0,8},{2,10},{4,12},{6,14},{8,16},{9,1},{10,18},{11,3},{12,20},{13... | collective-permute-start | bytes 3686408 | tf_op jit(solution)/shard_map/ppermute | solution.py:95
  10.8 2.7 %collective-permute-start.3 = (bf16[6,2,32,1280]{3,2,1,0:T(8,128)(2,1)S(1)}, bf16[6,2,32,1280]{3,2,1,0:T(8,128)(2,1)S(1)}, u32[]{:S(2)}, u32[]{:S(2)}) collective-permute-start(bf16[6,2,32,1280]{3,2,1,0:T(8,128)(2,1)S(1)} %copy-done.2), channel_id=1, source_target_pairs={{0,4},{1,0},{2,6},{3,2},{4,5},{5,1},{6,7},{7,3},{8,12},{9,8},{10,1... | collective-permute-start | bytes 2949128 | tf_op jit(solution)/shard_map/ppermute | solution.py:95
  13.5 3.4 %collective-permute-start.4 = (bf16[6,2,32,1280]{3,2,1,0:T(8,128)(2,1)S(1)}, bf16[6,2,32,1280]{3,2,1,0:T(8,128)(2,1)S(1)}, u32[]{:S(2)}, u32[]{:S(2)}) collective-permute-start(bf16[6,2,32,1280]{3,2,1,0:T(8,128)(2,1)S(1)} %copy-done.2), channel_id=1, source_target_pairs={{0,2},{2,0},{5,7},{7,5},{8,10},{10,8},{13,15},{15,13},{16,18},{18,... | collective-permute-start | bytes 2949128 | tf_op jit(solution)/shard_map/ppermute | solution.py:95
  18.3 5.4 %collective-permute-done.refs_2_ = bf16[6,80,1280]{2,1,0:T(8,128)(2,1)} collective-permute-done((bf16[6,80,1280]{2,1,0:T(8,128)(2,1)}, bf16[6,80,1280]{2,1,0:T(8,128)(2,1)}, u32[]{:S(2)}, u32[]{:S(2)}) %collective-permute-start) | collective-permute-done | bytes 1228832 | tf_op jit(solution)/shard_map/ppermute | solution.py:95
  23.6 5.2 %collective-permute-start.1 = (bf16[3,80,1280]{2,1,0:T(8,128)(2,1)}, bf16[3,80,1280]{2,1,0:T(8,128)(2,1)}, u32[]{:S(2)}, u32[]{:S(2)}) collective-permute-start(bf16[3,80,1280]{2,1,0:T(8,128)(2,1)} %get-tuple-element.39.refs_1_), channel_id=1, source_target_pairs={{0,8},{2,10},{4,12},{6,14},{8,16},{9,1},{10,18},{11,3},{12,20},{13... | collective-permute-start | bytes 1843208 | tf_op jit(solution)/shard_map/ppermute | solution.py:95
  28.8 1.7 %collective-permute-start.6 = (bf16[6,80,1280]{2,1,0:T(8,128)(2,1)}, bf16[6,80,1280]{2,1,0:T(8,128)(2,1)}, u32[]{:S(2)}, u32[]{:S(2)}) collective-permute-start(bf16[6,80,1280]{2,1,0:T(8,128)(2,1)} %collective-permute-done.refs_2_), channel_id=1, source_target_pairs={{8,16},{9,1},{10,18},{11,3},{12,20},{13,5},{14,22},{15,7},{16,24},... | collective-permute-start | bytes 3686408 | tf_op jit(solution)/shard_map/ppermute | solution.py:95
  30.5 4.5 %collective-permute-done.3.refs_1_ = bf16[6,2,32,1280]{3,2,1,0:T(8,128)(2,1)S(1)} collective-permute-done((bf16[6,2,32,1280]{3,2,1,0:T(8,128)(2,1)S(1)}, bf16[6,2,32,1280]{3,2,1,0:T(8,128)(2,1)S(1)}, u32[]{:S(2)}, u32[]{:S(2)}) %collective-permute-start.3) | collective-permute-done | bytes 983072 | tf_op jit(solution)/shard_map/ppermute | solution.py:95
  35.1 2.1 %collective-permute-done.4.refs_2_ = bf16[6,2,32,1280]{3,2,1,0:T(8,128)(2,1)S(1)} collective-permute-done((bf16[6,2,32,1280]{3,2,1,0:T(8,128)(2,1)S(1)}, bf16[6,2,32,1280]{3,2,1,0:T(8,128)(2,1)S(1)}, u32[]{:S(2)}, u32[]{:S(2)}) %collective-permute-start.4) | collective-permute-done | bytes 983072 | tf_op jit(solution)/shard_map/ppermute | solution.py:95
  37.2 2.9 %collective-permute-done.5.refs_3_ = bf16[6,2,32,1280]{3,2,1,0:T(8,128)(2,1)S(1)} collective-permute-done((bf16[6,2,32,1280]{3,2,1,0:T(8,128)(2,1)S(1)}, bf16[6,2,32,1280]{3,2,1,0:T(8,128)(2,1)S(1)}, u32[]{:S(2)}, u32[]{:S(2)}) %collective-permute-start.5) | collective-permute-done | bytes 983072 | tf_op jit(solution)/shard_map/ppermute | solution.py:95
  41.0 2.8 %collective-permute-start.10 = (bf16[6,2,32,1280]{3,2,1,0:T(8,128)(2,1)S(1)}, bf16[6,2,32,1280]{3,2,1,0:T(8,128)(2,1)}, u32[]{:S(2)}, u32[]{:S(2)}) collective-permute-start(bf16[6,2,32,1280]{3,2,1,0:T(8,128)(2,1)S(1)} %collective-permute-done.4.refs_2_), channel_id=1, source_target_pairs={{0,4},{2,6},{5,1},{7,3},{8,12},{10,14},{13,9},{15,11},{16,20},{18,... | collective-permute-start | bytes 2949128 | tf_op jit(solution)/shard_map/ppermute | solution.py:95
  47.7 2.3 %collective-permute-start.13 = (bf16[6,80,1280]{2,1,0:T(8,128)(2,1)}, bf16[6,80,1280]{2,1,0:T(8,128)(2,1)S(1)}, u32[]{:S(2)}, u32[]{:S(2)}) collective-permute-start(bf16[6,80,1280]{2,1,0:T(8,128)(2,1)} %collective-permute-done.refs_2_), channel_id=1, source_target_pairs={{0,1},{1,0},{2,3},{3,2},{4,5},{5,4},{6,7},{7,6},{8,9},{9,8},{10,11... | collective-permute-start | bytes 3686408 | tf_op jit(solution)/shard_map/ppermute | solution.py:95
  50.0 2.8 %collective-permute-start.14 = (bf16[6,80,1280]{2,1,0:T(8,128)(2,1)}, bf16[6,80,1280]{2,1,0:T(8,128)(2,1)S(1)}, u32[]{:S(2)}, u32[]{:S(2)}) collective-permute-start(bf16[6,80,1280]{2,1,0:T(8,128)(2,1)} %collective-permute-done.6.refs_4_.refs_0_), channel_id=1, source_target_pairs={{0,1},{1,0},{2,3},{3,2},{4,5},{5,4},{6,7},{7,6},{8,9},{9,8},{10,11... | collective-permute-start | bytes 3686408 | tf_op jit(solution)/shard_map/ppermute | solution.py:95
  52.8 6.6 %collective-permute-start.15 = (bf16[3,80,1280]{2,1,0:T(8,128)(2,1)}, bf16[3,80,1280]{2,1,0:T(8,128)(2,1)S(1)}, u32[]{:S(2)}, u32[]{:S(2)}) collective-permute-start(bf16[3,80,1280]{2,1,0:T(8,128)(2,1)} %collective-permute-done.1.refs_6_), channel_id=1, source_target_pairs={{0,1},{1,0},{2,3},{3,2},{4,5},{5,4},{6,7},{7,6},{8,9},{9,8},{10,11... | collective-permute-start | bytes 1843208 | tf_op jit(solution)/shard_map/ppermute | solution.py:95
  61.8 6.3 %activation.3 = bf16[10,3,32,1280]{3,2,1,0:T(8,128)(2,1)S(1)} custom-call(s32[4]{0:T(128)S(1)} %copy-done.4, s32[6,2]{1,0:T(8,128)S(1)} %collective-permute-done.11.sizes, f32[1,1280]{1,0:T(1,128)S(1)} %broadcast_in_dim.14.gain, f32[1,1280]{1,0:T(1,128)S(1)} %broadcast_in_dim.15.shift, bf16[1280,128]{1,0:T(8,128)(2,1)S(1)} %fusion.group, ...), custom_call_target="tpu_custom_call" | custom-call | flops 1966080 | bytes 983040 | tf_op jit(solution)/shard_map/activation/pallas_call | solution.py:257
  68.1 6.3 %activation.2 = bf16[10,3,32,1280]{3,2,1,0:T(8,128)(2,1)S(1)} custom-call(s32[4]{0:T(128)S(1)} %copy-done.4, s32[6,2]{1,0:T(8,128)S(1)} %collective-permute-done.11.sizes, f32[1,1280]{1,0:T(1,128)S(1)} %broadcast_in_dim.14.gain, f32[1,1280]{1,0:T(1,128)S(1)} %broadcast_in_dim.15.shift, bf16[1280,128]{1,0:T(8,128)(2,1)S(1)} %fusion.group, ...), custom_call_target="tpu_custom_call" | custom-call | flops 1966080 | bytes 983040 | tf_op jit(solution)/shard_map/activation/pallas_call | solution.py:257
  75.2 11.2 %convolution.2 = (bf16[2,6,32,256]{3,2,1,0:T(8,128)(2,1)S(1)}, bf16[2,6,32,256]{3,2,1,0:T(8,128)(2,1)S(1)}, bf16[2,6,32,256]{3,2,1,0:T(8,128)(2,1)S(1)}, bf16[2,6,32,256]{3,2,1,0:T(8,128)(2,1)S(1)}) custom-call(s32[4]{0:T(128)S(1)} %copy-done.4, bf16[960,1280]{1,0:T(8,128)(2,1)S(1)} %bitcast.8, bf16[960,1280]{1,0:T(8,128)(2,1)S(1)} %bitcast.6, ...), custom_call_target="tpu_custom_call" | custom-call | flops 8493465600 | bytes 5529600 | tf_op jit(solution)/shard_map/convolution/pallas_call | solution.py:413
  86.4 4.4 %collective-permute-start.21 = (bf16[6,80,1280]{2,1,0:T(8,128)(2,1)S(1)}, bf16[6,80,1280]{2,1,0:T(8,128)(2,1)S(1)}, u32[]{:S(2)}, u32[]{:S(2)}) collective-permute-start(bf16[6,80,1280]{2,1,0:T(8,128)(2,1)S(1)} %collective-permute-done.7.refs_2_), channel_id=1, source_target_pairs={{0,1},{1,0},{2,3},{3,2},{4,5},{5,4},{6,7},{7,6},{8,9},{9,8},{10,11... | collective-permute-start | bytes 3686408 | tf_op jit(solution)/shard_map/ppermute | solution.py:95
  91.5 1.7 %collective-permute-start.18 = (bf16[2,6,32,256]{3,2,1,0:T(8,128)(2,1)S(1)}, bf16[2,6,32,256]{3,2,1,0:T(8,128)(2,1)S(1)}, u32[]{:S(2)}, u32[]{:S(2)}) collective-permute-start(bf16[2,6,32,256]{3,2,1,0:T(8,128)(2,1)S(1)} %get-tuple-element.60), channel_id=1, source_target_pairs={{0,1},{1,5},{2,3},{3,7},{4,0},{5,4},{6,2},{7,6},{8,9},{9,13},{10,1... | collective-permute-start | bytes 589832 | tf_op jit(solution)/shard_map/ppermute | solution.py:95
  96.1 6.2 %convolution.3 = (bf16[2,6,32,128]{3,2,1,0:T(8,128)(2,1)S(1)}, bf16[2,6,32,128]{3,2,1,0:T(8,128)(2,1)S(1)}, bf16[2,6,32,128]{3,2,1,0:T(8,128)(2,1)S(1)}, bf16[2,6,32,128]{3,2,1,0:T(8,128)(2,1)S(1)}) custom-call(s32[4]{0:T(128)S(1)} %copy-done.4, bf16[960,1280]{1,0:T(8,128)(2,1)S(1)} %bitcast.9, bf16[960,1280]{1,0:T(8,128)(2,1)S(1)} %bitcast.7, ...), custom_call_target="tpu_custom_call" | custom-call | flops 2831155200 | bytes 1843200 | tf_op jit(solution)/shard_map/convolution/pallas_call | solution.py:413
  103.0 2.5 %collective-permute-start.24 = (bf16[2,6,32,128]{3,2,1,0:T(8,128)(2,1)S(1)}, bf16[2,6,32,128]{3,2,1,0:T(8,128)(2,1)S(1)}, u32[]{:S(2)}, u32[]{:S(2)}) collective-permute-start(bf16[2,6,32,128]{3,2,1,0:T(8,128)(2,1)S(1)} %get-tuple-element.66), channel_id=1, source_target_pairs={{0,1},{1,5},{2,3},{3,7},{4,0},{5,4},{6,2},{7,6},{8,9},{9,13},{10,1... | collective-permute-start | bytes 294920 | tf_op jit(solution)/shard_map/ppermute | solution.py:95
  107.3 3.5 %main_result.1.given = bf16[6,2,32,1280]{3,2,1,0:T(8,128)(2,1)} custom-call(s32[4]{0:T(128)S(1)} %copy-done.4, s32[6,2]{1,0:T(8,128)S(1)} %copy.10.sizes, bf16[6,2,32,1280]{3,2,1,0:T(8,128)(2,1)S(1)} %copy-done.3, f32[6,1,1280]{2,1,0:T(1,128)S(1)} %broadcast_in_dim.6.bias, bf16[2,6,32,256]{3,2,1,0:T(8,128)(2,1)S(1)} %collective-permute-done.17.refs_0_, ...), custom_call_target="tpu_custom_call" | custom-call | flops 1966080 | bytes 1966080 | tf_op jit(solution)/shard_map/main_result/pallas_call | solution.py:483
  110.9 1.9 %collective-permute-done.26.refs_3_ = bf16[2,6,32,128]{3,2,1,0:T(8,128)(2,1)S(1)} collective-permute-done((bf16[2,6,32,128]{3,2,1,0:T(8,128)(2,1)S(1)}, bf16[2,6,32,128]{3,2,1,0:T(8,128)(2,1)S(1)}, u32[]{:S(2)}, u32[]{:S(2)}) %collective-permute-start.26) | collective-permute-done | bytes 98336 | tf_op jit(solution)/shard_map/ppermute | solution.py:95
  112.8 3.4 %last_result.1 = bf16[6,2,32,1280]{3,2,1,0:T(8,128)(2,1)} custom-call(s32[4]{0:T(128)S(1)} %copy-done.4, s32[6,2]{1,0:T(8,128)S(1)} %copy.10.sizes, f32[6,1,1280]{2,1,0:T(1,128)S(1)} %broadcast_in_dim.6.bias, bf16[6,2,32,1280]{3,2,1,0:T(8,128)(2,1)} %main_result.1.given, ...), custom_call_target="tpu_custom_call", output_to_operand_aliasing={{}: (3, {})} | custom-call | flops 491520 | bytes 491520 | tf_op jit(solution)/shard_map/last_result/pallas_call | solution.py:541
  (67 shorter events, 16.7 us)
Async XLA Ops:
  4.1 19.5 %collective-permute-start = (bf16[6,80,1280]{2,1,0:T(8,128)(2,1)}, bf16[6,80,1280]{2,1,0:T(8,128)(2,1)}, u32[]{:S(2)}, u32[]{:S(2)}) collective-permute-start(bf16[6,80,1280]{2,1,0:T(8,128)(2,1)} %get-tuple-element.37.refs_0_), channel_id=1, source_target_pairs={{0,8},{2,10},{4,12},{6,14},{8,16},{9,1},{10,18},{11,3},{12,20},{13... | collective-permute-start | bytes 3686408 | tf_op jit(solution)/shard_map/ppermute | solution.py:95
  10.1 18.7 %collective-permute-start.2 = (bf16[6,2,32,1280]{3,2,1,0:T(8,128)(2,1)S(1)}, bf16[6,2,32,1280]{3,2,1,0:T(8,128)(2,1)S(1)}, u32[]{:S(2)}, u32[]{:S(2)}) collective-permute-start(bf16[6,2,32,1280]{3,2,1,0:T(8,128)(2,1)S(1)} %copy-done.2), channel_id=1, source_target_pairs={{0,0},{1,4},{2,2},{3,6},{4,1},{5,5},{6,3},{7,7},{8,8},{9,12},{10,1... | collective-permute-start | bytes 2949128 | tf_op jit(solution)/shard_map/ppermute | solution.py:95
  10.8 24.2 %collective-permute-start.3 = (bf16[6,2,32,1280]{3,2,1,0:T(8,128)(2,1)S(1)}, bf16[6,2,32,1280]{3,2,1,0:T(8,128)(2,1)S(1)}, u32[]{:S(2)}, u32[]{:S(2)}) collective-permute-start(bf16[6,2,32,1280]{3,2,1,0:T(8,128)(2,1)S(1)} %copy-done.2), channel_id=1, source_target_pairs={{0,4},{1,0},{2,6},{3,2},{4,5},{5,1},{6,7},{7,3},{8,12},{9,8},{10,1... | collective-permute-start | bytes 2949128 | tf_op jit(solution)/shard_map/ppermute | solution.py:95
  13.5 23.6 %collective-permute-start.4 = (bf16[6,2,32,1280]{3,2,1,0:T(8,128)(2,1)S(1)}, bf16[6,2,32,1280]{3,2,1,0:T(8,128)(2,1)S(1)}, u32[]{:S(2)}, u32[]{:S(2)}) collective-permute-start(bf16[6,2,32,1280]{3,2,1,0:T(8,128)(2,1)S(1)} %copy-done.2), channel_id=1, source_target_pairs={{0,2},{2,0},{5,7},{7,5},{8,10},{10,8},{13,15},{15,13},{16,18},{18,... | collective-permute-start | bytes 2949128 | tf_op jit(solution)/shard_map/ppermute | solution.py:95
  17.0 23.1 %collective-permute-start.5 = (bf16[6,2,32,1280]{3,2,1,0:T(8,128)(2,1)S(1)}, bf16[6,2,32,1280]{3,2,1,0:T(8,128)(2,1)S(1)}, u32[]{:S(2)}, u32[]{:S(2)}) collective-permute-start(bf16[6,2,32,1280]{3,2,1,0:T(8,128)(2,1)S(1)} %copy-done.2), channel_id=1, source_target_pairs={{1,2},{3,0},{4,7},{6,5},{9,10},{11,8},{12,15},{14,13},{17,18},{19,... | collective-permute-start | bytes 2949128 | tf_op jit(solution)/shard_map/ppermute | solution.py:95
  23.6 17.4 %collective-permute-start.1 = (bf16[3,80,1280]{2,1,0:T(8,128)(2,1)}, bf16[3,80,1280]{2,1,0:T(8,128)(2,1)}, u32[]{:S(2)}, u32[]{:S(2)}) collective-permute-start(bf16[3,80,1280]{2,1,0:T(8,128)(2,1)} %get-tuple-element.39.refs_1_), channel_id=1, source_target_pairs={{0,8},{2,10},{4,12},{6,14},{8,16},{9,1},{10,18},{11,3},{12,20},{13... | collective-permute-start | bytes 1843208 | tf_op jit(solution)/shard_map/ppermute | solution.py:95
  28.8 21.2 %collective-permute-start.6 = (bf16[6,80,1280]{2,1,0:T(8,128)(2,1)}, bf16[6,80,1280]{2,1,0:T(8,128)(2,1)}, u32[]{:S(2)}, u32[]{:S(2)}) collective-permute-start(bf16[6,80,1280]{2,1,0:T(8,128)(2,1)} %collective-permute-done.refs_2_), channel_id=1, source_target_pairs={{8,16},{9,1},{10,18},{11,3},{12,20},{13,5},{14,22},{15,7},{16,24},... | collective-permute-start | bytes 3686408 | tf_op jit(solution)/shard_map/ppermute | solution.py:95
  41.0 18.4 %collective-permute-start.10 = (bf16[6,2,32,1280]{3,2,1,0:T(8,128)(2,1)S(1)}, bf16[6,2,32,1280]{3,2,1,0:T(8,128)(2,1)}, u32[]{:S(2)}, u32[]{:S(2)}) collective-permute-start(bf16[6,2,32,1280]{3,2,1,0:T(8,128)(2,1)S(1)} %collective-permute-done.4.refs_2_), channel_id=1, source_target_pairs={{0,4},{2,6},{5,1},{7,3},{8,12},{10,14},{13,9},{15,11},{16,20},{18,... | collective-permute-start | bytes 2949128 | tf_op jit(solution)/shard_map/ppermute | solution.py:95
  43.8 15.6 %collective-permute-start.9 = (bf16[6,2,32,1280]{3,2,1,0:T(8,128)(2,1)S(1)}, bf16[6,2,32,1280]{3,2,1,0:T(8,128)(2,1)}, u32[]{:S(2)}, u32[]{:S(2)}) collective-permute-start(bf16[6,2,32,1280]{3,2,1,0:T(8,128)(2,1)S(1)} %collective-permute-done.2.refs_0_), channel_id=1, source_target_pairs={{1,3},{3,1},{4,6},{6,4},{9,11},{11,9},{12,14},{14,12},{17,19},{19,... | collective-permute-start | bytes 2949128 | tf_op jit(solution)/shard_map/ppermute | solution.py:95
  45.4 7.4 %collective-permute-start.8 = (bf16[3,80,1280]{2,1,0:T(8,128)(2,1)}, bf16[3,80,1280]{2,1,0:T(8,128)(2,1)}, u32[]{:S(2)}, u32[]{:S(2)}) collective-permute-start(bf16[3,80,1280]{2,1,0:T(8,128)(2,1)} %collective-permute-done.1.refs_6_), channel_id=1, source_target_pairs={{8,16},{9,1},{10,18},{11,3},{12,20},{13,5},{14,22},{15,7},{16,24},... | collective-permute-start | bytes 1843208 | tf_op jit(solution)/shard_map/ppermute | solution.py:95
  47.7 27.4 %collective-permute-start.13 = (bf16[6,80,1280]{2,1,0:T(8,128)(2,1)}, bf16[6,80,1280]{2,1,0:T(8,128)(2,1)S(1)}, u32[]{:S(2)}, u32[]{:S(2)}) collective-permute-start(bf16[6,80,1280]{2,1,0:T(8,128)(2,1)} %collective-permute-done.refs_2_), channel_id=1, source_target_pairs={{0,1},{1,0},{2,3},{3,2},{4,5},{5,4},{6,7},{7,6},{8,9},{9,8},{10,11... | collective-permute-start | bytes 3686408 | tf_op jit(solution)/shard_map/ppermute | solution.py:95
  50.0 25.1 %collective-permute-start.14 = (bf16[6,80,1280]{2,1,0:T(8,128)(2,1)}, bf16[6,80,1280]{2,1,0:T(8,128)(2,1)S(1)}, u32[]{:S(2)}, u32[]{:S(2)}) collective-permute-start(bf16[6,80,1280]{2,1,0:T(8,128)(2,1)} %collective-permute-done.6.refs_4_.refs_0_), channel_id=1, source_target_pairs={{0,1},{1,0},{2,3},{3,2},{4,5},{5,4},{6,7},{7,6},{8,9},{9,8},{10,11... | collective-permute-start | bytes 3686408 | tf_op jit(solution)/shard_map/ppermute | solution.py:95
  52.8 21.6 %collective-permute-start.15 = (bf16[3,80,1280]{2,1,0:T(8,128)(2,1)}, bf16[3,80,1280]{2,1,0:T(8,128)(2,1)S(1)}, u32[]{:S(2)}, u32[]{:S(2)}) collective-permute-start(bf16[3,80,1280]{2,1,0:T(8,128)(2,1)} %collective-permute-done.1.refs_6_), channel_id=1, source_target_pairs={{0,1},{1,0},{2,3},{3,2},{4,5},{5,4},{6,7},{7,6},{8,9},{9,8},{10,11... | collective-permute-start | bytes 1843208 | tf_op jit(solution)/shard_map/ppermute | solution.py:95
  59.4 15.8 %collective-permute-start.16 = (bf16[3,80,1280]{2,1,0:T(8,128)(2,1)}, bf16[3,80,1280]{2,1,0:T(8,128)(2,1)S(1)}, u32[]{:S(2)}, u32[]{:S(2)}) collective-permute-start(bf16[3,80,1280]{2,1,0:T(8,128)(2,1)} %collective-permute-done.8.refs_8_.refs_4_), channel_id=1, source_target_pairs={{0,1},{1,0},{2,3},{3,2},{4,5},{5,4},{6,7},{7,6},{8,9},{9,8},{10,11... | collective-permute-start | bytes 1843208 | tf_op jit(solution)/shard_map/ppermute | solution.py:95
  59.7 26.6 %collective-permute-start.7 = (bf16[6,80,1280]{2,1,0:T(8,128)(2,1)}, bf16[6,80,1280]{2,1,0:T(8,128)(2,1)S(1)}, u32[]{:S(2)}, u32[]{:S(2)}) collective-permute-start(bf16[6,80,1280]{2,1,0:T(8,128)(2,1)} %collective-permute-done.6.refs_4_.refs_0_), channel_id=1, source_target_pairs={{9,1},{11,3},{13,5},{15,7},{16,24},{18,26},{20,28},{22,30}} | collective-permute-start | bytes 3686408 | tf_op jit(solution)/shard_map/ppermute | solution.py:95
  74.4 11.9 %collective-permute-start.12 = (bf16[3,80,1280]{2,1,0:T(8,128)(2,1)}, bf16[3,80,1280]{2,1,0:T(8,128)(2,1)S(1)}, u32[]{:S(2)}, u32[]{:S(2)}) collective-permute-start(bf16[3,80,1280]{2,1,0:T(8,128)(2,1)} %collective-permute-done.8.refs_8_.refs_4_), channel_id=1, source_target_pairs={{9,1},{11,3},{13,5},{15,7},{16,24},{18,26},{20,28},{22,30}} | collective-permute-start | bytes 1843208 | tf_op jit(solution)/shard_map/ppermute | solution.py:95
  86.4 9.7 %collective-permute-start.21 = (bf16[6,80,1280]{2,1,0:T(8,128)(2,1)S(1)}, bf16[6,80,1280]{2,1,0:T(8,128)(2,1)S(1)}, u32[]{:S(2)}, u32[]{:S(2)}) collective-permute-start(bf16[6,80,1280]{2,1,0:T(8,128)(2,1)S(1)} %collective-permute-done.7.refs_2_), channel_id=1, source_target_pairs={{0,1},{1,0},{2,3},{3,2},{4,5},{5,4},{6,7},{7,6},{8,9},{9,8},{10,11... | collective-permute-start | bytes 3686408 | tf_op jit(solution)/shard_map/ppermute | solution.py:95
  90.8 12.2 %collective-permute-start.17 = (bf16[2,6,32,256]{3,2,1,0:T(8,128)(2,1)S(1)}, bf16[2,6,32,256]{3,2,1,0:T(8,128)(2,1)S(1)}, u32[]{:S(2)}, u32[]{:S(2)}) collective-permute-start(bf16[2,6,32,256]{3,2,1,0:T(8,128)(2,1)S(1)} %get-tuple-element.59), channel_id=1, source_target_pairs={{0,0},{1,4},{2,2},{3,6},{4,1},{5,5},{6,3},{7,7},{8,8},{9,12},{10,1... | collective-permute-start | bytes 589832 | tf_op jit(solution)/shard_map/ppermute | solution.py:95
  91.5 14.0 %collective-permute-start.18 = (bf16[2,6,32,256]{3,2,1,0:T(8,128)(2,1)S(1)}, bf16[2,6,32,256]{3,2,1,0:T(8,128)(2,1)S(1)}, u32[]{:S(2)}, u32[]{:S(2)}) collective-permute-start(bf16[2,6,32,256]{3,2,1,0:T(8,128)(2,1)S(1)} %get-tuple-element.60), channel_id=1, source_target_pairs={{0,1},{1,5},{2,3},{3,7},{4,0},{5,4},{6,2},{7,6},{8,9},{9,13},{10,1... | collective-permute-start | bytes 589832 | tf_op jit(solution)/shard_map/ppermute | solution.py:95
  93.2 13.3 %collective-permute-start.19 = (bf16[2,6,32,256]{3,2,1,0:T(8,128)(2,1)S(1)}, bf16[2,6,32,256]{3,2,1,0:T(8,128)(2,1)S(1)}, u32[]{:S(2)}, u32[]{:S(2)}) collective-permute-start(bf16[2,6,32,256]{3,2,1,0:T(8,128)(2,1)S(1)} %get-tuple-element.61), channel_id=1, source_target_pairs={{0,2},{1,6},{2,0},{3,4},{4,3},{5,7},{6,1},{7,5},{8,10},{9,14},{10,... | collective-permute-start | bytes 589832 | tf_op jit(solution)/shard_map/ppermute | solution.py:95
  94.7 12.6 %collective-permute-start.20 = (bf16[2,6,32,256]{3,2,1,0:T(8,128)(2,1)S(1)}, bf16[2,6,32,256]{3,2,1,0:T(8,128)(2,1)S(1)}, u32[]{:S(2)}, u32[]{:S(2)}) collective-permute-start(bf16[2,6,32,256]{3,2,1,0:T(8,128)(2,1)S(1)} %get-tuple-element.62), channel_id=1, source_target_pairs={{0,3},{1,7},{2,1},{3,5},{4,2},{5,6},{6,0},{7,4},{8,11},{9,15},{10,... | collective-permute-start | bytes 589832 | tf_op jit(solution)/shard_map/ppermute | solution.py:95
  102.3 8.5 %collective-permute-start.23 = (bf16[2,6,32,128]{3,2,1,0:T(8,128)(2,1)S(1)}, bf16[2,6,32,128]{3,2,1,0:T(8,128)(2,1)S(1)}, u32[]{:S(2)}, u32[]{:S(2)}) collective-permute-start(bf16[2,6,32,128]{3,2,1,0:T(8,128)(2,1)S(1)} %get-tuple-element.65), channel_id=1, source_target_pairs={{0,0},{1,4},{2,2},{3,6},{4,1},{5,5},{6,3},{7,7},{8,8},{9,12},{10,1... | collective-permute-start | bytes 294920 | tf_op jit(solution)/shard_map/ppermute | solution.py:95
  103.0 7.9 %collective-permute-start.24 = (bf16[2,6,32,128]{3,2,1,0:T(8,128)(2,1)S(1)}, bf16[2,6,32,128]{3,2,1,0:T(8,128)(2,1)S(1)}, u32[]{:S(2)}, u32[]{:S(2)}) collective-permute-start(bf16[2,6,32,128]{3,2,1,0:T(8,128)(2,1)S(1)} %get-tuple-element.66), channel_id=1, source_target_pairs={{0,1},{1,5},{2,3},{3,7},{4,0},{5,4},{6,2},{7,6},{8,9},{9,13},{10,1... | collective-permute-start | bytes 294920 | tf_op jit(solution)/shard_map/ppermute | solution.py:95
  106.5 6.3 %collective-permute-start.26 = (bf16[2,6,32,128]{3,2,1,0:T(8,128)(2,1)S(1)}, bf16[2,6,32,128]{3,2,1,0:T(8,128)(2,1)S(1)}, u32[]{:S(2)}, u32[]{:S(2)}) collective-permute-start(bf16[2,6,32,128]{3,2,1,0:T(8,128)(2,1)S(1)} %get-tuple-element.68), channel_id=1, source_target_pairs={{0,3},{1,7},{2,1},{3,5},{4,2},{5,6},{6,0},{7,4},{8,11},{9,15},{10,... | collective-permute-start | bytes 294920 | tf_op jit(solution)/shard_map/ppermute | solution.py:95
  (14 other events, 302.2 us)

commit v5 on v3

v5 whole, which is shorter than its diff:
```python
import functools

import jax
import jax.numpy as jnp
from jax import lax
from jax.experimental import pallas as pl
from jax.experimental.pallas import tpu as pltpu
from jax.sharding import PartitionSpec as P

GROUPS = 32
EPS = 1e-05
FRAME_BYTES = 8 << 20


def with_halo(x, sides, width):
    for axis, dim in sides:
        size, length = (lax.axis_size(axis), x.shape[dim])
        up = [(i, (i + 1) % size) for i in range(size - 1)]
        down = [(j, i) for i, j in up]
        last = lax.slice_in_dim(x, length - width, length, axis=dim)
        first = lax.slice_in_dim(x, 0, width, axis=dim)
        before = lax.ppermute(last, axis, up)
        after = lax.ppermute(first, axis, down)
        x = jnp.concatenate([before, x, after], axis=dim)
    return x


def tap_product(window, panel):
    return lax.dot_general(
        window, panel, (((3,), (1,)), ((), ())), preferred_element_type=jnp.float32
    )


def row_plan(latents, buckets, gn_gain, gn_shift, conv_weight, time_bias):
    frames, rows, cols, chans = latents.shape
    members = chans // GROUPS
    row_ids = lax.axis_index("space") * rows + jnp.arange(rows, dtype=jnp.int32)
    col_ids = jnp.arange(cols, dtype=jnp.int32)
    valid = (
        (row_ids[None, :, None] < buckets[:, 0][:, None, None])
        & (col_ids[None, None, :] < buckets[:, 1][:, None, None])
    ).astype(jnp.float32)
    count = (buckets[:, 0] * buckets[:, 1]).astype(jnp.float32)[:, None] * members
    values = latents.astype(jnp.float32).reshape(frames, rows, cols, GROUPS, members)
    weight_mask = valid[:, :, :, None, None]
    total = lax.psum(jnp.sum(values * weight_mask, axis=(1, 2, 4)), "space")
    mean = total / count
    centered = values - mean[:, None, None, :, None]
    spread = lax.psum(jnp.sum(centered * centered * weight_mask, axis=(1, 2, 4)), "space") / count
    normed = (centered / jnp.sqrt(spread[:, None, None, :, None] + EPS)).reshape(
        frames, rows, cols, chans
    )
    normed = normed * gn_gain + gn_shift
    act = (valid[..., None] * jax.nn.silu(normed)).astype(jnp.bfloat16)
    extended = with_halo(act, (("space", 1),), 1)
    padded = jnp.pad(extended, ((0, 0), (0, 0), (1, 1), (0, 0)))

    def add_tap(index, accum):
        window = lax.dynamic_slice(
            padded, (0, index // 3, index % 3, 0), (frames, rows, cols, chans)
        )
        panel = lax.dynamic_index_in_dim(conv_weight, index, 0, keepdims=False)
        return accum + tap_product(window, lax.all_gather(panel, "dp", axis=0, tiled=True))

    conv = lax.fori_loop(0, 9, add_tap, jnp.zeros((frames, rows, cols, chans), jnp.float32))
    conv_out = conv.astype(jnp.bfloat16)
    summed = latents.astype(jnp.float32) + valid[..., None] * (
        conv_out.astype(jnp.float32) + time_bias[:, None, None, :]
    )
    return summed.astype(jnp.bfloat16)


class Grid:
    def __init__(self, mesh):
        dp, space = mesh.shape["dp"], mesh.shape["space"]
        self.X = self.C = 2
        self.Z, self.Y = dp // 2, space // 2
        self.places = [
            (z, x, y, c)
            for z in range(self.Z)
            for x in range(2)
            for y in range(self.Y)
            for c in range(2)
        ]

    def linear(self, z, x, y, c):
        return ((z * 2 + x) * self.Y + y) * 2 + c

    def permute(self, value, target):
        pairs = []
        for place in self.places:
            goal = target(*place)
            if goal is not None:
                pairs.append((self.linear(*place), self.linear(*goal)))
        return lax.ppermute(value, ("dp", "space"), pairs)


LANES = 128
ANY = pl.BlockSpec(memory_space=pl.ANY)
VMEM = pl.BlockSpec(memory_space=pltpu.VMEM)
SMEM = pl.BlockSpec(memory_space=pltpu.SMEM)


def params(mib):
    return pltpu.CompilerParams(vmem_limit_bytes=mib << 20)


def start_all(pairs, sems):
    copies = [pltpu.make_async_copy(src, dst, sems.at[n]) for n, (src, dst) in enumerate(pairs)]
    for copy in copies:
        copy.start()
    return copies


def piece_kernel(part, where, weight, out, sems):
    rows = pl.ds(pl.multiple_of(where[2] * part, part), part)
    pairs = [(weight.at[tap, rows, :], out.at[tap]) for tap in range(out.shape[0])]
    for copy in start_all(pairs, sems):
        copy.wait()


def own_piece(where, weight, part):
    taps, _, chans = weight.shape
    return pl.pallas_call(
        functools.partial(piece_kernel, part),
        out_shape=jax.ShapeDtypeStruct((taps, part, chans), weight.dtype),
        in_specs=[SMEM, ANY],
        out_specs=VMEM,
        scratch_shapes=[pltpu.SemaphoreType.DMA((taps,))],
        compiler_params=params(56),
        cost_estimate=pl.CostEstimate(flops=0, transcendentals=0, bytes_accessed=4 << 20),
        name="own_piece",
    )(where, weight)


def choose(index, sources, target, sem, wait):
    for value, source in enumerate(sources):

        @pl.when(index == value)
        def _(source=source):
            copy = pltpu.make_async_copy(source, target, sem)
            copy.wait() if wait else copy.start()


def exact_dot(value, ones):
    total = None
    for _ in range(3):
        top = value.astype(jnp.bfloat16)
        term = jnp.dot(top, ones, preferred_element_type=jnp.float32)
        total = term if total is None else total + term
        value = value - top.astype(jnp.float32)
    return total


def per_frame(values, rest):
    ids = lax.broadcasted_iota(jnp.int32, (8, LANES), 0)
    out = jnp.full((8, LANES), rest, jnp.float32)
    for f, value in enumerate(values):
        out = jnp.where(ids == f, value, out)
    return out


def cells_of(sizes, f, first_row, rows):
    held = jnp.clip(sizes[f, 0] - first_row, 0, rows)
    return (held * sizes[f, 1]).astype(jnp.float32)


def stats_kernel(where, sizes, latents, group, group_t, out, sums, scale):
    frames, rows, cols, chans = latents.shape
    members = chans // GROUPS
    first_row = rows * (2 * where[2] + where[3])
    col_ids = lax.broadcasted_iota(jnp.int32, (cols, LANES), 0)

    def add(f, centred):
        masks = [
            col_ids < jnp.where(first_row + r < sizes[f, 0], sizes[f, 1], 0) for r in range(rows)
        ]
        for tile in range(chans // LANES):
            lanes = slice(tile * LANES, (tile + 1) * LANES)
            total = jnp.zeros((8, LANES), jnp.float32)
            for r in range(rows):
                v = latents[f, r, :, lanes].astype(jnp.float32)
                if centred:
                    v = v - scale[f, :, lanes]
                    v = v * v
                v = jnp.where(masks[r], v, 0.0)
                total += jnp.sum(v.reshape(cols // 8, 8, LANES), axis=0)
            sums[f, :, lanes] = total
        return 0

    sums[...] = jnp.zeros_like(sums)
    lax.fori_loop(0, frames, lambda f, _: add(f, False), 0)
    counts = [cells_of(sizes, f, first_row, rows) * members for f in range(frames)]
    count = jnp.maximum(per_frame(counts, 1.0), 1.0)
    mean = exact_dot(jnp.sum(sums[...], axis=1), group[...]) / count
    out[0] = mean
    spread_mean = exact_dot(mean, group_t[...])
    for f in range(frames):
        scale[f] = spread_mean[f : f + 1]
    lax.fori_loop(0, frames, lambda f, _: add(f, True), 0)
    out[1] = exact_dot(jnp.sum(sums[...], axis=1), group[...])


def local_stats(where, sizes, latents, group):
    chans = latents.shape[3]
    return pl.pallas_call(
        stats_kernel,
        out_shape=jax.ShapeDtypeStruct((2, 8, LANES), jnp.float32),
        in_specs=[SMEM, SMEM] + [VMEM] * 3,
        out_specs=VMEM,
        scratch_shapes=[
            pltpu.VMEM((8, 8, chans), jnp.float32),
            pltpu.VMEM((8, 1, chans), jnp.float32),
        ],
        compiler_params=params(4),
        cost_estimate=pl.CostEstimate(
            flops=latents.size // 8, transcendentals=0, bytes_accessed=latents.size // 8
        ),
        name="local_stats",
    )(where, sizes, latents, *group)


def block_rows(where, rows, k):
    return rows * (2 * (where[2] ^ (k // 2)) + (where[1] ^ (k % 2)))


def activate(where, sizes, shift, scale, blocks, act, first_round):
    frames, rows, cols, chans = blocks.shape[1:]
    col_ids = lax.broadcasted_iota(jnp.int32, (cols, LANES), 0)

    def body(f, _):
        for tile in range(chans // LANES):
            lanes = slice(tile * LANES, (tile + 1) * LANES)
            middle = scale[f, :, lanes]
            factor = scale[8 + f, :, lanes]
            offset = shift[:, lanes]
            for n in range(2):
                first = block_rows(where, rows, first_round + n)
                for r in range(rows):
                    limit = jnp.where(first + r < sizes[f, 0], sizes[f, 1], 0)
                    v = blocks[n, f, r, :, lanes].astype(jnp.float32)
                    v = 0.5 * ((v - middle) * factor + offset)
                    v = v + v * jnp.tanh(v)
                    v = jnp.where(col_ids < limit, v, 0.0)
                    act[first + r + 1, f, :, lanes] = v.astype(jnp.bfloat16)
        return 0

    lax.fori_loop(0, frames, body, 0)


def fetch(where, choices, blocks, sems):
    away = jnp.where(where[3] == where[1], 0, 1)
    for wait in (False, True):
        for n, pair in enumerate(choices):
            choose(away, pair, blocks.at[n], sems.at[n], wait)


def first_act_kernel(where, sizes, gain, shift, group, group_t, s0, s1, s2, s3, *refs):
    own, first, sibling, second, act, scale, blocks, sems = refs
    frames, rows, cols, chans = blocks.shape[1:]
    members = chans // GROUPS
    fetch(where, [(own, first), (sibling, second)], blocks, sems)
    whole = per_frame(
        [(sizes[f, 0] * sizes[f, 1] * members).astype(jnp.float32) for f in range(frames)], 1.0
    )
    counts = [
        per_frame(
            [
                cells_of(sizes, f, block_rows(where, rows, k), rows) * members
                for f in range(frames)
            ],
            0.0,
        )
        for k in range(4)
    ]
    stats = (s0, s1, s2, s3)
    mean = sum(count * stat[0] for count, stat in zip(counts, stats)) / whole
    squares = sum(
        stat[1] + count * (stat[0] - mean) * (stat[0] - mean)
        for count, stat in zip(counts, stats)
    )
    factor = exact_dot(1.0 / jnp.sqrt(squares / whole + EPS), group_t[...]) * gain[...]
    middle = exact_dot(mean, group_t[...])
    del group
    for f in range(frames):
        scale[f] = middle[f : f + 1]
        scale[8 + f] = factor[f : f + 1]
    edge = jnp.zeros((frames, cols, chans), jnp.bfloat16)
    act[0] = edge
    act[act.shape[0] - 1] = edge
    activate(where, sizes, shift, scale, blocks, act, 0)


def second_act_kernel(where, sizes, shift, scale, given, *refs):
    first, relay0, second, relay1, act, blocks, sems = refs
    del given
    fetch(where, [(first, relay0), (second, relay1)], blocks, sems)
    activate(where, sizes, shift, scale, blocks, act, 2)


def act_params(frames, rows, cols, chans):
    elements = 2 * frames * rows * cols * chans
    return dict(
        compiler_params=params(16),
        cost_estimate=pl.CostEstimate(
            flops=elements // 8, transcendentals=0, bytes_accessed=elements // 8
        ),
    )


def first_activation(where, sizes, gain, shift, group, stats, blocks):
    frames, rows, cols, chans = blocks[0].shape
    return pl.pallas_call(
        first_act_kernel,
        out_shape=[
            jax.ShapeDtypeStruct((4 * rows + 2, frames, cols, chans), jnp.bfloat16),
            jax.ShapeDtypeStruct((16, 1, chans), jnp.float32),
        ],
        in_specs=[SMEM, SMEM] + [VMEM] * 8 + [ANY] * 4,
        out_specs=[VMEM] * 2,
        scratch_shapes=[
            pltpu.VMEM((2, frames, rows, cols, chans), jnp.bfloat16),
            pltpu.SemaphoreType.DMA((2,)),
        ],
        name="first_activation",
        **act_params(frames, rows, cols, chans),
    )(where, sizes, gain[None, :], shift[None, :], *group, *stats, *blocks)


def second_activation(where, sizes, shift, scale, act, blocks):
    frames, rows, cols, chans = blocks[0].shape
    return pl.pallas_call(
        second_act_kernel,
        out_shape=jax.ShapeDtypeStruct(act.shape, act.dtype),
        in_specs=[SMEM, SMEM] + [VMEM] * 3 + [ANY] * 4,
        out_specs=VMEM,
        scratch_shapes=[
            pltpu.VMEM((2, frames, rows, cols, chans), jnp.bfloat16),
            pltpu.SemaphoreType.DMA((2,)),
        ],
        input_output_aliases={4: 0},
        name="second_activation",
        **act_params(frames, rows, cols, chans),
    )(where, sizes, shift[None, :], scale, act, *blocks)


def group_matrix(chans):
    member = jnp.arange(chans, dtype=jnp.int32)[:, None] // (chans // GROUPS)
    return (member == jnp.arange(LANES, dtype=jnp.int32)[None, :]).astype(jnp.bfloat16)


def shifted_sum(left, middle, right, cols):
    size = middle.shape[0]
    col = lax.broadcasted_iota(jnp.int32, middle.shape, 0) % cols
    left = jnp.where(col == 0, 0.0, pltpu.roll(left, 1, 0))
    right = jnp.where(col == cols - 1, 0.0, pltpu.roll(right, size - 1, 0))
    return middle + left + right


def window(act, base, dr, chunk, line, cols):
    return act[pl.ds(pl.multiple_of(base + dr * line, cols), chunk), :]


def product(rows, weight):
    return lax.dot_general(
        rows, weight, (((1,), (1,)), ((), ())), preferred_element_type=jnp.float32
    )


def give_rows(where, result, outs, rows):
    width = result.shape[3]
    for k, out in enumerate(outs):
        out[:, :, :, 0:width] = result[pl.ds(block_rows(where, rows, k), rows)]
        if out.shape[3] > width:
            blank = out.shape[:3] + (out.shape[3] - width,)
            out[:, :, :, width:] = jnp.zeros(blank, out.dtype)


def all_rows(act, result, cols, compute):
    height, frames = result.shape[:2]
    line = frames * cols
    chunk = height * line // 2
    lines = chunk // line

    def body(m, _):
        base = pl.multiple_of(m * chunk, chunk)
        value = compute(act, base, chunk, line).astype(jnp.bfloat16)
        result[pl.ds(m * lines, lines)] = value.reshape(lines, frames, cols, value.shape[1])
        return 0

    lax.fori_loop(0, 2, body, 0)


def from_below(hop, c):
    return 2 * hop + c


def from_above(hop, c):
    return 2 * hop + 1 - c


def main_kernel(rows, cols, part, where, act, *refs):
    z, c = where[0], where[3]
    own, hops, refs = refs[0], refs[1:5], refs[5:]
    outs, weight, result, sems = refs[:4], *refs[4:]
    low = jnp.where(z < 2, 0, 1)

    def rows_of(place):
        return pl.ds(pl.multiple_of(place * part, part), part)

    first = jnp.where(z == 0, from_above(0, c), from_below(0, c))
    second = jnp.where(
        z == 0, from_above(1, c), jnp.where(z == 3, from_below(1, c), from_above(0, c))
    )
    first_rows = rows_of(jnp.where(z == 0, 1, z - 1) - low)
    second_rows = rows_of(jnp.where(z < 3, 2, 0))
    for wait in (False, True):
        choose(0, (own,), weight.at[:, rows_of(z - low), :], sems.at[0], wait)
        choose(first, hops[:2], weight.at[:, first_rows, :], sems.at[1], wait)
        choose(second, hops, weight.at[:, second_rows, :], sems.at[2], wait)

    def compute(act, base, chunk, line):
        columns = []
        for dc in range(3):
            total = None
            for dr in range(3):
                term = product(window(act, base, dr, chunk, line, cols), weight[3 * dr + dc])
                total = term if total is None else total + term
            columns.append(total)
        return shifted_sum(*columns, cols)

    all_rows(act, result, cols, compute)
    give_rows(where, result, outs, rows)


def farthest(where):
    z, c = where[0], where[3]
    return jnp.where(
        z < 2,
        jnp.where(z == 0, from_above(1, c), from_above(0, c)),
        jnp.where(z == 2, from_below(0, c), from_below(1, c)),
    )


def tap_rows(act, weight, part, base, chunk, line, cols, first):
    total = None
    for n in range(weight.shape[0] // 3):
        taps = weight[3 * n : 3 * n + 3].reshape(3 * part, weight.shape[2])
        term = product(window(act, base, first + n, chunk, line, cols), taps)
        total = term if total is None else total + term
    return total


def last_kernel(rows, cols, part, where, act, *refs):
    hops, refs = refs[:4], refs[4:]
    outs, weight, result, sems = refs[:4], *refs[4:]
    for wait in (False, True):
        choose(farthest(where), hops, weight, sems.at[0], wait)

    def compute(act, base, chunk, line):
        total = tap_rows(act, weight, part, base, chunk, line, cols, 0)
        columns = [total[:, dc * part : (dc + 1) * part] for dc in range(3)]
        return shifted_sum(*columns, cols)

    all_rows(act, result, cols, compute)
    give_rows(where, result, outs, rows)


def convolution(kernel, where, act, weights, part, rows, shards):
    padded, frames, cols, chans = act.shape
    height = padded - 2
    taps, width = 9, part * shards
    lanes = -(-width // LANES) * LANES
    out = jax.ShapeDtypeStruct((rows, frames, cols, lanes), jnp.bfloat16)
    return pl.pallas_call(
        functools.partial(kernel, rows, cols, part),
        out_shape=[out] * 4,
        in_specs=[SMEM, VMEM] + [ANY] * len(weights),
        out_specs=[VMEM] * 4,
        scratch_shapes=[
            pltpu.VMEM((taps, width, chans), jnp.bfloat16),
            pltpu.VMEM((height, frames, cols, width), jnp.bfloat16),
            pltpu.SemaphoreType.DMA((3,)),
        ],
        compiler_params=params(24),
        cost_estimate=pl.CostEstimate(
            flops=height * frames * cols, transcendentals=0, bytes_accessed=width * chans
        ),
        name="convolution",
    )(where, act.reshape(padded * frames * cols, chans), *weights)


def place_of(where, k):
    return 2 * (where[3] ^ (k % 2)) + (where[2] ^ (k // 2))


def bring(where, parts, buffer, sems):
    copies = [
        pltpu.make_async_copy(part, buffer.at[place_of(where, k)], sems.at[k])
        for k, part in enumerate(parts)
    ]
    for copy in copies:
        copy.start()
    for copy in copies:
        copy.wait()


def window_of(low, chans):
    quarter = chans // 4
    wide = -(-quarter // LANES) * LANES
    if low:
        return slice(0, wide), slice(0, quarter)
    return slice(chans - wide, chans), slice(wide - quarter, wide)


def main_result_kernel(where, sizes, latents, bias, *refs):
    parts, out, slab, buffer, sems = refs[:4], *refs[4:]
    frames, rows, cols, chans = latents.shape
    part = chans // 16
    bring(where, parts, buffer, sems)
    first_row = rows * (2 * where[2] + where[3])
    col_ids = lax.broadcasted_iota(jnp.int32, (cols, 12 * part), 0)

    def finish(low):
        lanes = slice(low * 4 * part, (low + 3) * 4 * part)
        rest = slice(12 * part, chans) if low == 0 else slice(0, 4 * part)
        view, _ = window_of(low, chans)

        def body(f, _):
            for r in range(rows):
                chunks = [
                    buffer[q, r, f, :, n * part : (n + 1) * part].astype(jnp.float32)
                    for n in range(3)
                    for q in range(4)
                ]
                value = jnp.concatenate(chunks, axis=1) + bias[f, :, lanes]
                limit = jnp.where(first_row + r < sizes[f, 0], sizes[f, 1], 0)
                value = jnp.where(col_ids < limit, value, 0.0)
                value += latents[f, r, :, lanes].astype(jnp.float32)
                out[f, r, :, lanes] = value.astype(jnp.bfloat16)
                out[f, r, :, rest] = latents[f, r, :, rest]
                slab[f, r] = out[f, r, :, view]
            return 0

        lax.fori_loop(0, frames, body, 0)

    for low in (0, 1):
        pl.when((where[0] >= 2) == bool(low))(functools.partial(finish, low))


def main_result(where, sizes, latents, bias, parts):
    frames, rows, cols, chans = latents.shape
    view, _ = window_of(1, chans)
    return pl.pallas_call(
        main_result_kernel,
        out_shape=[
            jax.ShapeDtypeStruct(latents.shape, latents.dtype),
            jax.ShapeDtypeStruct((frames, rows, cols, view.stop), latents.dtype),
        ],
        in_specs=[SMEM, SMEM, VMEM, VMEM] + [ANY] * 4,
        out_specs=[VMEM] * 2,
        scratch_shapes=[
            pltpu.VMEM((4,) + parts[0].shape, jnp.bfloat16),
            pltpu.SemaphoreType.DMA((4,)),
        ],
        compiler_params=params(12),
        cost_estimate=pl.CostEstimate(
            flops=latents.size // 8, transcendentals=0, bytes_accessed=latents.size // 8
        ),
        name="main_result",
    )(where, sizes, latents, bias, *parts)


def last_result_kernel(where, sizes, bias, slab, p0, p1, p2, p3, given, out, done, sems):
    del given
    frames, rows, cols, wide = slab.shape
    chans = out.shape[3]
    part = chans // 16
    y, c = where[2], where[3]
    first_row = rows * (2 * y + c)
    col_ids = lax.broadcasted_iota(jnp.int32, (cols, 4 * part), 0)

    def part_of(q, f, r):
        pieces = [ref[r, f, :, 0:part].astype(jnp.float32) for ref in (p0, p1, p2, p3)]
        near = [pieces[0], pieces[1]] if q // 2 == 0 else [pieces[1], pieces[0]]
        other = [pieces[2], pieces[3]] if q // 2 == 0 else [pieces[3], pieces[2]]
        pair = [jnp.where(c == 0, *near), jnp.where(c == 0, *other)]
        return jnp.where(y == q % 2, pair[0], pair[1])

    def finish(low):
        view, inner = window_of(low, chans)
        lanes = slice(0, 4 * part) if low else slice(chans - 4 * part, chans)
        copies = []
        for f in range(frames):
            for r in range(rows):
                value = jnp.concatenate([part_of(q, f, r) for q in range(4)], axis=1)
                value = value + bias[f, :, lanes]
                limit = jnp.where(first_row + r < sizes[f, 0], sizes[f, 1], 0)
                value = jnp.where(col_ids < limit, value, 0.0)
                value += slab[f, r, :, inner].astype(jnp.float32)
                done[f, r] = slab[f, r]
                done[f, r, :, inner] = value.astype(jnp.bfloat16)
            copies.append(
                pltpu.make_async_copy(done.at[f], out.at[f, :, :, view], sems.at[f])
            )
            copies[-1].start()
        for copy in copies:
            copy.wait()

    for low in (0, 1):
        pl.when((where[0] >= 2) == bool(low))(functools.partial(finish, low))


def last_result(where, sizes, bias, given, slab, parts):
    return pl.pallas_call(
        last_result_kernel,
        out_shape=jax.ShapeDtypeStruct(given.shape, given.dtype),
        in_specs=[SMEM, SMEM, VMEM, VMEM] + [VMEM] * 4 + [ANY],
        out_specs=ANY,
        scratch_shapes=[
            pltpu.VMEM(slab.shape, slab.dtype),
            pltpu.SemaphoreType.DMA((slab.shape[0],)),
        ],
        input_output_aliases={8: 0},
        compiler_params=params(4),
        cost_estimate=pl.CostEstimate(
            flops=given.size, transcendentals=0, bytes_accessed=given.size
        ),
        name="last_result",
    )(where, sizes, bias, slab, *parts, given)


def frame_plan(grid, latents, buckets, gn_gain, gn_shift, conv_weight, time_bias):
    frames, rows, cols, chans = latents.shape
    part = conv_weight.shape[1] // 2
    dp_index, space_index = lax.axis_index("dp"), lax.axis_index("space")
    z, x = dp_index // 2, dp_index % 2
    y, c = space_index // 2, space_index % 2
    where = jnp.stack([z, x, y, c]).astype(jnp.int32)

    def spread(values):
        return [
            grid.permute(v, lambda z, x, y, c, k=k: (z, c, y ^ (k // 2), x ^ (k % 2)))
            for k, v in enumerate(values)
        ]

    def hop(value, step):
        def target(z, x, y, c):
            if c == 0:
                return (z + 1, x, y, c) if step - 1 <= z < 3 else None
            return (z - 1, x, y, c) if 1 <= z <= 4 - step else None

        return grid.permute(value, target)

    def swap(value):
        return grid.permute(value, lambda z, x, y, c: (z, x, y, 1 - c))

    group = group_matrix(chans)
    group = (group, group.T)

    piece = own_piece(where, conv_weight, part)
    hop1 = hop(piece, 1)
    first = grid.permute(
        latents, lambda z, x, y, c: (z, x, 1 - y, c) if c == x else (z, 1 - x, y, 1 - c)
    )
    second = grid.permute(
        latents, lambda z, x, y, c: (z, 1 - x, y, c) if c == x else (z, x, 1 - y, 1 - c)
    )
    sibling = grid.permute(latents, lambda z, x, y, c: (z, x, y, 1 - c) if c != x else None)
    stats = local_stats(where, buckets, latents, group)
    stats = [
        grid.permute(stats, lambda z, x, y, c, k=k: (z, c ^ (k % 2), y ^ (k // 2), x))
        for k in range(4)
    ]
    sizes = grid.permute(buckets, lambda z, x, y, c: (z, c, y, x))
    hop1, first, sibling, stats, sizes = lax.optimization_barrier(
        (hop1, first, sibling, stats, sizes)
    )

    hop2 = hop(hop1, 2)
    swap1 = swap(hop1)
    relay0 = grid.permute(first, lambda z, x, y, c: (z, x, 1 - y, c) if c != x else None)
    relay1 = grid.permute(first, lambda z, x, y, c: (z, 1 - x, y, c) if c == x else None)
    act, scale = first_activation(
        where, sizes, gn_gain, gn_shift, group, stats, [latents, first, sibling, second]
    )
    hop2, relay0, relay1, act = lax.optimization_barrier((hop2, relay0, relay1, act))

    hop3 = hop(hop2, 3)
    swap2 = swap(hop2)
    act = second_activation(
        where, sizes, gn_shift, scale, act, [first, relay0, second, relay1]
    )
    near = [hop1, swap1, hop2, swap2]
    main = convolution(main_kernel, where, act, [piece] + near, part, rows, 3)

    main = spread(main)
    hop3, main[0] = lax.optimization_barrier((hop3, main[0]))
    swap3 = swap(hop3)
    last = convolution(last_kernel, where, act, [hop2, swap2, hop3, swap3], part, rows, 1)
    bias = time_bias[:, None, :]
    result, slab = main_result(where, buckets, latents, bias, main)
    return last_result(where, buckets, bias, result, slab, spread(last))


def solution(mesh):
    in_specs = (
        P("dp", "space", None, None),
        P("dp", None),
        P(),
        P(),
        P(None, "dp", None),
        P("dp", None),
    )
    grid = Grid(mesh)

    def body(latents, *rest):
        if (grid.Z, grid.Y) == (4, 2) and latents.shape[1] == 2:
            return frame_plan(grid, latents, *rest)
        return row_plan(latents, *rest)

    return jax.shard_map(
        body, mesh=mesh, in_specs=in_specs, out_specs=P("dp", "space", None, None), check_vma=False
    )
```

time: 175 us -> 105 us (0.60)
  Pallas kernels: 95.1 us -> 33.7 us
  waiting for transfers between devices: 32 us -> 19 us
  starting transfers between devices: 42.1 us -> 50.4 us
  local copies, waits for them, and re-layouts: 3.28 us -> 0.16 us
    pallas_call x1, Pallas kernels: 57.7 us -> 3.68 us  [own_piece(): pl.pallas_call(functools.partial(piece_kernel, part), out_shape=jax.Shape...]
    ppermute x21 -> x24, waiting for transfers between devices: 32 us -> 19 us  [permute(): return lax.ppermute(value, ('dp', 'space'), pairs)]
    ppermute x21 -> x24, starting transfers between devices: 42.1 us -> 50.4 us  [permute(): return lax.ppermute(value, ('dp', 'space'), pairs)]
    pallas_call x3 -> x4, Pallas kernels: 16 us -> 12.3 us  [the longest x1 3.57 us: first_activation(): pl.pallas_call(first_act_kernel, out_shape=[jax.ShapeDtypeStruct((4 * row...]
    unnamed x22 -> x15, local copies, waits for them, and re-layouts: 3.15 us -> 0.12 us
    pallas_call x2, Pallas kernels: 17.9 us -> 15.5 us  [convolution(): pl.pallas_call(functools.partial(kernel, rows, cols, part), out_shape=[ou...]
  transfers between devices with their start and end apart: 21 -> 24, of which waited for: 5 -> 5; matrix products, arithmetic and copies ran while one was open for 1% -> 0% of each run, Pallas kernels for 19% -> 27%
where the time goes in v5:
time: 105 us
  starting transfers between devices  50.4 us (48%)
  Pallas kernels  33.7 us (32%)
  waiting for transfers between devices  19 us (18%)
    ppermute x24, starting transfers between devices, permute(): return lax.ppermute(value, ('dp', 'space'), pairs)  50.4 us
    ppermute x24, waiting for transfers between devices, permute(): return lax.ppermute(value, ('dp', 'space'), pairs)  19 us
    pallas_call x2, Pallas kernels, convolution(): pl.pallas_call(functools.partial(kernel, rows, cols, part), out_shape=[ou...  15.5 us
    pallas_call x1, Pallas kernels, own_piece(): pl.pallas_call(functools.partial(piece_kernel, part), out_shape=jax.Shape...  3.68 us
    pallas_call x1, Pallas kernels, first_activation(): pl.pallas_call(first_act_kernel, out_shape=[jax.ShapeDtypeStruct((4 * row...  3.57 us
    pallas_call x1, Pallas kernels, main_result(): pl.pallas_call(main_result_kernel, out_shape=[jax.ShapeDtypeStruct(latent...  3.52 us
    pallas_call x1, Pallas kernels, second_activation(): pl.pallas_call(second_act_kernel, out_shape=jax.ShapeDtypeStruct(act.shap...  3.06 us
    pallas_call x1, Pallas kernels, last_result(): pl.pallas_call(last_result_kernel, out_shape=jax.ShapeDtypeStruct(given.s...  2.23 us
  transfers between devices with their start and end apart: 24, of which 5 were waited for; matrix products, arithmetic and copies ran while one was open for 0% of the time, Pallas kernels for 27%

profile of v5, /device:TPU:0, one launch (start us, length us, event | category | flops | bytes accessed | tf_op | source)
XLA Modules:
  0.0 104.6 jit_solution(11297399876200044570)
XLA Ops:
  0.7 3.7 %own_piece.1.refs_0_ = bf16[9,80,1280]{2,1,0:T(8,128)(2,1)} custom-call(s32[4]{0:T(128)} %pad_add_fusion.where, bf16[9,160,1280]{2,1,0:T(8,128)(2,1)} %weight.1), custom_call_target="tpu_custom_call" | custom-call | bytes 4194304 | tf_op jit(solution)/shard_map/own_piece/pallas_call | solution.py:124
  4.4 6.2 %collective-permute-start = (bf16[9,80,1280]{2,1,0:T(8,128)(2,1)}, bf16[9,80,1280]{2,1,0:T(8,128)(2,1)}, u32[]{:S(2)}, u32[]{:S(2)}) collective-permute-start(bf16[9,80,1280]{2,1,0:T(8,128)(2,1)} %own_piece.1.refs_0_), channel_id=1, source_target_pairs={{0,8},{2,10},{4,12},{6,14},{8,16},{9,1},{10,18},{11,3},{12,20},{13... | collective-permute-start | bytes 5529608 | tf_op jit(solution)/shard_map/ppermute | solution.py:95
  10.5 1.5 %collective-permute-start.1 = (bf16[6,2,32,1280]{3,2,1,0:T(8,128)(2,1)S(1)}, bf16[6,2,32,1280]{3,2,1,0:T(8,128)(2,1)S(1)}, u32[]{:S(2)}, u32[]{:S(2)}) collective-permute-start(bf16[6,2,32,1280]{3,2,1,0:T(8,128)(2,1)S(1)} %copy-done), channel_id=1, source_target_pairs={{0,2},{1,4},{2,0},{3,6},{4,1},{5,7},{6,3},{7,5},{8,10},{9,12},{10,... | collective-permute-start | bytes 2949128 | tf_op jit(solution)/shard_map/ppermute | solution.py:95
  14.5 2.1 %local_stats.1 = f32[2,8,128]{2,1,0:T(8,128)S(1)} custom-call(s32[4]{0:T(128)S(1)} %copy-done.2, s32[6,2]{1,0:T(8,128)S(1)} %copy.12.sizes, bf16[6,2,32,1280]{3,2,1,0:T(8,128)(2,1)S(1)} %copy-done, bf16[1280,128]{1,0:T(8,128)(2,1)S(1)} %fusion.group, bf16[128,1280]{1,0:T(8,128)(2,1)S(1)} %fusion.1.group_t), custom_call_target="tpu_custom_call" | custom-call | flops 61440 | bytes 61440 | tf_op jit(solution)/shard_map/local_stats/pallas_call | solution.py:206
  17.3 8.3 %collective-permute-start.4 = (f32[2,8,128]{2,1,0:T(8,128)S(1)}, f32[2,8,128]{2,1,0:T(8,128)S(1)}, u32[]{:S(2)}, u32[]{:S(2)}) collective-permute-start(f32[2,8,128]{2,1,0:T(8,128)S(1)} %local_stats.1), channel_id=1, source_target_pairs={{0,4},{1,0},{2,6},{3,2},{4,5},{5,1},{6,7},{7,3},{8,12},{9,8},{10,1... | collective-permute-start | bytes 24584 | tf_op jit(solution)/shard_map/ppermute | solution.py:95
  25.6 1.5 %collective-permute-start.5 = (f32[2,8,128]{2,1,0:T(8,128)S(1)}, f32[2,8,128]{2,1,0:T(8,128)S(1)}, u32[]{:S(2)}, u32[]{:S(2)}) collective-permute-start(f32[2,8,128]{2,1,0:T(8,128)S(1)} %local_stats.1), channel_id=1, source_target_pairs={{0,2},{1,6},{2,0},{3,4},{4,3},{5,7},{6,1},{7,5},{8,10},{9,14},{10,... | collective-permute-start | bytes 24584 | tf_op jit(solution)/shard_map/ppermute | solution.py:95
  27.1 3.1 %collective-permute-start.6 = (f32[2,8,128]{2,1,0:T(8,128)S(1)}, f32[2,8,128]{2,1,0:T(8,128)S(1)}, u32[]{:S(2)}, u32[]{:S(2)}) collective-permute-start(f32[2,8,128]{2,1,0:T(8,128)S(1)} %local_stats.1), channel_id=1, source_target_pairs={{0,6},{1,2},{2,4},{3,0},{4,7},{5,3},{6,5},{7,1},{8,14},{9,10},{10,... | collective-permute-start | bytes 24584 | tf_op jit(solution)/shard_map/ppermute | solution.py:95
  30.2 1.4 %collective-permute-done.6.s3 = f32[2,8,128]{2,1,0:T(8,128)S(1)} collective-permute-done((f32[2,8,128]{2,1,0:T(8,128)S(1)}, f32[2,8,128]{2,1,0:T(8,128)S(1)}, u32[]{:S(2)}, u32[]{:S(2)}) %collective-permute-start.6) | collective-permute-done | bytes 8224 | tf_op jit(solution)/shard_map/ppermute | solution.py:95
  32.4 2.3 %collective-permute-start.11 = (bf16[6,2,32,1280]{3,2,1,0:T(8,128)(2,1)S(1)}, bf16[6,2,32,1280]{3,2,1,0:T(8,128)(2,1)S(1)}, u32[]{:S(2)}, u32[]{:S(2)}) collective-permute-start(bf16[6,2,32,1280]{3,2,1,0:T(8,128)(2,1)S(1)} %copy-done), channel_id=1, source_target_pairs={{0,4},{1,2},{2,6},{3,0},{4,7},{5,1},{6,5},{7,3},{8,12},{9,10},{10,... | collective-permute-start | bytes 2949128 | tf_op jit(solution)/shard_map/ppermute | solution.py:95
  34.7 2.0 %collective-permute-start.10 = (bf16[6,2,32,1280]{3,2,1,0:T(8,128)(2,1)S(1)}, bf16[6,2,32,1280]{3,2,1,0:T(8,128)(2,1)S(1)}, u32[]{:S(2)}, u32[]{:S(2)}) collective-permute-start(bf16[6,2,32,1280]{3,2,1,0:T(8,128)(2,1)S(1)} %collective-permute-done.1.refs_1_.refs_0_), channel_id=1, source_target_pairs={{0,4},{2,6},{5,1},{7,3},{8,12},{10,14},{13,9},{15,11},{16,20},{18,... | collective-permute-start | bytes 2949128 | tf_op jit(solution)/shard_map/ppermute | solution.py:95
  37.6 8.7 %collective-permute-done.11.refs_3_.refs_2_ = bf16[6,2,32,1280]{3,2,1,0:T(8,128)(2,1)S(1)} collective-permute-done((bf16[6,2,32,1280]{3,2,1,0:T(8,128)(2,1)S(1)}, bf16[6,2,32,1280]{3,2,1,0:T(8,128)(2,1)S(1)}, u32[]{:S(2)}, u32[]{:S(2)}) %collective-permute-start.11) | collective-permute-done | bytes 983072 | tf_op jit(solution)/shard_map/ppermute | solution.py:95
  46.3 3.6 %first_activation.1 = (bf16[10,6,32,1280]{3,2,1,0:T(8,128)(2,1)S(1)}, f32[16,1,1280]{2,1,0:T(1,128)S(1)}) custom-call(s32[4]{0:T(128)S(1)} %copy-done.2, s32[6,2]{1,0:T(8,128)S(1)} %collective-permute-done.7.sizes, f32[1,1280]{1,0:T(1,128)S(1)} %broadcast_in_dim.13.gain, f32[1,1280]{1,0:T(1,128)S(1)} %broadcast_in_dim.14.shift, ...), custom_call_target="tpu_custom_call" | custom-call | flops 122880 | bytes 122880 | tf_op jit(solution)/shard_map/first_activation/pallas_call | solution.py:313
  49.9 7.0 %collective-permute-done.10.refs_3_ = bf16[6,2,32,1280]{3,2,1,0:T(8,128)(2,1)S(1)} collective-permute-done((bf16[6,2,32,1280]{3,2,1,0:T(8,128)(2,1)S(1)}, bf16[6,2,32,1280]{3,2,1,0:T(8,128)(2,1)S(1)}, u32[]{:S(2)}, u32[]{:S(2)}) %collective-permute-start.10) | collective-permute-done | bytes 983072 | tf_op jit(solution)/shard_map/ppermute | solution.py:95
  57.6 3.1 %second_activation.1 = bf16[10,6,32,1280]{3,2,1,0:T(8,128)(2,1)S(1)} custom-call(s32[4]{0:T(128)S(1)} %copy-done.2, s32[6,2]{1,0:T(8,128)S(1)} %collective-permute-done.7.sizes, f32[1,1280]{1,0:T(1,128)S(1)} %broadcast_in_dim.14.shift, f32[16,1,1280]{2,1,0:T(1,128)S(1)} %get-tuple-element.41.scale, ...), custom_call_target="tpu_custom_call", output_to_operand_aliasing={{}: (4, {})} | custom-call | flops 122880 | bytes 122880 | tf_op jit(solution)/shard_map/second_activation/pallas_call | solution.py:332
  60.7 10.6 %convolution.2 = (bf16[2,6,32,256]{3,2,1,0:T(8,128)(2,1)S(1)}, bf16[2,6,32,256]{3,2,1,0:T(8,128)(2,1)S(1)}, bf16[2,6,32,256]{3,2,1,0:T(8,128)(2,1)S(1)}, bf16[2,6,32,256]{3,2,1,0:T(8,128)(2,1)S(1)}) custom-call(s32[4]{0:T(128)S(1)} %copy-done.2, bf16[1920,1280]{1,0:T(8,128)(2,1)S(1)} %bitcast.5, bf16[9,80,1280]{2,1,0:T(8,128)(2,1)S(1)} %copy-done.1, ...), custom_call_target="tpu_custom_call" | custom-call | flops 1536 | bytes 307200 | tf_op jit(solution)/shard_map/convolution/pallas_call | solution.py:475
  72.0 10.4 %collective-permute-start.19 = (bf16[9,80,1280]{2,1,0:T(8,128)(2,1)S(1)}, bf16[9,80,1280]{2,1,0:T(8,128)(2,1)S(1)}, u32[]{:S(2)}, u32[]{:S(2)}) collective-permute-start(bf16[9,80,1280]{2,1,0:T(8,128)(2,1)S(1)} %collective-permute-done.12.refs_2_), channel_id=1, source_target_pairs={{0,1},{1,0},{2,3},{3,2},{4,5},{5,4},{6,7},{7,6},{8,9},{9,8},{10,11... | collective-permute-start | bytes 5529608 | tf_op jit(solution)/shard_map/ppermute | solution.py:95
  82.4 1.5 %collective-permute-start.17 = (bf16[2,6,32,256]{3,2,1,0:T(8,128)(2,1)S(1)}, bf16[2,6,32,256]{3,2,1,0:T(8,128)(2,1)S(1)}, u32[]{:S(2)}, u32[]{:S(2)}) collective-permute-start(bf16[2,6,32,256]{3,2,1,0:T(8,128)(2,1)S(1)} %get-tuple-element.48), channel_id=1, source_target_pairs={{0,2},{1,6},{2,0},{3,4},{4,3},{5,7},{6,1},{7,5},{8,10},{9,14},{10,... | collective-permute-start | bytes 589832 | tf_op jit(solution)/shard_map/ppermute | solution.py:95
  84.0 2.1 %collective-permute-start.18 = (bf16[2,6,32,256]{3,2,1,0:T(8,128)(2,1)S(1)}, bf16[2,6,32,256]{3,2,1,0:T(8,128)(2,1)S(1)}, u32[]{:S(2)}, u32[]{:S(2)}) collective-permute-start(bf16[2,6,32,256]{3,2,1,0:T(8,128)(2,1)S(1)} %get-tuple-element.49), channel_id=1, source_target_pairs={{0,3},{1,7},{2,1},{3,5},{4,2},{5,6},{6,0},{7,4},{8,11},{9,15},{10,... | collective-permute-start | bytes 589832 | tf_op jit(solution)/shard_map/ppermute | solution.py:95
  86.1 4.9 %convolution.3 = (bf16[2,6,32,128]{3,2,1,0:T(8,128)(2,1)S(1)}, bf16[2,6,32,128]{3,2,1,0:T(8,128)(2,1)S(1)}, bf16[2,6,32,128]{3,2,1,0:T(8,128)(2,1)S(1)}, bf16[2,6,32,128]{3,2,1,0:T(8,128)(2,1)S(1)}) custom-call(s32[4]{0:T(128)S(1)} %copy-done.2, bf16[1920,1280]{1,0:T(8,128)(2,1)S(1)} %bitcast.6, ...), custom_call_target="tpu_custom_call" | custom-call | flops 1536 | bytes 102400 | tf_op jit(solution)/shard_map/convolution/pallas_call | solution.py:475
  91.7 3.6 %collective-permute-start.21 = (bf16[2,6,32,128]{3,2,1,0:T(8,128)(2,1)S(1)}, bf16[2,6,32,128]{3,2,1,0:T(8,128)(2,1)S(1)}, u32[]{:S(2)}, u32[]{:S(2)}) collective-permute-start(bf16[2,6,32,128]{3,2,1,0:T(8,128)(2,1)S(1)} %get-tuple-element.53), channel_id=1, source_target_pairs={{0,1},{1,5},{2,3},{3,7},{4,0},{5,4},{6,2},{7,6},{8,9},{9,13},{10,1... | collective-permute-start | bytes 294920 | tf_op jit(solution)/shard_map/ppermute | solution.py:95
  95.3 1.5 %collective-permute-start.22 = (bf16[2,6,32,128]{3,2,1,0:T(8,128)(2,1)S(1)}, bf16[2,6,32,128]{3,2,1,0:T(8,128)(2,1)S(1)}, u32[]{:S(2)}, u32[]{:S(2)}) collective-permute-start(bf16[2,6,32,128]{3,2,1,0:T(8,128)(2,1)S(1)} %get-tuple-element.54), channel_id=1, source_target_pairs={{0,2},{1,6},{2,0},{3,4},{4,3},{5,7},{6,1},{7,5},{8,10},{9,14},{10,... | collective-permute-start | bytes 294920 | tf_op jit(solution)/shard_map/ppermute | solution.py:95
  96.8 3.5 %main_result.1 = (bf16[6,2,32,1280]{3,2,1,0:T(8,128)(2,1)}, bf16[6,2,32,384]{3,2,1,0:T(8,128)(2,1)S(1)}) custom-call(s32[4]{0:T(128)S(1)} %copy-done.2, s32[6,2]{1,0:T(8,128)S(1)} %copy.12.sizes, bf16[6,2,32,1280]{3,2,1,0:T(8,128)(2,1)S(1)} %copy-done, f32[6,1,1280]{2,1,0:T(1,128)S(1)} %broadcast_in_dim.12.bias, ...), custom_call_target="tpu_custom_call" | custom-call | flops 61440 | bytes 61440 | tf_op jit(solution)/shard_map/main_result/pallas_call | solution.py:554
  101.1 1.3 %collective-permute-done.23.p3 = bf16[2,6,32,128]{3,2,1,0:T(8,128)(2,1)S(1)} collective-permute-done((bf16[2,6,32,128]{3,2,1,0:T(8,128)(2,1)S(1)}, bf16[2,6,32,128]{3,2,1,0:T(8,128)(2,1)S(1)}, u32[]{:S(2)}, u32[]{:S(2)}) %collective-permute-start.23) | collective-permute-done | bytes 98336 | tf_op jit(solution)/shard_map/ppermute | solution.py:95
  102.4 2.2 %last_result.1 = bf16[6,2,32,1280]{3,2,1,0:T(8,128)(2,1)} custom-call(s32[4]{0:T(128)S(1)} %copy-done.2, s32[6,2]{1,0:T(8,128)S(1)} %copy.12.sizes, f32[6,1,1280]{2,1,0:T(1,128)S(1)} %broadcast_in_dim.12.bias, bf16[6,2,32,384]{3,2,1,0:T(8,128)(2,1)S(1)} %get-tuple-element.50.slab, ...), custom_call_target="tpu_custom_call", output_to_operand_aliasing={{}: (8, {})} | custom-call | flops 491520 | bytes 491520 | tf_op jit(solution)/shard_map/last_result/pallas_call | solution.py:615
  (54 shorter events, 8.3 us)
Async XLA Ops:
  4.4 27.2 %collective-permute-start = (bf16[9,80,1280]{2,1,0:T(8,128)(2,1)}, bf16[9,80,1280]{2,1,0:T(8,128)(2,1)}, u32[]{:S(2)}, u32[]{:S(2)}) collective-permute-start(bf16[9,80,1280]{2,1,0:T(8,128)(2,1)} %own_piece.1.refs_0_), channel_id=1, source_target_pairs={{0,8},{2,10},{4,12},{6,14},{8,16},{9,1},{10,18},{11,3},{12,20},{13... | collective-permute-start | bytes 5529608 | tf_op jit(solution)/shard_map/ppermute | solution.py:95
  10.5 21.0 %collective-permute-start.1 = (bf16[6,2,32,1280]{3,2,1,0:T(8,128)(2,1)S(1)}, bf16[6,2,32,1280]{3,2,1,0:T(8,128)(2,1)S(1)}, u32[]{:S(2)}, u32[]{:S(2)}) collective-permute-start(bf16[6,2,32,1280]{3,2,1,0:T(8,128)(2,1)S(1)} %copy-done), channel_id=1, source_target_pairs={{0,2},{1,4},{2,0},{3,6},{4,1},{5,7},{6,3},{7,5},{8,10},{9,12},{10,... | collective-permute-start | bytes 2949128 | tf_op jit(solution)/shard_map/ppermute | solution.py:95
  12.1 19.5 %collective-permute-start.2 = (bf16[6,2,32,1280]{3,2,1,0:T(8,128)(2,1)S(1)}, bf16[6,2,32,1280]{3,2,1,0:T(8,128)(2,1)S(1)}, u32[]{:S(2)}, u32[]{:S(2)}) collective-permute-start(bf16[6,2,32,1280]{3,2,1,0:T(8,128)(2,1)S(1)} %copy-done), channel_id=1, source_target_pairs={{1,0},{3,2},{4,5},{6,7},{9,8},{11,10},{12,13},{14,15},{17,16},{19,... | collective-permute-start | bytes 2949128 | tf_op jit(solution)/shard_map/ppermute | solution.py:95
  13.8 3.5 %collective-permute-start.7 = (s32[6,2]{1,0:T(8,128)S(1)}, s32[6,2]{1,0:T(8,128)S(1)}, u32[]{:S(2)}, u32[]{:S(2)}) collective-permute-start(s32[6,2]{1,0:T(8,128)S(1)} %copy.12.sizes), channel_id=1, source_target_pairs={{0,0},{1,4},{2,2},{3,6},{4,1},{5,5},{6,3},{7,7},{8,8},{9,12},{10,1... | collective-permute-start | bytes 152 | tf_op jit(solution)/shard_map/ppermute | solution.py:95
  16.6 9.0 %collective-permute-start.3 = (f32[2,8,128]{2,1,0:T(8,128)S(1)}, f32[2,8,128]{2,1,0:T(8,128)S(1)}, u32[]{:S(2)}, u32[]{:S(2)}) collective-permute-start(f32[2,8,128]{2,1,0:T(8,128)S(1)} %local_stats.1), channel_id=1, source_target_pairs={{0,0},{1,4},{2,2},{3,6},{4,1},{5,5},{6,3},{7,7},{8,8},{9,12},{10,1... | collective-permute-start | bytes 24584 | tf_op jit(solution)/shard_map/ppermute | solution.py:95
  17.3 9.8 %collective-permute-start.4 = (f32[2,8,128]{2,1,0:T(8,128)S(1)}, f32[2,8,128]{2,1,0:T(8,128)S(1)}, u32[]{:S(2)}, u32[]{:S(2)}) collective-permute-start(f32[2,8,128]{2,1,0:T(8,128)S(1)} %local_stats.1), channel_id=1, source_target_pairs={{0,4},{1,0},{2,6},{3,2},{4,5},{5,1},{6,7},{7,3},{8,12},{9,8},{10,1... | collective-permute-start | bytes 24584 | tf_op jit(solution)/shard_map/ppermute | solution.py:95
  25.6 4.6 %collective-permute-start.5 = (f32[2,8,128]{2,1,0:T(8,128)S(1)}, f32[2,8,128]{2,1,0:T(8,128)S(1)}, u32[]{:S(2)}, u32[]{:S(2)}) collective-permute-start(f32[2,8,128]{2,1,0:T(8,128)S(1)} %local_stats.1), channel_id=1, source_target_pairs={{0,2},{1,6},{2,0},{3,4},{4,3},{5,7},{6,1},{7,5},{8,10},{9,14},{10,... | collective-permute-start | bytes 24584 | tf_op jit(solution)/shard_map/ppermute | solution.py:95
  27.1 4.4 %collective-permute-start.6 = (f32[2,8,128]{2,1,0:T(8,128)S(1)}, f32[2,8,128]{2,1,0:T(8,128)S(1)}, u32[]{:S(2)}, u32[]{:S(2)}) collective-permute-start(f32[2,8,128]{2,1,0:T(8,128)S(1)} %local_stats.1), channel_id=1, source_target_pairs={{0,6},{1,2},{2,4},{3,0},{4,7},{5,3},{6,5},{7,1},{8,14},{9,10},{10,... | collective-permute-start | bytes 24584 | tf_op jit(solution)/shard_map/ppermute | solution.py:95
  31.6 25.2 %collective-permute-start.8 = (bf16[9,80,1280]{2,1,0:T(8,128)(2,1)}, bf16[9,80,1280]{2,1,0:T(8,128)(2,1)S(1)}, u32[]{:S(2)}, u32[]{:S(2)}) collective-permute-start(bf16[9,80,1280]{2,1,0:T(8,128)(2,1)} %collective-permute-done.refs_1_), channel_id=1, source_target_pairs={{8,16},{9,1},{10,18},{11,3},{12,20},{13,5},{14,22},{15,7},{16,24},... | collective-permute-start | bytes 5529608 | tf_op jit(solution)/shard_map/ppermute | solution.py:95
  32.4 13.9 %collective-permute-start.11 = (bf16[6,2,32,1280]{3,2,1,0:T(8,128)(2,1)S(1)}, bf16[6,2,32,1280]{3,2,1,0:T(8,128)(2,1)S(1)}, u32[]{:S(2)}, u32[]{:S(2)}) collective-permute-start(bf16[6,2,32,1280]{3,2,1,0:T(8,128)(2,1)S(1)} %copy-done), channel_id=1, source_target_pairs={{0,4},{1,2},{2,6},{3,0},{4,7},{5,1},{6,5},{7,3},{8,12},{9,10},{10,... | collective-permute-start | bytes 2949128 | tf_op jit(solution)/shard_map/ppermute | solution.py:95
  34.7 22.1 %collective-permute-start.10 = (bf16[6,2,32,1280]{3,2,1,0:T(8,128)(2,1)S(1)}, bf16[6,2,32,1280]{3,2,1,0:T(8,128)(2,1)S(1)}, u32[]{:S(2)}, u32[]{:S(2)}) collective-permute-start(bf16[6,2,32,1280]{3,2,1,0:T(8,128)(2,1)S(1)} %collective-permute-done.1.refs_1_.refs_0_), channel_id=1, source_target_pairs={{0,4},{2,6},{5,1},{7,3},{8,12},{10,14},{13,9},{15,11},{16,20},{18,... | collective-permute-start | bytes 2949128 | tf_op jit(solution)/shard_map/ppermute | solution.py:95
  36.6 20.2 %collective-permute-start.9 = (bf16[6,2,32,1280]{3,2,1,0:T(8,128)(2,1)S(1)}, bf16[6,2,32,1280]{3,2,1,0:T(8,128)(2,1)S(1)}, u32[]{:S(2)}, u32[]{:S(2)}) collective-permute-start(bf16[6,2,32,1280]{3,2,1,0:T(8,128)(2,1)S(1)} %collective-permute-done.1.refs_1_.refs_0_), channel_id=1, source_target_pairs={{1,3},{3,1},{4,6},{6,4},{9,11},{11,9},{12,14},{14,12},{17,19},{19,... | collective-permute-start | bytes 2949128 | tf_op jit(solution)/shard_map/ppermute | solution.py:95
  37.4 23.3 %collective-permute-start.13 = (bf16[9,80,1280]{2,1,0:T(8,128)(2,1)}, bf16[9,80,1280]{2,1,0:T(8,128)(2,1)S(1)}, u32[]{:S(2)}, u32[]{:S(2)}) collective-permute-start(bf16[9,80,1280]{2,1,0:T(8,128)(2,1)} %collective-permute-done.refs_1_), channel_id=1, source_target_pairs={{0,1},{1,0},{2,3},{3,2},{4,5},{5,4},{6,7},{7,6},{8,9},{9,8},{10,11... | collective-permute-start | bytes 5529608 | tf_op jit(solution)/shard_map/ppermute | solution.py:95
  56.8 3.9 %collective-permute-start.14 = (bf16[9,80,1280]{2,1,0:T(8,128)(2,1)S(1)}, bf16[9,80,1280]{2,1,0:T(8,128)(2,1)S(1)}, u32[]{:S(2)}, u32[]{:S(2)}) collective-permute-start(bf16[9,80,1280]{2,1,0:T(8,128)(2,1)S(1)} %collective-permute-done.8.refs_3_.refs_0_), channel_id=1, source_target_pairs={{0,1},{1,0},{2,3},{3,2},{4,5},{5,4},{6,7},{7,6},{8,9},{9,8},{10,11... | collective-permute-start | bytes 5529608 | tf_op jit(solution)/shard_map/ppermute | solution.py:95
  56.8 15.2 %collective-permute-start.12 = (bf16[9,80,1280]{2,1,0:T(8,128)(2,1)S(1)}, bf16[9,80,1280]{2,1,0:T(8,128)(2,1)S(1)}, u32[]{:S(2)}, u32[]{:S(2)}) collective-permute-start(bf16[9,80,1280]{2,1,0:T(8,128)(2,1)S(1)} %collective-permute-done.8.refs_3_.refs_0_), channel_id=1, source_target_pairs={{9,1},{11,3},{13,5},{15,7},{16,24},{18,26},{20,28},{22,30}} | collective-permute-start | bytes 5529608 | tf_op jit(solution)/shard_map/ppermute | solution.py:95
  71.3 0.7 collective-permute-start.15
  72.0 14.0 %collective-permute-start.19 = (bf16[9,80,1280]{2,1,0:T(8,128)(2,1)S(1)}, bf16[9,80,1280]{2,1,0:T(8,128)(2,1)S(1)}, u32[]{:S(2)}, u32[]{:S(2)}) collective-permute-start(bf16[9,80,1280]{2,1,0:T(8,128)(2,1)S(1)} %collective-permute-done.12.refs_2_), channel_id=1, source_target_pairs={{0,1},{1,0},{2,3},{3,2},{4,5},{5,4},{6,7},{7,6},{8,9},{9,8},{10,11... | collective-permute-start | bytes 5529608 | tf_op jit(solution)/shard_map/ppermute | solution.py:95
  82.4 12.9 %collective-permute-start.16 = (bf16[2,6,32,256]{3,2,1,0:T(8,128)(2,1)S(1)}, bf16[2,6,32,256]{3,2,1,0:T(8,128)(2,1)S(1)}, u32[]{:S(2)}, u32[]{:S(2)}) collective-permute-start(bf16[2,6,32,256]{3,2,1,0:T(8,128)(2,1)S(1)} %get-tuple-element.47), channel_id=1, source_target_pairs={{0,1},{1,5},{2,3},{3,7},{4,0},{5,4},{6,2},{7,6},{8,9},{9,13},{10,1... | collective-permute-start | bytes 589832 | tf_op jit(solution)/shard_map/ppermute | solution.py:95
  82.4 14.4 %collective-permute-start.17 = (bf16[2,6,32,256]{3,2,1,0:T(8,128)(2,1)S(1)}, bf16[2,6,32,256]{3,2,1,0:T(8,128)(2,1)S(1)}, u32[]{:S(2)}, u32[]{:S(2)}) collective-permute-start(bf16[2,6,32,256]{3,2,1,0:T(8,128)(2,1)S(1)} %get-tuple-element.48), channel_id=1, source_target_pairs={{0,2},{1,6},{2,0},{3,4},{4,3},{5,7},{6,1},{7,5},{8,10},{9,14},{10,... | collective-permute-start | bytes 589832 | tf_op jit(solution)/shard_map/ppermute | solution.py:95
  84.0 12.9 %collective-permute-start.18 = (bf16[2,6,32,256]{3,2,1,0:T(8,128)(2,1)S(1)}, bf16[2,6,32,256]{3,2,1,0:T(8,128)(2,1)S(1)}, u32[]{:S(2)}, u32[]{:S(2)}) collective-permute-start(bf16[2,6,32,256]{3,2,1,0:T(8,128)(2,1)S(1)} %get-tuple-element.49), channel_id=1, source_target_pairs={{0,3},{1,7},{2,1},{3,5},{4,2},{5,6},{6,0},{7,4},{8,11},{9,15},{10,... | collective-permute-start | bytes 589832 | tf_op jit(solution)/shard_map/ppermute | solution.py:95
  91.0 9.4 %collective-permute-start.20 = (bf16[2,6,32,128]{3,2,1,0:T(8,128)(2,1)S(1)}, bf16[2,6,32,128]{3,2,1,0:T(8,128)(2,1)S(1)}, u32[]{:S(2)}, u32[]{:S(2)}) collective-permute-start(bf16[2,6,32,128]{3,2,1,0:T(8,128)(2,1)S(1)} %get-tuple-element.52), channel_id=1, source_target_pairs={{0,0},{1,4},{2,2},{3,6},{4,1},{5,5},{6,3},{7,7},{8,8},{9,12},{10,1... | collective-permute-start | bytes 294920 | tf_op jit(solution)/shard_map/ppermute | solution.py:95
  91.7 8.7 %collective-permute-start.21 = (bf16[2,6,32,128]{3,2,1,0:T(8,128)(2,1)S(1)}, bf16[2,6,32,128]{3,2,1,0:T(8,128)(2,1)S(1)}, u32[]{:S(2)}, u32[]{:S(2)}) collective-permute-start(bf16[2,6,32,128]{3,2,1,0:T(8,128)(2,1)S(1)} %get-tuple-element.53), channel_id=1, source_target_pairs={{0,1},{1,5},{2,3},{3,7},{4,0},{5,4},{6,2},{7,6},{8,9},{9,13},{10,1... | collective-permute-start | bytes 294920 | tf_op jit(solution)/shard_map/ppermute | solution.py:95
  95.3 5.8 %collective-permute-start.22 = (bf16[2,6,32,128]{3,2,1,0:T(8,128)(2,1)S(1)}, bf16[2,6,32,128]{3,2,1,0:T(8,128)(2,1)S(1)}, u32[]{:S(2)}, u32[]{:S(2)}) collective-permute-start(bf16[2,6,32,128]{3,2,1,0:T(8,128)(2,1)S(1)} %get-tuple-element.54), channel_id=1, source_target_pairs={{0,2},{1,6},{2,0},{3,4},{4,3},{5,7},{6,1},{7,5},{8,10},{9,14},{10,... | collective-permute-start | bytes 294920 | tf_op jit(solution)/shard_map/ppermute | solution.py:95
  96.8 5.6 %collective-permute-start.23 = (bf16[2,6,32,128]{3,2,1,0:T(8,128)(2,1)S(1)}, bf16[2,6,32,128]{3,2,1,0:T(8,128)(2,1)S(1)}, u32[]{:S(2)}, u32[]{:S(2)}) collective-permute-start(bf16[2,6,32,128]{3,2,1,0:T(8,128)(2,1)S(1)} %get-tuple-element.55), channel_id=1, source_target_pairs={{0,3},{1,7},{2,1},{3,5},{4,2},{5,6},{6,0},{7,4},{8,11},{9,15},{10,... | collective-permute-start | bytes 294920 | tf_op jit(solution)/shard_map/ppermute | solution.py:95
  (7 other events, 118.4 us)

commit v6 on v5

--- a/solution.py
+++ b/solution.py
@@ -112,25 +112,26 @@
     return copies
 
 
-def piece_kernel(part, where, weight, out, sems):
-    rows = pl.ds(pl.multiple_of(where[2] * part, part), part)
+def piece_kernel(part, weight, out, sems):
+    y = lax.axis_index("space") // 2
+    rows = pl.ds(pl.multiple_of(y * part, part), part)
     pairs = [(weight.at[tap, rows, :], out.at[tap]) for tap in range(out.shape[0])]
     for copy in start_all(pairs, sems):
         copy.wait()
 
 
-def own_piece(where, weight, part):
+def own_piece(weight, part):
     taps, _, chans = weight.shape
     return pl.pallas_call(
         functools.partial(piece_kernel, part),
         out_shape=jax.ShapeDtypeStruct((taps, part, chans), weight.dtype),
-        in_specs=[SMEM, ANY],
+        in_specs=[ANY],
         out_specs=VMEM,
         scratch_shapes=[pltpu.SemaphoreType.DMA((taps,))],
         compiler_params=params(56),
         cost_estimate=pl.CostEstimate(flops=0, transcendentals=0, bytes_accessed=4 << 20),
         name="own_piece",
-    )(where, weight)
+    )(weight)
 
 
 def choose(index, sources, target, sem, wait):
@@ -165,68 +166,97 @@
     return (held * sizes[f, 1]).astype(jnp.float32)
 
 
-def stats_kernel(where, sizes, latents, group, group_t, out, sums, scale):
-    frames, rows, cols, chans = latents.shape
+def block_rows(where, rows, k):
+    return rows * (2 * (where[2] ^ (k // 2)) + (where[1] ^ (k % 2)))
+
+
+def fetch(where, choices, blocks, sems):
+    away = jnp.where(where[3] == where[1], 0, 1)
+    for wait in (False, True):
+        for n, pair in enumerate(choices):
+            choose(away, pair, blocks.at[n], sems.at[n], wait)
+
+
+def cells_in(where, sizes, rounds, frames, rows, members, rest):
+    return per_frame(
+        [
+            sum(cells_of(sizes, f, block_rows(where, rows, k), rows) for k in rounds) * members
+            for f in range(frames)
+        ],
+        rest,
+    )
+
+
+def reduce_blocks(where, sizes, blocks, rounds, group, group_t, sums, scale):
+    frames, rows, cols, chans = blocks.shape[1:]
     members = chans // GROUPS
-    first_row = rows * (2 * where[2] + where[3])
     col_ids = lax.broadcasted_iota(jnp.int32, (cols, LANES), 0)
+    first_rows = [block_rows(where, rows, k) for k in rounds]
 
     def add(f, centred):
-        masks = [
-            col_ids < jnp.where(first_row + r < sizes[f, 0], sizes[f, 1], 0) for r in range(rows)
-        ]
+        places = [(k, r, first + r) for k, first in zip(rounds, first_rows) for r in range(rows)]
+        masks = [col_ids < jnp.where(row < sizes[f, 0], sizes[f, 1], 0) for _, _, row in places]
         for tile in range(chans // LANES):
             lanes = slice(tile * LANES, (tile + 1) * LANES)
             total = jnp.zeros((8, LANES), jnp.float32)
-            for r in range(rows):
-                v = latents[f, r, :, lanes].astype(jnp.float32)
+            for (k, r, _), mask in zip(places, masks):
+                v = blocks[k, f, r, :, lanes].astype(jnp.float32)
                 if centred:
                     v = v - scale[f, :, lanes]
                     v = v * v
-                v = jnp.where(masks[r], v, 0.0)
+                v = jnp.where(mask, v, 0.0)
                 total += jnp.sum(v.reshape(cols // 8, 8, LANES), axis=0)
             sums[f, :, lanes] = total
         return 0
 
     sums[...] = jnp.zeros_like(sums)
     lax.fori_loop(0, frames, lambda f, _: add(f, False), 0)
-    counts = [cells_of(sizes, f, first_row, rows) * members for f in range(frames)]
-    count = jnp.maximum(per_frame(counts, 1.0), 1.0)
+    count = jnp.maximum(cells_in(where, sizes, rounds, frames, rows, members, 1.0), 1.0)
     mean = exact_dot(jnp.sum(sums[...], axis=1), group[...]) / count
+    wide = exact_dot(mean, group_t[...])
+    for f in range(frames):
+        scale[f] = wide[f : f + 1]
+    lax.fori_loop(0, frames, lambda f, _: add(f, True), 0)
+    return mean, exact_dot(jnp.sum(sums[...], axis=1), group[...])
+
+
+def stats_kernel(where, sizes, group, group_t, own, first, sibling, second, *refs):
+    out, blocks, sums, scale, sems = refs
+    fetch(where, [(own, first), (sibling, second)], blocks, sems)
+    mean, squares = reduce_blocks(where, sizes, blocks, (0, 1), group, group_t, sums, scale)
     out[0] = mean
-    spread_mean = exact_dot(mean, group_t[...])
+    out[1] = squares
+
+
+def act_kernel(where, sizes, gain, shift, group, group_t, stats, *refs):
+    own, first, sibling, second, relay0, relay1, act, blocks, sums, scale, sems = refs
+    frames, rows, cols, chans = blocks.shape[1:]
+    members = chans // GROUPS
+    fetch(
+        where,
+        [(own, first), (sibling, second), (first, relay0), (second, relay1)],
+        blocks,
+        sems,
+    )
+    mean1, squares1 = reduce_blocks(where, sizes, blocks, (2, 3), group, group_t, sums, scale)
+    mean0, squares0 = stats[0], stats[1]
+    count0 = cells_in(where, sizes, (0, 1), frames, rows, members, 0.0)
+    count1 = cells_in(where, sizes, (2, 3), frames, rows, members, 0.0)
+    whole = jnp.maximum(count0 + count1, 1.0)
+    mean = (count0 * mean0 + count1 * mean1) / whole
+    squares = squares0 + squares1
+    squares += count0 * (mean0 - mean) * (mean0 - mean)
+    squares += count1 * (mean1 - mean) * (mean1 - mean)
+    factor = exact_dot(1.0 / jnp.sqrt(squares / whole + EPS), group_t[...]) * gain[...]
+    middle = exact_dot(mean, group_t[...])
     for f in range(frames):
-        scale[f] = spread_mean[f : f + 1]
-    lax.fori_loop(0, frames, lambda f, _: add(f, True), 0)
-    out[1] = exact_dot(jnp.sum(sums[...], axis=1), group[...])
-
-
-def local_stats(where, sizes, latents, group):
-    chans = latents.shape[3]
-    return pl.pallas_call(
-        stats_kernel,
-        out_shape=jax.ShapeDtypeStruct((2, 8, LANES), jnp.float32),
-        in_specs=[SMEM, SMEM] + [VMEM] * 3,
-        out_specs=VMEM,
-        scratch_shapes=[
-            pltpu.VMEM((8, 8, chans), jnp.float32),
-            pltpu.VMEM((8, 1, chans), jnp.float32),
-        ],
-        compiler_params=params(4),
-        cost_estimate=pl.CostEstimate(
-            flops=latents.size // 8, transcendentals=0, bytes_accessed=latents.size // 8
-        ),
-        name="local_stats",
-    )(where, sizes, latents, *group)
-
-
-def block_rows(where, rows, k):
-    return rows * (2 * (where[2] ^ (k // 2)) + (where[1] ^ (k % 2)))
-
-
-def activate(where, sizes, shift, scale, blocks, act, first_round):
-    frames, rows, cols, chans = blocks.shape[1:]
+        scale[f] = middle[f : f + 1]
+        scale[8 + f] = factor[f : f + 1]
+    edge = jnp.zeros((frames, cols, chans), jnp.bfloat16)
+    act[0] = edge
+    act[act.shape[0] - 1] = edge
     col_ids = lax.broadcasted_iota(jnp.int32, (cols, LANES), 0)
+    first_rows = [block_rows(where, rows, k) for k in range(4)]
 
     def body(f, _):
         for tile in range(chans // LANES):
@@ -234,73 +264,29 @@
             middle = scale[f, :, lanes]
             factor = scale[8 + f, :, lanes]
             offset = shift[:, lanes]
-            for n in range(2):
-                first = block_rows(where, rows, first_round + n)
+            for k in range(4):
                 for r in range(rows):
-                    limit = jnp.where(first + r < sizes[f, 0], sizes[f, 1], 0)
-                    v = blocks[n, f, r, :, lanes].astype(jnp.float32)
+                    row = first_rows[k] + r
+                    limit = jnp.where(row < sizes[f, 0], sizes[f, 1], 0)
+                    v = blocks[k, f, r, :, lanes].astype(jnp.float32)
                     v = 0.5 * ((v - middle) * factor + offset)
                     v = v + v * jnp.tanh(v)
                     v = jnp.where(col_ids < limit, v, 0.0)
-                    act[first + r + 1, f, :, lanes] = v.astype(jnp.bfloat16)
+                    act[row + 1, f, :, lanes] = v.astype(jnp.bfloat16)
         return 0
 
     lax.fori_loop(0, frames, body, 0)
 
 
-def fetch(where, choices, blocks, sems):
-    away = jnp.where(where[3] == where[1], 0, 1)
-    for wait in (False, True):
-        for n, pair in enumerate(choices):
-            choose(away, pair, blocks.at[n], sems.at[n], wait)
-
-
-def first_act_kernel(where, sizes, gain, shift, group, group_t, s0, s1, s2, s3, *refs):
-    own, first, sibling, second, act, scale, blocks, sems = refs
-    frames, rows, cols, chans = blocks.shape[1:]
-    members = chans // GROUPS
-    fetch(where, [(own, first), (sibling, second)], blocks, sems)
-    whole = per_frame(
-        [(sizes[f, 0] * sizes[f, 1] * members).astype(jnp.float32) for f in range(frames)], 1.0
-    )
-    counts = [
-        per_frame(
-            [
-                cells_of(sizes, f, block_rows(where, rows, k), rows) * members
-                for f in range(frames)
-            ],
-            0.0,
-        )
-        for k in range(4)
-    ]
-    stats = (s0, s1, s2, s3)
-    mean = sum(count * stat[0] for count, stat in zip(counts, stats)) / whole
-    squares = sum(
-        stat[1] + count * (stat[0] - mean) * (stat[0] - mean)
-        for count, stat in zip(counts, stats)
-    )
-    factor = exact_dot(1.0 / jnp.sqrt(squares / whole + EPS), group_t[...]) * gain[...]
-    middle = exact_dot(mean, group_t[...])
-    del group
-    for f in range(frames):
-        scale[f] = middle[f : f + 1]
-        scale[8 + f] = factor[f : f + 1]
-    edge = jnp.zeros((frames, cols, chans), jnp.bfloat16)
-    act[0] = edge
-    act[act.shape[0] - 1] = edge
-    activate(where, sizes, shift, scale, blocks, act, 0)
-
-
-def second_act_kernel(where, sizes, shift, scale, given, *refs):
-    first, relay0, second, relay1, act, blocks, sems = refs
-    del given
-    fetch(where, [(first, relay0), (second, relay1)], blocks, sems)
-    activate(where, sizes, shift, scale, blocks, act, 2)
-
-
-def act_params(frames, rows, cols, chans):
-    elements = 2 * frames * rows * cols * chans
+def act_params(count, frames, rows, cols, chans):
+    elements = frames * rows * cols * chans
     return dict(
+        scratch_shapes=[
+            pltpu.VMEM((count, frames, rows, cols, chans), jnp.bfloat16),
+            pltpu.VMEM((8, 8, chans), jnp.float32),
+            pltpu.VMEM((16, 1, chans), jnp.float32),
+            pltpu.SemaphoreType.DMA((count,)),
+        ],
         compiler_params=params(16),
         cost_estimate=pl.CostEstimate(
             flops=elements // 8, transcendentals=0, bytes_accessed=elements // 8
@@ -308,40 +294,27 @@
     )
 
 
-def first_activation(where, sizes, gain, shift, group, stats, blocks):
+def early_stats(where, sizes, group, blocks):
+    return pl.pallas_call(
+        stats_kernel,
+        out_shape=jax.ShapeDtypeStruct((2, 8, LANES), jnp.float32),
+        in_specs=[SMEM, SMEM] + [VMEM] * 2 + [ANY] * 4,
+        out_specs=VMEM,
+        name="early_stats",
+        **act_params(2, *blocks[0].shape),
+    )(where, sizes, *group, *blocks)
+
+
+def activation(where, sizes, gain, shift, group, stats, blocks):
     frames, rows, cols, chans = blocks[0].shape
     return pl.pallas_call(
-        first_act_kernel,
-        out_shape=[
-            jax.ShapeDtypeStruct((4 * rows + 2, frames, cols, chans), jnp.bfloat16),
-            jax.ShapeDtypeStruct((16, 1, chans), jnp.float32),
-        ],
-        in_specs=[SMEM, SMEM] + [VMEM] * 8 + [ANY] * 4,
-        out_specs=[VMEM] * 2,
-        scratch_shapes=[
-            pltpu.VMEM((2, frames, rows, cols, chans), jnp.bfloat16),
-            pltpu.SemaphoreType.DMA((2,)),
-        ],
-        name="first_activation",
-        **act_params(frames, rows, cols, chans),
-    )(where, sizes, gain[None, :], shift[None, :], *group, *stats, *blocks)
-
-
-def second_activation(where, sizes, shift, scale, act, blocks):
-    frames, rows, cols, chans = blocks[0].shape
-    return pl.pallas_call(
-        second_act_kernel,
-        out_shape=jax.ShapeDtypeStruct(act.shape, act.dtype),
-        in_specs=[SMEM, SMEM] + [VMEM] * 3 + [ANY] * 4,
+        act_kernel,
+        out_shape=jax.ShapeDtypeStruct((4 * rows + 2, frames, cols, chans), jnp.bfloat16),
+        in_specs=[SMEM, SMEM] + [VMEM] * 5 + [ANY] * 6,
         out_specs=VMEM,
-        scratch_shapes=[
-            pltpu.VMEM((2, frames, rows, cols, chans), jnp.bfloat16),
-            pltpu.SemaphoreType.DMA((2,)),
-        ],
-        input_output_aliases={4: 0},
-        name="second_activation",
-        **act_params(frames, rows, cols, chans),
-    )(where, sizes, shift[None, :], scale, act, *blocks)
+        name="activation",
+        **act_params(4, frames, rows, cols, chans),
+    )(where, sizes, gain[None, :], shift[None, :], *group, stats, *blocks)
 
 
 def group_matrix(chans):
@@ -658,7 +631,7 @@
     group = group_matrix(chans)
     group = (group, group.T)
 
-    piece = own_piece(where, conv_weight, part)
+    piece = own_piece(conv_weight, part)
     hop1 = hop(piece, 1)
     first = grid.permute(
         latents, lambda z, x, y, c: (z, x, 1 - y, c) if c == x else (z, 1 - x, y, 1 - c)
@@ -667,35 +640,28 @@
         latents, lambda z, x, y, c: (z, 1 - x, y, c) if c == x else (z, x, 1 - y, 1 - c)
     )
     sibling = grid.permute(latents, lambda z, x, y, c: (z, x, y, 1 - c) if c != x else None)
-    stats = local_stats(where, buckets, latents, group)
-    stats = [
-        grid.permute(stats, lambda z, x, y, c, k=k: (z, c ^ (k % 2), y ^ (k // 2), x))
-        for k in range(4)
-    ]
     sizes = grid.permute(buckets, lambda z, x, y, c: (z, c, y, x))
-    hop1, first, sibling, stats, sizes = lax.optimization_barrier(
-        (hop1, first, sibling, stats, sizes)
-    )
 
     hop2 = hop(hop1, 2)
-    swap1 = swap(hop1)
+    first, second, sibling, sizes = lax.optimization_barrier((first, second, sibling, sizes))
     relay0 = grid.permute(first, lambda z, x, y, c: (z, x, 1 - y, c) if c != x else None)
     relay1 = grid.permute(first, lambda z, x, y, c: (z, 1 - x, y, c) if c == x else None)
-    act, scale = first_activation(
-        where, sizes, gn_gain, gn_shift, group, stats, [latents, first, sibling, second]
-    )
-    hop2, relay0, relay1, act = lax.optimization_barrier((hop2, relay0, relay1, act))
+    blocks = [latents, first, sibling, second]
+    stats = early_stats(where, sizes, group, blocks)
+    swap1 = swap(hop1)
+    hop2, relay0, relay1, stats, swap1 = lax.optimization_barrier(
+        (hop2, relay0, relay1, stats, swap1)
+    )
 
     hop3 = hop(hop2, 3)
     swap2 = swap(hop2)
-    act = second_activation(
-        where, sizes, gn_shift, scale, act, [first, relay0, second, relay1]
-    )
+    blocks += [relay0, relay1]
+    act = activation(where, sizes, gn_gain, gn_shift, group, stats, blocks)
     near = [hop1, swap1, hop2, swap2]
     main = convolution(main_kernel, where, act, [piece] + near, part, rows, 3)
 
+    hop3, main = lax.optimization_barrier((hop3, main))
     main = spread(main)
-    hop3, main[0] = lax.optimization_barrier((hop3, main[0]))
     swap3 = swap(hop3)
     last = convolution(last_kernel, where, act, [hop2, swap2, hop3, swap3], part, rows, 1)
     bias = time_bias[:, None, :]

time: 105 us -> 103 us (0.981)
  starting transfers between devices: 50.4 us -> 35.4 us
  waiting for transfers between devices: 19 us -> 27 us
  Pallas kernels: 33.7 us -> 38.3 us
    ppermute x24 -> x20, starting transfers between devices: 50.4 us -> 35.4 us  [permute(): return lax.ppermute(value, ('dp', 'space'), pairs)]
    ppermute x24 -> x20, waiting for transfers between devices: 19 us -> 27 us  [permute(): return lax.ppermute(value, ('dp', 'space'), pairs)]
    pallas_call x3 -> x2, Pallas kernels: 8.76 us -> 12.9 us  [the longest x1 8.67 us: activation(): pl.pallas_call(act_kernel, out_shape=jax.ShapeDtypeStruct((4 * rows + 2,...]
    pallas_call x2, Pallas kernels: 15.5 us -> 16.7 us  [convolution(): pl.pallas_call(functools.partial(kernel, rows, cols, part), out_shape=[ou...]
  transfers between devices with their start and end apart: 24 -> 20, of which waited for: 5 -> 6; matrix products, arithmetic and copies ran while one was open for 0% -> 1% of each run, Pallas kernels for 27% -> 33%
where the time goes in v6:
time: 103 us; the launch traced here: 102 us
  Pallas kernels  38.3 us (37%)
  starting transfers between devices  35.4 us (34%)
  waiting for transfers between devices  27 us (26%)
    ppermute x20, starting transfers between devices, permute(): return lax.ppermute(value, ('dp', 'space'), pairs)  35.4 us
    ppermute x20, waiting for transfers between devices, permute(): return lax.ppermute(value, ('dp', 'space'), pairs)  27 us
    pallas_call x2, Pallas kernels, convolution(): pl.pallas_call(functools.partial(kernel, rows, cols, part), out_shape=[ou...  16.7 us
    pallas_call x1, Pallas kernels, activation(): pl.pallas_call(act_kernel, out_shape=jax.ShapeDtypeStruct((4 * rows + 2,...  8.67 us
    pallas_call x1, Pallas kernels, early_stats(): pl.pallas_call(stats_kernel, out_shape=jax.ShapeDtypeStruct((2, 8, LANES)...  4.24 us
    pallas_call x1, Pallas kernels, main_result(): pl.pallas_call(main_result_kernel, out_shape=[jax.ShapeDtypeStruct(latent...  3.52 us
    pallas_call x1, Pallas kernels, own_piece(): pl.pallas_call(functools.partial(piece_kernel, part), out_shape=jax.Shape...  2.95 us
    pallas_call x1, Pallas kernels, last_result(): pl.pallas_call(last_result_kernel, out_shape=jax.ShapeDtypeStruct(given.s...  2.23 us
  transfers between devices with their start and end apart: 20, of which 6 were waited for; matrix products, arithmetic and copies ran while one was open for 1% of the time, Pallas kernels for 33%

profile of v6, /device:TPU:0, one launch (start us, length us, event | category | flops | bytes accessed | tf_op | source)
XLA Modules:
  0.0 101.6 jit_solution(4939652971221866867)
XLA Ops:
  0.0 2.9 %own_piece.1.refs_0_ = bf16[9,80,1280]{2,1,0:T(8,128)(2,1)} custom-call(bf16[9,160,1280]{2,1,0:T(8,128)(2,1)} %weight.1), custom_call_target="tpu_custom_call" | custom-call | bytes 4194304 | tf_op jit(solution)/shard_map/own_piece/pallas_call | solution.py:125
  3.0 6.2 %collective-permute-start = (bf16[9,80,1280]{2,1,0:T(8,128)(2,1)}, bf16[9,80,1280]{2,1,0:T(8,128)(2,1)}, u32[]{:S(2)}, u32[]{:S(2)}) collective-permute-start(bf16[9,80,1280]{2,1,0:T(8,128)(2,1)} %own_piece.1.refs_0_), channel_id=1, source_target_pairs={{0,8},{2,10},{4,12},{6,14},{8,16},{9,1},{10,18},{11,3},{12,20},{13... | collective-permute-start | bytes 5529608 | tf_op jit(solution)/shard_map/ppermute | solution.py:95
  9.1 1.5 %collective-permute-start.2 = (bf16[6,2,32,1280]{3,2,1,0:T(8,128)(2,1)S(1)}, bf16[6,2,32,1280]{3,2,1,0:T(8,128)(2,1)}, u32[]{:S(2)}, u32[]{:S(2)}) collective-permute-start(bf16[6,2,32,1280]{3,2,1,0:T(8,128)(2,1)S(1)} %copy-done), channel_id=1, source_target_pairs={{0,2},{1,4},{2,0},{3,6},{4,1},{5,7},{6,3},{7,5},{8,10},{9,12},{10,... | collective-permute-start | bytes 2949128 | tf_op jit(solution)/shard_map/ppermute | solution.py:95
  10.6 1.3 %collective-permute-start.4 = (bf16[6,2,32,1280]{3,2,1,0:T(8,128)(2,1)S(1)}, bf16[6,2,32,1280]{3,2,1,0:T(8,128)(2,1)}, u32[]{:S(2)}, u32[]{:S(2)}) collective-permute-start(bf16[6,2,32,1280]{3,2,1,0:T(8,128)(2,1)S(1)} %copy-done), channel_id=1, source_target_pairs={{1,0},{3,2},{4,5},{6,7},{9,8},{11,10},{12,13},{14,15},{17,16},{19,... | collective-permute-start | bytes 2949128 | tf_op jit(solution)/shard_map/ppermute | solution.py:95
  12.7 16.3 %collective-permute-done.refs_1_ = bf16[9,80,1280]{2,1,0:T(8,128)(2,1)} collective-permute-done((bf16[9,80,1280]{2,1,0:T(8,128)(2,1)}, bf16[9,80,1280]{2,1,0:T(8,128)(2,1)}, u32[]{:S(2)}, u32[]{:S(2)}) %collective-permute-start) | collective-permute-done | bytes 1843232 | tf_op jit(solution)/shard_map/ppermute | solution.py:95
  29.0 0.8 collective-permute-start.1
  29.8 2.5 %collective-permute-start.8 = (bf16[9,80,1280]{2,1,0:T(8,128)(2,1)}, bf16[9,80,1280]{2,1,0:T(8,128)(2,1)}, u32[]{:S(2)}, u32[]{:S(2)}) collective-permute-start(bf16[9,80,1280]{2,1,0:T(8,128)(2,1)} %collective-permute-done.refs_1_), channel_id=1, source_target_pairs={{0,1},{1,0},{2,3},{3,2},{4,5},{5,4},{6,7},{7,6},{8,9},{9,8},{10,11... | collective-permute-start | bytes 5529608 | tf_op jit(solution)/shard_map/ppermute | solution.py:95
  32.9 0.9 collective-permute-done.3.second.refs_3_
  34.6 5.6 %collective-permute-start.7 = (bf16[6,2,32,1280]{3,2,1,0:T(8,128)(2,1)}, bf16[6,2,32,1280]{3,2,1,0:T(8,128)(2,1)S(1)}, u32[]{:S(2)}, u32[]{:S(2)}) collective-permute-start(bf16[6,2,32,1280]{3,2,1,0:T(8,128)(2,1)} %collective-permute-done.2.first.refs_1_), channel_id=1, source_target_pairs={{0,4},{2,6},{5,1},{7,3},{8,12},{10,14},{13,9},{15,11},{16,20},{18,... | collective-permute-start | bytes 2949128 | tf_op jit(solution)/shard_map/ppermute | solution.py:95
  40.6 4.2 %early_stats.1.stats = f32[2,8,128]{2,1,0:T(8,128)S(1)} custom-call(s32[4]{0:T(128)S(1)} %pad_add_fusion.where, s32[6,2]{1,0:T(8,128)S(1)} %collective-permute-done.5.sizes, bf16[1280,128]{1,0:T(8,128)(2,1)S(1)} %fusion.group, bf16[128,1280]{1,0:T(8,128)(2,1)S(1)} %fusion.1.group_t, bf16[6,2,32,1280]{3,2,1,0:T(8,128)(2,1)S(1)} %copy-done, ...), custom_call_target="tpu_custom_call" | custom-call | flops 61440 | bytes 61440 | tf_op jit(solution)/shard_map/early_stats/pallas_call | solution.py:298
  44.9 7.2 %collective-permute-done.7.refs_5_ = bf16[6,2,32,1280]{3,2,1,0:T(8,128)(2,1)S(1)} collective-permute-done((bf16[6,2,32,1280]{3,2,1,0:T(8,128)(2,1)}, bf16[6,2,32,1280]{3,2,1,0:T(8,128)(2,1)S(1)}, u32[]{:S(2)}, u32[]{:S(2)}) %collective-permute-start.7) | collective-permute-done | bytes 983072 | tf_op jit(solution)/shard_map/ppermute | solution.py:95
  52.1 0.9 collective-permute-start.10
  53.0 0.8 collective-permute-start.9
  53.8 8.7 %activation.1 = bf16[10,6,32,1280]{3,2,1,0:T(8,128)(2,1)S(1)} custom-call(s32[4]{0:T(128)S(1)} %pad_add_fusion.where, s32[6,2]{1,0:T(8,128)S(1)} %collective-permute-done.5.sizes, f32[1,1280]{1,0:T(1,128)S(1)} %broadcast_in_dim.12.gain, f32[1,1280]{1,0:T(1,128)S(1)} %broadcast_in_dim.13.shift, bf16[1280,128]{1,0:T(8,128)(2,1)S(1)} %fusion.group, ...), custom_call_target="tpu_custom_call" | custom-call | flops 61440 | bytes 61440 | tf_op jit(solution)/shard_map/activation/pallas_call | solution.py:310
  62.5 11.8 %convolution.2 = (bf16[2,6,32,256]{3,2,1,0:T(8,128)(2,1)S(1)}, bf16[2,6,32,256]{3,2,1,0:T(8,128)(2,1)S(1)}, bf16[2,6,32,256]{3,2,1,0:T(8,128)(2,1)S(1)}, bf16[2,6,32,256]{3,2,1,0:T(8,128)(2,1)S(1)}) custom-call(s32[4]{0:T(128)S(1)} %pad_add_fusion.where, bf16[1920,1280]{1,0:T(8,128)(2,1)S(1)} %bitcast.5, bf16[9,80,1280]{2,1,0:T(8,128)(2,1)S(1)} %copy-done.1, ...), custom_call_target="tpu_custom_call" | custom-call | flops 1536 | bytes 307200 | tf_op jit(solution)/shard_map/convolution/pallas_call | solution.py:448
  74.4 3.9 %collective-permute-start.15 = (bf16[9,80,1280]{2,1,0:T(8,128)(2,1)S(1)}, bf16[9,80,1280]{2,1,0:T(8,128)(2,1)S(1)}, u32[]{:S(2)}, u32[]{:S(2)}) collective-permute-start(bf16[9,80,1280]{2,1,0:T(8,128)(2,1)S(1)} %collective-permute-done.9.refs_2_), channel_id=1, source_target_pairs={{0,1},{1,0},{2,3},{3,2},{4,5},{5,4},{6,7},{7,6},{8,9},{9,8},{10,11... | collective-permute-start | bytes 5529608 | tf_op jit(solution)/shard_map/ppermute | solution.py:95
  79.0 2.9 %collective-permute-start.12 = (bf16[2,6,32,256]{3,2,1,0:T(8,128)(2,1)S(1)}, bf16[2,6,32,256]{3,2,1,0:T(8,128)(2,1)S(1)}, u32[]{:S(2)}, u32[]{:S(2)}) collective-permute-start(bf16[2,6,32,256]{3,2,1,0:T(8,128)(2,1)S(1)} %get-tuple-element.43), channel_id=1, source_target_pairs={{0,1},{1,5},{2,3},{3,7},{4,0},{5,4},{6,2},{7,6},{8,9},{9,13},{10,1... | collective-permute-start | bytes 589832 | tf_op jit(solution)/shard_map/ppermute | solution.py:95
  81.8 1.5 %collective-permute-start.13 = (bf16[2,6,32,256]{3,2,1,0:T(8,128)(2,1)S(1)}, bf16[2,6,32,256]{3,2,1,0:T(8,128)(2,1)S(1)}, u32[]{:S(2)}, u32[]{:S(2)}) collective-permute-start(bf16[2,6,32,256]{3,2,1,0:T(8,128)(2,1)S(1)} %get-tuple-element.44), channel_id=1, source_target_pairs={{0,2},{1,6},{2,0},{3,4},{4,3},{5,7},{6,1},{7,5},{8,10},{9,14},{10,... | collective-permute-start | bytes 589832 | tf_op jit(solution)/shard_map/ppermute | solution.py:95
  83.4 4.9 %convolution.3 = (bf16[2,6,32,128]{3,2,1,0:T(8,128)(2,1)S(1)}, bf16[2,6,32,128]{3,2,1,0:T(8,128)(2,1)S(1)}, bf16[2,6,32,128]{3,2,1,0:T(8,128)(2,1)S(1)}, bf16[2,6,32,128]{3,2,1,0:T(8,128)(2,1)S(1)}) custom-call(s32[4]{0:T(128)S(1)} %pad_add_fusion.where, bf16[1920,1280]{1,0:T(8,128)(2,1)S(1)} %bitcast.6, ...), custom_call_target="tpu_custom_call" | custom-call | flops 1536 | bytes 102400 | tf_op jit(solution)/shard_map/convolution/pallas_call | solution.py:448
  88.9 3.3 %collective-permute-start.17 = (bf16[2,6,32,128]{3,2,1,0:T(8,128)(2,1)S(1)}, bf16[2,6,32,128]{3,2,1,0:T(8,128)(2,1)S(1)}, u32[]{:S(2)}, u32[]{:S(2)}) collective-permute-start(bf16[2,6,32,128]{3,2,1,0:T(8,128)(2,1)S(1)} %get-tuple-element.49), channel_id=1, source_target_pairs={{0,1},{1,5},{2,3},{3,7},{4,0},{5,4},{6,2},{7,6},{8,9},{9,13},{10,1... | collective-permute-start | bytes 294920 | tf_op jit(solution)/shard_map/ppermute | solution.py:95
  92.3 1.5 %collective-permute-start.18 = (bf16[2,6,32,128]{3,2,1,0:T(8,128)(2,1)S(1)}, bf16[2,6,32,128]{3,2,1,0:T(8,128)(2,1)S(1)}, u32[]{:S(2)}, u32[]{:S(2)}) collective-permute-start(bf16[2,6,32,128]{3,2,1,0:T(8,128)(2,1)S(1)} %get-tuple-element.50), channel_id=1, source_target_pairs={{0,2},{1,6},{2,0},{3,4},{4,3},{5,7},{6,1},{7,5},{8,10},{9,14},{10,... | collective-permute-start | bytes 294920 | tf_op jit(solution)/shard_map/ppermute | solution.py:95
  93.9 3.5 %main_result.1 = (bf16[6,2,32,1280]{3,2,1,0:T(8,128)(2,1)}, bf16[6,2,32,384]{3,2,1,0:T(8,128)(2,1)S(1)}) custom-call(s32[4]{0:T(128)S(1)} %pad_add_fusion.where, s32[6,2]{1,0:T(8,128)S(1)} %copy.10.sizes, bf16[6,2,32,1280]{3,2,1,0:T(8,128)(2,1)S(1)} %copy-done, f32[6,1,1280]{2,1,0:T(1,128)S(1)} %broadcast_in_dim.11.bias, ...), custom_call_target="tpu_custom_call" | custom-call | flops 61440 | bytes 61440 | tf_op jit(solution)/shard_map/main_result/pallas_call | solution.py:527
  98.1 1.3 %collective-permute-done.19.p3 = bf16[2,6,32,128]{3,2,1,0:T(8,128)(2,1)S(1)} collective-permute-done((bf16[2,6,32,128]{3,2,1,0:T(8,128)(2,1)S(1)}, bf16[2,6,32,128]{3,2,1,0:T(8,128)(2,1)S(1)}, u32[]{:S(2)}, u32[]{:S(2)}) %collective-permute-start.19) | collective-permute-done | bytes 98336 | tf_op jit(solution)/shard_map/ppermute | solution.py:95
  99.4 2.2 %last_result.1 = bf16[6,2,32,1280]{3,2,1,0:T(8,128)(2,1)} custom-call(s32[4]{0:T(128)S(1)} %pad_add_fusion.where, s32[6,2]{1,0:T(8,128)S(1)} %copy.10.sizes, f32[6,1,1280]{2,1,0:T(1,128)S(1)} %broadcast_in_dim.11.bias, bf16[6,2,32,384]{3,2,1,0:T(8,128)(2,1)S(1)} %get-tuple-element.46.slab, ...), custom_call_target="tpu_custom_call", output_to_operand_aliasing={{}: (8, {})} | custom-call | flops 491520 | bytes 491520 | tf_op jit(solution)/shard_map/last_result/pallas_call | solution.py:588
  (43 shorter events, 4.5 us)
Async XLA Ops:
  0.0 11.9 %copy-start.5 = (s32[6,2]{0,1:T(2,128)S(1)}, s32[6,2]{0,1:T(2,128)}, u32[]{:S(2)}) copy-start(s32[6,2]{0,1:T(2,128)} %param.7) | copy-start | bytes 148
  3.0 26.1 %collective-permute-start = (bf16[9,80,1280]{2,1,0:T(8,128)(2,1)}, bf16[9,80,1280]{2,1,0:T(8,128)(2,1)}, u32[]{:S(2)}, u32[]{:S(2)}) collective-permute-start(bf16[9,80,1280]{2,1,0:T(8,128)(2,1)} %own_piece.1.refs_0_), channel_id=1, source_target_pairs={{0,8},{2,10},{4,12},{6,14},{8,16},{9,1},{10,18},{11,3},{12,20},{13... | collective-permute-start | bytes 5529608 | tf_op jit(solution)/shard_map/ppermute | solution.py:95
  9.1 23.8 %collective-permute-start.2 = (bf16[6,2,32,1280]{3,2,1,0:T(8,128)(2,1)S(1)}, bf16[6,2,32,1280]{3,2,1,0:T(8,128)(2,1)}, u32[]{:S(2)}, u32[]{:S(2)}) collective-permute-start(bf16[6,2,32,1280]{3,2,1,0:T(8,128)(2,1)S(1)} %copy-done), channel_id=1, source_target_pairs={{0,2},{1,4},{2,0},{3,6},{4,1},{5,7},{6,3},{7,5},{8,10},{9,12},{10,... | collective-permute-start | bytes 2949128 | tf_op jit(solution)/shard_map/ppermute | solution.py:95
  10.6 23.2 %collective-permute-start.3 = (bf16[6,2,32,1280]{3,2,1,0:T(8,128)(2,1)S(1)}, bf16[6,2,32,1280]{3,2,1,0:T(8,128)(2,1)}, u32[]{:S(2)}, u32[]{:S(2)}) collective-permute-start(bf16[6,2,32,1280]{3,2,1,0:T(8,128)(2,1)S(1)} %copy-done), channel_id=1, source_target_pairs={{0,4},{1,2},{2,6},{3,0},{4,7},{5,1},{6,5},{7,3},{8,12},{9,10},{10,... | collective-permute-start | bytes 2949128 | tf_op jit(solution)/shard_map/ppermute | solution.py:95
  10.6 23.2 %collective-permute-start.4 = (bf16[6,2,32,1280]{3,2,1,0:T(8,128)(2,1)S(1)}, bf16[6,2,32,1280]{3,2,1,0:T(8,128)(2,1)}, u32[]{:S(2)}, u32[]{:S(2)}) collective-permute-start(bf16[6,2,32,1280]{3,2,1,0:T(8,128)(2,1)S(1)} %copy-done), channel_id=1, source_target_pairs={{1,0},{3,2},{4,5},{6,7},{9,8},{11,10},{12,13},{14,15},{17,16},{19,... | collective-permute-start | bytes 2949128 | tf_op jit(solution)/shard_map/ppermute | solution.py:95
  12.0 17.8 %collective-permute-start.5 = (s32[6,2]{1,0:T(8,128)S(1)}, s32[6,2]{1,0:T(8,128)S(1)}, u32[]{:S(2)}, u32[]{:S(2)}) collective-permute-start(s32[6,2]{1,0:T(8,128)S(1)} %copy.10.sizes), channel_id=1, source_target_pairs={{0,0},{1,4},{2,2},{3,6},{4,1},{5,5},{6,3},{7,7},{8,8},{9,12},{10,1... | collective-permute-start | bytes 152 | tf_op jit(solution)/shard_map/ppermute | solution.py:95
  29.0 23.0 %collective-permute-start.1 = (bf16[9,80,1280]{2,1,0:T(8,128)(2,1)}, bf16[9,80,1280]{2,1,0:T(8,128)(2,1)S(1)}, u32[]{:S(2)}, u32[]{:S(2)}) collective-permute-start(bf16[9,80,1280]{2,1,0:T(8,128)(2,1)} %collective-permute-done.refs_1_), channel_id=1, source_target_pairs={{8,16},{9,1},{10,18},{11,3},{12,20},{13,5},{14,22},{15,7},{16,24},... | collective-permute-start | bytes 5529608 | tf_op jit(solution)/shard_map/ppermute | solution.py:95
  29.8 22.3 %collective-permute-start.8 = (bf16[9,80,1280]{2,1,0:T(8,128)(2,1)}, bf16[9,80,1280]{2,1,0:T(8,128)(2,1)}, u32[]{:S(2)}, u32[]{:S(2)}) collective-permute-start(bf16[9,80,1280]{2,1,0:T(8,128)(2,1)} %collective-permute-done.refs_1_), channel_id=1, source_target_pairs={{0,1},{1,0},{2,3},{3,2},{4,5},{5,4},{6,7},{7,6},{8,9},{9,8},{10,11... | collective-permute-start | bytes 5529608 | tf_op jit(solution)/shard_map/ppermute | solution.py:95
  33.9 11.0 %collective-permute-start.6 = (bf16[6,2,32,1280]{3,2,1,0:T(8,128)(2,1)}, bf16[6,2,32,1280]{3,2,1,0:T(8,128)(2,1)S(1)}, u32[]{:S(2)}, u32[]{:S(2)}) collective-permute-start(bf16[6,2,32,1280]{3,2,1,0:T(8,128)(2,1)} %collective-permute-done.2.first.refs_1_), channel_id=1, source_target_pairs={{1,3},{3,1},{4,6},{6,4},{9,11},{11,9},{12,14},{14,12},{17,19},{19,... | collective-permute-start | bytes 2949128 | tf_op jit(solution)/shard_map/ppermute | solution.py:95
  34.6 17.5 %collective-permute-start.7 = (bf16[6,2,32,1280]{3,2,1,0:T(8,128)(2,1)}, bf16[6,2,32,1280]{3,2,1,0:T(8,128)(2,1)S(1)}, u32[]{:S(2)}, u32[]{:S(2)}) collective-permute-start(bf16[6,2,32,1280]{3,2,1,0:T(8,128)(2,1)} %collective-permute-done.2.first.refs_1_), channel_id=1, source_target_pairs={{0,4},{2,6},{5,1},{7,3},{8,12},{10,14},{13,9},{15,11},{16,20},{18,... | collective-permute-start | bytes 2949128 | tf_op jit(solution)/shard_map/ppermute | solution.py:95
  40.6 13.2 %copy-start.3 = (f32[1280]{0:T(1024)S(1)}, f32[1280]{0:T(1024)}, u32[]{:S(2)}) copy-start(f32[1280]{0:T(1024)} %param.8) | copy-start | bytes 15364
  40.6 13.2 %copy-start.4 = (f32[1280]{0:T(1024)S(1)}, f32[1280]{0:T(1024)}, u32[]{:S(2)}) copy-start(f32[1280]{0:T(1024)} %param.9) | copy-start | bytes 15364
  52.1 10.5 %collective-permute-start.10 = (bf16[9,80,1280]{2,1,0:T(8,128)(2,1)S(1)}, bf16[9,80,1280]{2,1,0:T(8,128)(2,1)S(1)}, u32[]{:S(2)}, u32[]{:S(2)}) collective-permute-start(bf16[9,80,1280]{2,1,0:T(8,128)(2,1)S(1)} %collective-permute-done.1.refs_3_.refs_0_), channel_id=1, source_target_pairs={{0,1},{1,0},{2,3},{3,2},{4,5},{5,4},{6,7},{7,6},{8,9},{9,8},{10,11... | collective-permute-start | bytes 5529608 | tf_op jit(solution)/shard_map/ppermute | solution.py:95
  53.0 21.4 %collective-permute-start.9 = (bf16[9,80,1280]{2,1,0:T(8,128)(2,1)S(1)}, bf16[9,80,1280]{2,1,0:T(8,128)(2,1)S(1)}, u32[]{:S(2)}, u32[]{:S(2)}) collective-permute-start(bf16[9,80,1280]{2,1,0:T(8,128)(2,1)S(1)} %collective-permute-done.1.refs_3_.refs_0_), channel_id=1, source_target_pairs={{9,1},{11,3},{13,5},{15,7},{16,24},{18,26},{20,28},{22,30}} | collective-permute-start | bytes 5529608 | tf_op jit(solution)/shard_map/ppermute | solution.py:95
  74.4 19.4 %copy-start.2 = (f32[6,1280]{1,0:T(8,128)S(1)}, f32[6,1280]{1,0:T(8,128)}, u32[]{:S(2)}) copy-start(f32[6,1280]{1,0:T(8,128)} %param.11) | copy-start | bytes 92164
  74.4 9.0 %collective-permute-start.15 = (bf16[9,80,1280]{2,1,0:T(8,128)(2,1)S(1)}, bf16[9,80,1280]{2,1,0:T(8,128)(2,1)S(1)}, u32[]{:S(2)}, u32[]{:S(2)}) collective-permute-start(bf16[9,80,1280]{2,1,0:T(8,128)(2,1)S(1)} %collective-permute-done.9.refs_2_), channel_id=1, source_target_pairs={{0,1},{1,0},{2,3},{3,2},{4,5},{5,4},{6,7},{7,6},{8,9},{9,8},{10,11... | collective-permute-start | bytes 5529608 | tf_op jit(solution)/shard_map/ppermute | solution.py:95
  78.3 10.6 %collective-permute-start.11 = (bf16[2,6,32,256]{3,2,1,0:T(8,128)(2,1)S(1)}, bf16[2,6,32,256]{3,2,1,0:T(8,128)(2,1)S(1)}, u32[]{:S(2)}, u32[]{:S(2)}) collective-permute-start(bf16[2,6,32,256]{3,2,1,0:T(8,128)(2,1)S(1)} %get-tuple-element.42), channel_id=1, source_target_pairs={{0,0},{1,4},{2,2},{3,6},{4,1},{5,5},{6,3},{7,7},{8,8},{9,12},{10,1... | collective-permute-start | bytes 589832 | tf_op jit(solution)/shard_map/ppermute | solution.py:95
  79.0 13.3 %collective-permute-start.12 = (bf16[2,6,32,256]{3,2,1,0:T(8,128)(2,1)S(1)}, bf16[2,6,32,256]{3,2,1,0:T(8,128)(2,1)S(1)}, u32[]{:S(2)}, u32[]{:S(2)}) collective-permute-start(bf16[2,6,32,256]{3,2,1,0:T(8,128)(2,1)S(1)} %get-tuple-element.43), channel_id=1, source_target_pairs={{0,1},{1,5},{2,3},{3,7},{4,0},{5,4},{6,2},{7,6},{8,9},{9,13},{10,1... | collective-permute-start | bytes 589832 | tf_op jit(solution)/shard_map/ppermute | solution.py:95
  81.8 12.0 %collective-permute-start.13 = (bf16[2,6,32,256]{3,2,1,0:T(8,128)(2,1)S(1)}, bf16[2,6,32,256]{3,2,1,0:T(8,128)(2,1)S(1)}, u32[]{:S(2)}, u32[]{:S(2)}) collective-permute-start(bf16[2,6,32,256]{3,2,1,0:T(8,128)(2,1)S(1)} %get-tuple-element.44), channel_id=1, source_target_pairs={{0,2},{1,6},{2,0},{3,4},{4,3},{5,7},{6,1},{7,5},{8,10},{9,14},{10,... | collective-permute-start | bytes 589832 | tf_op jit(solution)/shard_map/ppermute | solution.py:95
  83.4 10.5 %collective-permute-start.14 = (bf16[2,6,32,256]{3,2,1,0:T(8,128)(2,1)S(1)}, bf16[2,6,32,256]{3,2,1,0:T(8,128)(2,1)S(1)}, u32[]{:S(2)}, u32[]{:S(2)}) collective-permute-start(bf16[2,6,32,256]{3,2,1,0:T(8,128)(2,1)S(1)} %get-tuple-element.45), channel_id=1, source_target_pairs={{0,3},{1,7},{2,1},{3,5},{4,2},{5,6},{6,0},{7,4},{8,11},{9,15},{10,... | collective-permute-start | bytes 589832 | tf_op jit(solution)/shard_map/ppermute | solution.py:95
  88.3 9.1 %collective-permute-start.16 = (bf16[2,6,32,128]{3,2,1,0:T(8,128)(2,1)S(1)}, bf16[2,6,32,128]{3,2,1,0:T(8,128)(2,1)S(1)}, u32[]{:S(2)}, u32[]{:S(2)}) collective-permute-start(bf16[2,6,32,128]{3,2,1,0:T(8,128)(2,1)S(1)} %get-tuple-element.48), channel_id=1, source_target_pairs={{0,0},{1,4},{2,2},{3,6},{4,1},{5,5},{6,3},{7,7},{8,8},{9,12},{10,1... | collective-permute-start | bytes 294920 | tf_op jit(solution)/shard_map/ppermute | solution.py:95
  88.9 8.5 %collective-permute-start.17 = (bf16[2,6,32,128]{3,2,1,0:T(8,128)(2,1)S(1)}, bf16[2,6,32,128]{3,2,1,0:T(8,128)(2,1)S(1)}, u32[]{:S(2)}, u32[]{:S(2)}) collective-permute-start(bf16[2,6,32,128]{3,2,1,0:T(8,128)(2,1)S(1)} %get-tuple-element.49), channel_id=1, source_target_pairs={{0,1},{1,5},{2,3},{3,7},{4,0},{5,4},{6,2},{7,6},{8,9},{9,13},{10,1... | collective-permute-start | bytes 294920 | tf_op jit(solution)/shard_map/ppermute | solution.py:95
  92.3 5.8 %collective-permute-start.18 = (bf16[2,6,32,128]{3,2,1,0:T(8,128)(2,1)S(1)}, bf16[2,6,32,128]{3,2,1,0:T(8,128)(2,1)S(1)}, u32[]{:S(2)}, u32[]{:S(2)}) collective-permute-start(bf16[2,6,32,128]{3,2,1,0:T(8,128)(2,1)S(1)} %get-tuple-element.50), channel_id=1, source_target_pairs={{0,2},{1,6},{2,0},{3,4},{4,3},{5,7},{6,1},{7,5},{8,10},{9,14},{10,... | collective-permute-start | bytes 294920 | tf_op jit(solution)/shard_map/ppermute | solution.py:95
  93.8 5.6 %collective-permute-start.19 = (bf16[2,6,32,128]{3,2,1,0:T(8,128)(2,1)S(1)}, bf16[2,6,32,128]{3,2,1,0:T(8,128)(2,1)S(1)}, u32[]{:S(2)}, u32[]{:S(2)}) collective-permute-start(bf16[2,6,32,128]{3,2,1,0:T(8,128)(2,1)S(1)} %get-tuple-element.51), channel_id=1, source_target_pairs={{0,3},{1,7},{2,1},{3,5},{4,2},{5,6},{6,0},{7,4},{8,11},{9,15},{10,... | collective-permute-start | bytes 294920 | tf_op jit(solution)/shard_map/ppermute | solution.py:95
  (2 other events, 17.8 us)

commit v7 on v6

--- a/solution.py
+++ b/solution.py
@@ -232,13 +232,19 @@
     own, first, sibling, second, relay0, relay1, act, blocks, sums, scale, sems = refs
     frames, rows, cols, chans = blocks.shape[1:]
     members = chans // GROUPS
-    fetch(
-        where,
-        [(own, first), (sibling, second), (first, relay0), (second, relay1)],
-        blocks,
-        sems,
-    )
+    away = jnp.where(where[3] == where[1], 0, 1)
+    choices = [(own, first), (sibling, second), (first, relay0), (second, relay1)]
+
+    def bring_block(k, wait):
+        choose(away, choices[k], blocks.at[k], sems.at[k], wait)
+
+    for k in (2, 3, 0, 1):
+        bring_block(k, False)
+    for k in (2, 3):
+        bring_block(k, True)
     mean1, squares1 = reduce_blocks(where, sizes, blocks, (2, 3), group, group_t, sums, scale)
+    for k in (0, 1):
+        bring_block(k, True)
     mean0, squares0 = stats[0], stats[1]
     count0 = cells_in(where, sizes, (0, 1), frames, rows, members, 0.0)
     count1 = cells_in(where, sizes, (2, 3), frames, rows, members, 0.0)
@@ -352,7 +358,7 @@
 def all_rows(act, result, cols, compute):
     height, frames = result.shape[:2]
     line = frames * cols
-    chunk = height * line // 2
+    chunk = height * line
     lines = chunk // line
 
     def body(m, _):
@@ -361,7 +367,7 @@
         result[pl.ds(m * lines, lines)] = value.reshape(lines, frames, cols, value.shape[1])
         return 0
 
-    lax.fori_loop(0, 2, body, 0)
+    lax.fori_loop(0, 1, body, 0)
 
 
 def from_below(hop, c):

time: 103 us -> 103 us (level)
  transfers between devices with their start and end apart: 20 -> 20, of which waited for: 6 -> 6; matrix products, arithmetic and copies ran while one was open for 1% -> 1% of each run, Pallas kernels for 33% -> 32%
where the time goes in v7:
time: 103 us; the launch traced here: 102 us
  Pallas kernels  37.4 us (36%)
  starting transfers between devices  36.3 us (35%)
  waiting for transfers between devices  27 us (26%)
    ppermute x20, starting transfers between devices, permute(): return lax.ppermute(value, ('dp', 'space'), pairs)  36.3 us
    ppermute x20, waiting for transfers between devices, permute(): return lax.ppermute(value, ('dp', 'space'), pairs)  27 us
    pallas_call x2, Pallas kernels, convolution(): pl.pallas_call(functools.partial(kernel, rows, cols, part), out_shape=[ou...  16.4 us
    pallas_call x1, Pallas kernels, activation(): pl.pallas_call(act_kernel, out_shape=jax.ShapeDtypeStruct((4 * rows + 2,...  8.13 us
    pallas_call x1, Pallas kernels, early_stats(): pl.pallas_call(stats_kernel, out_shape=jax.ShapeDtypeStruct((2, 8, LANES)...  4.24 us
    pallas_call x1, Pallas kernels, main_result(): pl.pallas_call(main_result_kernel, out_shape=[jax.ShapeDtypeStruct(latent...  3.52 us
    pallas_call x1, Pallas kernels, own_piece(): pl.pallas_call(functools.partial(piece_kernel, part), out_shape=jax.Shape...  2.95 us
    pallas_call x1, Pallas kernels, last_result(): pl.pallas_call(last_result_kernel, out_shape=jax.ShapeDtypeStruct(given.s...  2.23 us
  transfers between devices with their start and end apart: 20, of which 6 were waited for; matrix products, arithmetic and copies ran while one was open for 1% of the time, Pallas kernels for 32%

profile of v7, /device:TPU:0, one launch (start us, length us, event | category | flops | bytes accessed | tf_op | source)
XLA Modules:
  0.0 101.7 jit_solution(15734298394682661281)
XLA Ops:
  0.0 2.9 %own_piece.1.refs_0_ = bf16[9,80,1280]{2,1,0:T(8,128)(2,1)} custom-call(bf16[9,160,1280]{2,1,0:T(8,128)(2,1)} %weight.1), custom_call_target="tpu_custom_call" | custom-call | bytes 4194304 | tf_op jit(solution)/shard_map/own_piece/pallas_call | solution.py:125
  3.0 6.2 %collective-permute-start = (bf16[9,80,1280]{2,1,0:T(8,128)(2,1)}, bf16[9,80,1280]{2,1,0:T(8,128)(2,1)}, u32[]{:S(2)}, u32[]{:S(2)}) collective-permute-start(bf16[9,80,1280]{2,1,0:T(8,128)(2,1)} %own_piece.1.refs_0_), channel_id=1, source_target_pairs={{0,8},{2,10},{4,12},{6,14},{8,16},{9,1},{10,18},{11,3},{12,20},{13... | collective-permute-start | bytes 5529608 | tf_op jit(solution)/shard_map/ppermute | solution.py:95
  9.1 1.5 %collective-permute-start.2 = (bf16[6,2,32,1280]{3,2,1,0:T(8,128)(2,1)S(1)}, bf16[6,2,32,1280]{3,2,1,0:T(8,128)(2,1)}, u32[]{:S(2)}, u32[]{:S(2)}) collective-permute-start(bf16[6,2,32,1280]{3,2,1,0:T(8,128)(2,1)S(1)} %copy-done), channel_id=1, source_target_pairs={{0,2},{1,4},{2,0},{3,6},{4,1},{5,7},{6,3},{7,5},{8,10},{9,12},{10,... | collective-permute-start | bytes 2949128 | tf_op jit(solution)/shard_map/ppermute | solution.py:95
  10.6 1.3 %collective-permute-start.4 = (bf16[6,2,32,1280]{3,2,1,0:T(8,128)(2,1)S(1)}, bf16[6,2,32,1280]{3,2,1,0:T(8,128)(2,1)}, u32[]{:S(2)}, u32[]{:S(2)}) collective-permute-start(bf16[6,2,32,1280]{3,2,1,0:T(8,128)(2,1)S(1)} %copy-done), channel_id=1, source_target_pairs={{1,0},{3,2},{4,5},{6,7},{9,8},{11,10},{12,13},{14,15},{17,16},{19,... | collective-permute-start | bytes 2949128 | tf_op jit(solution)/shard_map/ppermute | solution.py:95
  12.7 16.3 %collective-permute-done.refs_1_ = bf16[9,80,1280]{2,1,0:T(8,128)(2,1)} collective-permute-done((bf16[9,80,1280]{2,1,0:T(8,128)(2,1)}, bf16[9,80,1280]{2,1,0:T(8,128)(2,1)}, u32[]{:S(2)}, u32[]{:S(2)}) %collective-permute-start) | collective-permute-done | bytes 1843232 | tf_op jit(solution)/shard_map/ppermute | solution.py:95
  29.0 0.8 collective-permute-start.1
  29.8 2.5 %collective-permute-start.8 = (bf16[9,80,1280]{2,1,0:T(8,128)(2,1)}, bf16[9,80,1280]{2,1,0:T(8,128)(2,1)}, u32[]{:S(2)}, u32[]{:S(2)}) collective-permute-start(bf16[9,80,1280]{2,1,0:T(8,128)(2,1)} %collective-permute-done.refs_1_), channel_id=1, source_target_pairs={{0,1},{1,0},{2,3},{3,2},{4,5},{5,4},{6,7},{7,6},{8,9},{9,8},{10,11... | collective-permute-start | bytes 5529608 | tf_op jit(solution)/shard_map/ppermute | solution.py:95
  32.9 0.9 collective-permute-done.3.second.refs_3_
  34.6 5.6 %collective-permute-start.7 = (bf16[6,2,32,1280]{3,2,1,0:T(8,128)(2,1)}, bf16[6,2,32,1280]{3,2,1,0:T(8,128)(2,1)S(1)}, u32[]{:S(2)}, u32[]{:S(2)}) collective-permute-start(bf16[6,2,32,1280]{3,2,1,0:T(8,128)(2,1)} %collective-permute-done.2.first.refs_1_), channel_id=1, source_target_pairs={{0,4},{2,6},{5,1},{7,3},{8,12},{10,14},{13,9},{15,11},{16,20},{18,... | collective-permute-start | bytes 2949128 | tf_op jit(solution)/shard_map/ppermute | solution.py:95
  40.6 4.2 %early_stats.1.stats = f32[2,8,128]{2,1,0:T(8,128)S(1)} custom-call(s32[4]{0:T(128)S(1)} %pad_add_fusion.where, s32[6,2]{1,0:T(8,128)S(1)} %collective-permute-done.5.sizes, bf16[1280,128]{1,0:T(8,128)(2,1)S(1)} %fusion.group, bf16[128,1280]{1,0:T(8,128)(2,1)S(1)} %fusion.1.group_t, bf16[6,2,32,1280]{3,2,1,0:T(8,128)(2,1)S(1)} %copy-done, ...), custom_call_target="tpu_custom_call" | custom-call | flops 61440 | bytes 61440 | tf_op jit(solution)/shard_map/early_stats/pallas_call | solution.py:304
  44.9 7.2 %collective-permute-done.7.refs_5_ = bf16[6,2,32,1280]{3,2,1,0:T(8,128)(2,1)S(1)} collective-permute-done((bf16[6,2,32,1280]{3,2,1,0:T(8,128)(2,1)}, bf16[6,2,32,1280]{3,2,1,0:T(8,128)(2,1)S(1)}, u32[]{:S(2)}, u32[]{:S(2)}) %collective-permute-start.7) | collective-permute-done | bytes 983072 | tf_op jit(solution)/shard_map/ppermute | solution.py:95
  52.1 0.9 collective-permute-start.10
  53.8 8.1 %activation.1 = bf16[10,6,32,1280]{3,2,1,0:T(8,128)(2,1)S(1)} custom-call(s32[4]{0:T(128)S(1)} %pad_add_fusion.where, s32[6,2]{1,0:T(8,128)S(1)} %collective-permute-done.5.sizes, f32[1,1280]{1,0:T(1,128)S(1)} %broadcast_in_dim.12.gain, f32[1,1280]{1,0:T(1,128)S(1)} %broadcast_in_dim.13.shift, bf16[1280,128]{1,0:T(8,128)(2,1)S(1)} %fusion.group, ...), custom_call_target="tpu_custom_call" | custom-call | flops 61440 | bytes 61440 | tf_op jit(solution)/shard_map/activation/pallas_call | solution.py:316
  62.0 11.7 %convolution.2 = (bf16[2,6,32,256]{3,2,1,0:T(8,128)(2,1)S(1)}, bf16[2,6,32,256]{3,2,1,0:T(8,128)(2,1)S(1)}, bf16[2,6,32,256]{3,2,1,0:T(8,128)(2,1)S(1)}, bf16[2,6,32,256]{3,2,1,0:T(8,128)(2,1)S(1)}) custom-call(s32[4]{0:T(128)S(1)} %pad_add_fusion.where, bf16[1920,1280]{1,0:T(8,128)(2,1)S(1)} %bitcast.5, bf16[9,80,1280]{2,1,0:T(8,128)(2,1)S(1)} %copy-done.1, ...), custom_call_target="tpu_custom_call" | custom-call | flops 1536 | bytes 307200 | tf_op jit(solution)/shard_map/convolution/pallas_call | solution.py:454
  73.8 4.6 %collective-permute-start.15 = (bf16[9,80,1280]{2,1,0:T(8,128)(2,1)S(1)}, bf16[9,80,1280]{2,1,0:T(8,128)(2,1)S(1)}, u32[]{:S(2)}, u32[]{:S(2)}) collective-permute-start(bf16[9,80,1280]{2,1,0:T(8,128)(2,1)S(1)} %collective-permute-done.9.refs_2_), channel_id=1, source_target_pairs={{0,1},{1,0},{2,3},{3,2},{4,5},{5,4},{6,7},{7,6},{8,9},{9,8},{10,11... | collective-permute-start | bytes 5529608 | tf_op jit(solution)/shard_map/ppermute | solution.py:95
  78.3 0.8 collective-permute-start.11
  79.2 2.9 %collective-permute-start.12 = (bf16[2,6,32,256]{3,2,1,0:T(8,128)(2,1)S(1)}, bf16[2,6,32,256]{3,2,1,0:T(8,128)(2,1)S(1)}, u32[]{:S(2)}, u32[]{:S(2)}) collective-permute-start(bf16[2,6,32,256]{3,2,1,0:T(8,128)(2,1)S(1)} %get-tuple-element.43), channel_id=1, source_target_pairs={{0,1},{1,5},{2,3},{3,7},{4,0},{5,4},{6,2},{7,6},{8,9},{9,13},{10,1... | collective-permute-start | bytes 589832 | tf_op jit(solution)/shard_map/ppermute | solution.py:95
  82.0 1.5 %collective-permute-start.13 = (bf16[2,6,32,256]{3,2,1,0:T(8,128)(2,1)S(1)}, bf16[2,6,32,256]{3,2,1,0:T(8,128)(2,1)S(1)}, u32[]{:S(2)}, u32[]{:S(2)}) collective-permute-start(bf16[2,6,32,256]{3,2,1,0:T(8,128)(2,1)S(1)} %get-tuple-element.44), channel_id=1, source_target_pairs={{0,2},{1,6},{2,0},{3,4},{4,3},{5,7},{6,1},{7,5},{8,10},{9,14},{10,... | collective-permute-start | bytes 589832 | tf_op jit(solution)/shard_map/ppermute | solution.py:95
  83.5 4.6 %convolution.3 = (bf16[2,6,32,128]{3,2,1,0:T(8,128)(2,1)S(1)}, bf16[2,6,32,128]{3,2,1,0:T(8,128)(2,1)S(1)}, bf16[2,6,32,128]{3,2,1,0:T(8,128)(2,1)S(1)}, bf16[2,6,32,128]{3,2,1,0:T(8,128)(2,1)S(1)}) custom-call(s32[4]{0:T(128)S(1)} %pad_add_fusion.where, bf16[1920,1280]{1,0:T(8,128)(2,1)S(1)} %bitcast.6, ...), custom_call_target="tpu_custom_call" | custom-call | flops 1536 | bytes 102400 | tf_op jit(solution)/shard_map/convolution/pallas_call | solution.py:454
  88.9 3.3 %collective-permute-start.17 = (bf16[2,6,32,128]{3,2,1,0:T(8,128)(2,1)S(1)}, bf16[2,6,32,128]{3,2,1,0:T(8,128)(2,1)S(1)}, u32[]{:S(2)}, u32[]{:S(2)}) collective-permute-start(bf16[2,6,32,128]{3,2,1,0:T(8,128)(2,1)S(1)} %get-tuple-element.49), channel_id=1, source_target_pairs={{0,1},{1,5},{2,3},{3,7},{4,0},{5,4},{6,2},{7,6},{8,9},{9,13},{10,1... | collective-permute-start | bytes 294920 | tf_op jit(solution)/shard_map/ppermute | solution.py:95
  92.2 1.5 %collective-permute-start.18 = (bf16[2,6,32,128]{3,2,1,0:T(8,128)(2,1)S(1)}, bf16[2,6,32,128]{3,2,1,0:T(8,128)(2,1)S(1)}, u32[]{:S(2)}, u32[]{:S(2)}) collective-permute-start(bf16[2,6,32,128]{3,2,1,0:T(8,128)(2,1)S(1)} %get-tuple-element.50), channel_id=1, source_target_pairs={{0,2},{1,6},{2,0},{3,4},{4,3},{5,7},{6,1},{7,5},{8,10},{9,14},{10,... | collective-permute-start | bytes 294920 | tf_op jit(solution)/shard_map/ppermute | solution.py:95
  93.8 3.5 %main_result.1 = (bf16[6,2,32,1280]{3,2,1,0:T(8,128)(2,1)}, bf16[6,2,32,384]{3,2,1,0:T(8,128)(2,1)S(1)}) custom-call(s32[4]{0:T(128)S(1)} %pad_add_fusion.where, s32[6,2]{1,0:T(8,128)S(1)} %copy.10.sizes, bf16[6,2,32,1280]{3,2,1,0:T(8,128)(2,1)S(1)} %copy-done, f32[6,1,1280]{2,1,0:T(1,128)S(1)} %broadcast_in_dim.11.bias, ...), custom_call_target="tpu_custom_call" | custom-call | flops 61440 | bytes 61440 | tf_op jit(solution)/shard_map/main_result/pallas_call | solution.py:533
  98.0 1.3 %collective-permute-done.19.p3 = bf16[2,6,32,128]{3,2,1,0:T(8,128)(2,1)S(1)} collective-permute-done((bf16[2,6,32,128]{3,2,1,0:T(8,128)(2,1)S(1)}, bf16[2,6,32,128]{3,2,1,0:T(8,128)(2,1)S(1)}, u32[]{:S(2)}, u32[]{:S(2)}) %collective-permute-start.19) | collective-permute-done | bytes 98336 | tf_op jit(solution)/shard_map/ppermute | solution.py:95
  99.3 2.2 %last_result.1 = bf16[6,2,32,1280]{3,2,1,0:T(8,128)(2,1)} custom-call(s32[4]{0:T(128)S(1)} %pad_add_fusion.where, s32[6,2]{1,0:T(8,128)S(1)} %copy.10.sizes, f32[6,1,1280]{2,1,0:T(1,128)S(1)} %broadcast_in_dim.11.bias, bf16[6,2,32,384]{3,2,1,0:T(8,128)(2,1)S(1)} %get-tuple-element.46.slab, ...), custom_call_target="tpu_custom_call", output_to_operand_aliasing={{}: (8, {})} | custom-call | flops 491520 | bytes 491520 | tf_op jit(solution)/shard_map/last_result/pallas_call | solution.py:594
  (43 shorter events, 4.6 us)
Async XLA Ops:
  0.0 11.9 %copy-start.5 = (s32[6,2]{0,1:T(2,128)S(1)}, s32[6,2]{0,1:T(2,128)}, u32[]{:S(2)}) copy-start(s32[6,2]{0,1:T(2,128)} %param.7) | copy-start | bytes 148
  3.0 26.1 %collective-permute-start = (bf16[9,80,1280]{2,1,0:T(8,128)(2,1)}, bf16[9,80,1280]{2,1,0:T(8,128)(2,1)}, u32[]{:S(2)}, u32[]{:S(2)}) collective-permute-start(bf16[9,80,1280]{2,1,0:T(8,128)(2,1)} %own_piece.1.refs_0_), channel_id=1, source_target_pairs={{0,8},{2,10},{4,12},{6,14},{8,16},{9,1},{10,18},{11,3},{12,20},{13... | collective-permute-start | bytes 5529608 | tf_op jit(solution)/shard_map/ppermute | solution.py:95
  9.1 23.8 %collective-permute-start.2 = (bf16[6,2,32,1280]{3,2,1,0:T(8,128)(2,1)S(1)}, bf16[6,2,32,1280]{3,2,1,0:T(8,128)(2,1)}, u32[]{:S(2)}, u32[]{:S(2)}) collective-permute-start(bf16[6,2,32,1280]{3,2,1,0:T(8,128)(2,1)S(1)} %copy-done), channel_id=1, source_target_pairs={{0,2},{1,4},{2,0},{3,6},{4,1},{5,7},{6,3},{7,5},{8,10},{9,12},{10,... | collective-permute-start | bytes 2949128 | tf_op jit(solution)/shard_map/ppermute | solution.py:95
  10.6 23.2 %collective-permute-start.3 = (bf16[6,2,32,1280]{3,2,1,0:T(8,128)(2,1)S(1)}, bf16[6,2,32,1280]{3,2,1,0:T(8,128)(2,1)}, u32[]{:S(2)}, u32[]{:S(2)}) collective-permute-start(bf16[6,2,32,1280]{3,2,1,0:T(8,128)(2,1)S(1)} %copy-done), channel_id=1, source_target_pairs={{0,4},{1,2},{2,6},{3,0},{4,7},{5,1},{6,5},{7,3},{8,12},{9,10},{10,... | collective-permute-start | bytes 2949128 | tf_op jit(solution)/shard_map/ppermute | solution.py:95
  10.6 23.2 %collective-permute-start.4 = (bf16[6,2,32,1280]{3,2,1,0:T(8,128)(2,1)S(1)}, bf16[6,2,32,1280]{3,2,1,0:T(8,128)(2,1)}, u32[]{:S(2)}, u32[]{:S(2)}) collective-permute-start(bf16[6,2,32,1280]{3,2,1,0:T(8,128)(2,1)S(1)} %copy-done), channel_id=1, source_target_pairs={{1,0},{3,2},{4,5},{6,7},{9,8},{11,10},{12,13},{14,15},{17,16},{19,... | collective-permute-start | bytes 2949128 | tf_op jit(solution)/shard_map/ppermute | solution.py:95
  12.0 17.8 %collective-permute-start.5 = (s32[6,2]{1,0:T(8,128)S(1)}, s32[6,2]{1,0:T(8,128)S(1)}, u32[]{:S(2)}, u32[]{:S(2)}) collective-permute-start(s32[6,2]{1,0:T(8,128)S(1)} %copy.10.sizes), channel_id=1, source_target_pairs={{0,0},{1,4},{2,2},{3,6},{4,1},{5,5},{6,3},{7,7},{8,8},{9,12},{10,1... | collective-permute-start | bytes 152 | tf_op jit(solution)/shard_map/ppermute | solution.py:95
  29.0 23.0 %collective-permute-start.1 = (bf16[9,80,1280]{2,1,0:T(8,128)(2,1)}, bf16[9,80,1280]{2,1,0:T(8,128)(2,1)S(1)}, u32[]{:S(2)}, u32[]{:S(2)}) collective-permute-start(bf16[9,80,1280]{2,1,0:T(8,128)(2,1)} %collective-permute-done.refs_1_), channel_id=1, source_target_pairs={{8,16},{9,1},{10,18},{11,3},{12,20},{13,5},{14,22},{15,7},{16,24},... | collective-permute-start | bytes 5529608 | tf_op jit(solution)/shard_map/ppermute | solution.py:95
  29.8 22.3 %collective-permute-start.8 = (bf16[9,80,1280]{2,1,0:T(8,128)(2,1)}, bf16[9,80,1280]{2,1,0:T(8,128)(2,1)}, u32[]{:S(2)}, u32[]{:S(2)}) collective-permute-start(bf16[9,80,1280]{2,1,0:T(8,128)(2,1)} %collective-permute-done.refs_1_), channel_id=1, source_target_pairs={{0,1},{1,0},{2,3},{3,2},{4,5},{5,4},{6,7},{7,6},{8,9},{9,8},{10,11... | collective-permute-start | bytes 5529608 | tf_op jit(solution)/shard_map/ppermute | solution.py:95
  33.9 11.0 %collective-permute-start.6 = (bf16[6,2,32,1280]{3,2,1,0:T(8,128)(2,1)}, bf16[6,2,32,1280]{3,2,1,0:T(8,128)(2,1)S(1)}, u32[]{:S(2)}, u32[]{:S(2)}) collective-permute-start(bf16[6,2,32,1280]{3,2,1,0:T(8,128)(2,1)} %collective-permute-done.2.first.refs_1_), channel_id=1, source_target_pairs={{1,3},{3,1},{4,6},{6,4},{9,11},{11,9},{12,14},{14,12},{17,19},{19,... | collective-permute-start | bytes 2949128 | tf_op jit(solution)/shard_map/ppermute | solution.py:95
  34.6 17.5 %collective-permute-start.7 = (bf16[6,2,32,1280]{3,2,1,0:T(8,128)(2,1)}, bf16[6,2,32,1280]{3,2,1,0:T(8,128)(2,1)S(1)}, u32[]{:S(2)}, u32[]{:S(2)}) collective-permute-start(bf16[6,2,32,1280]{3,2,1,0:T(8,128)(2,1)} %collective-permute-done.2.first.refs_1_), channel_id=1, source_target_pairs={{0,4},{2,6},{5,1},{7,3},{8,12},{10,14},{13,9},{15,11},{16,20},{18,... | collective-permute-start | bytes 2949128 | tf_op jit(solution)/shard_map/ppermute | solution.py:95
  40.6 13.2 %copy-start.3 = (f32[1280]{0:T(1024)S(1)}, f32[1280]{0:T(1024)}, u32[]{:S(2)}) copy-start(f32[1280]{0:T(1024)} %param.8) | copy-start | bytes 15364
  40.6 13.2 %copy-start.4 = (f32[1280]{0:T(1024)S(1)}, f32[1280]{0:T(1024)}, u32[]{:S(2)}) copy-start(f32[1280]{0:T(1024)} %param.9) | copy-start | bytes 15364
  52.1 9.9 %collective-permute-start.10 = (bf16[9,80,1280]{2,1,0:T(8,128)(2,1)S(1)}, bf16[9,80,1280]{2,1,0:T(8,128)(2,1)S(1)}, u32[]{:S(2)}, u32[]{:S(2)}) collective-permute-start(bf16[9,80,1280]{2,1,0:T(8,128)(2,1)S(1)} %collective-permute-done.1.refs_3_.refs_0_), channel_id=1, source_target_pairs={{0,1},{1,0},{2,3},{3,2},{4,5},{5,4},{6,7},{7,6},{8,9},{9,8},{10,11... | collective-permute-start | bytes 5529608 | tf_op jit(solution)/shard_map/ppermute | solution.py:95
  53.0 20.7 %collective-permute-start.9 = (bf16[9,80,1280]{2,1,0:T(8,128)(2,1)S(1)}, bf16[9,80,1280]{2,1,0:T(8,128)(2,1)S(1)}, u32[]{:S(2)}, u32[]{:S(2)}) collective-permute-start(bf16[9,80,1280]{2,1,0:T(8,128)(2,1)S(1)} %collective-permute-done.1.refs_3_.refs_0_), channel_id=1, source_target_pairs={{9,1},{11,3},{13,5},{15,7},{16,24},{18,26},{20,28},{22,30}} | collective-permute-start | bytes 5529608 | tf_op jit(solution)/shard_map/ppermute | solution.py:95
  73.7 20.0 %copy-start.2 = (f32[6,1280]{1,0:T(8,128)S(1)}, f32[6,1280]{1,0:T(8,128)}, u32[]{:S(2)}) copy-start(f32[6,1280]{1,0:T(8,128)} %param.11) | copy-start | bytes 92164
  73.8 9.8 %collective-permute-start.15 = (bf16[9,80,1280]{2,1,0:T(8,128)(2,1)S(1)}, bf16[9,80,1280]{2,1,0:T(8,128)(2,1)S(1)}, u32[]{:S(2)}, u32[]{:S(2)}) collective-permute-start(bf16[9,80,1280]{2,1,0:T(8,128)(2,1)S(1)} %collective-permute-done.9.refs_2_), channel_id=1, source_target_pairs={{0,1},{1,0},{2,3},{3,2},{4,5},{5,4},{6,7},{7,6},{8,9},{9,8},{10,11... | collective-permute-start | bytes 5529608 | tf_op jit(solution)/shard_map/ppermute | solution.py:95
  78.3 10.6 %collective-permute-start.11 = (bf16[2,6,32,256]{3,2,1,0:T(8,128)(2,1)S(1)}, bf16[2,6,32,256]{3,2,1,0:T(8,128)(2,1)S(1)}, u32[]{:S(2)}, u32[]{:S(2)}) collective-permute-start(bf16[2,6,32,256]{3,2,1,0:T(8,128)(2,1)S(1)} %get-tuple-element.42), channel_id=1, source_target_pairs={{0,0},{1,4},{2,2},{3,6},{4,1},{5,5},{6,3},{7,7},{8,8},{9,12},{10,1... | collective-permute-start | bytes 589832 | tf_op jit(solution)/shard_map/ppermute | solution.py:95
  79.2 13.1 %collective-permute-start.12 = (bf16[2,6,32,256]{3,2,1,0:T(8,128)(2,1)S(1)}, bf16[2,6,32,256]{3,2,1,0:T(8,128)(2,1)S(1)}, u32[]{:S(2)}, u32[]{:S(2)}) collective-permute-start(bf16[2,6,32,256]{3,2,1,0:T(8,128)(2,1)S(1)} %get-tuple-element.43), channel_id=1, source_target_pairs={{0,1},{1,5},{2,3},{3,7},{4,0},{5,4},{6,2},{7,6},{8,9},{9,13},{10,1... | collective-permute-start | bytes 589832 | tf_op jit(solution)/shard_map/ppermute | solution.py:95
  82.0 11.7 %collective-permute-start.13 = (bf16[2,6,32,256]{3,2,1,0:T(8,128)(2,1)S(1)}, bf16[2,6,32,256]{3,2,1,0:T(8,128)(2,1)S(1)}, u32[]{:S(2)}, u32[]{:S(2)}) collective-permute-start(bf16[2,6,32,256]{3,2,1,0:T(8,128)(2,1)S(1)} %get-tuple-element.44), channel_id=1, source_target_pairs={{0,2},{1,6},{2,0},{3,4},{4,3},{5,7},{6,1},{7,5},{8,10},{9,14},{10,... | collective-permute-start | bytes 589832 | tf_op jit(solution)/shard_map/ppermute | solution.py:95
  83.5 10.2 %collective-permute-start.14 = (bf16[2,6,32,256]{3,2,1,0:T(8,128)(2,1)S(1)}, bf16[2,6,32,256]{3,2,1,0:T(8,128)(2,1)S(1)}, u32[]{:S(2)}, u32[]{:S(2)}) collective-permute-start(bf16[2,6,32,256]{3,2,1,0:T(8,128)(2,1)S(1)} %get-tuple-element.45), channel_id=1, source_target_pairs={{0,3},{1,7},{2,1},{3,5},{4,2},{5,6},{6,0},{7,4},{8,11},{9,15},{10,... | collective-permute-start | bytes 589832 | tf_op jit(solution)/shard_map/ppermute | solution.py:95
  88.2 9.1 %collective-permute-start.16 = (bf16[2,6,32,128]{3,2,1,0:T(8,128)(2,1)S(1)}, bf16[2,6,32,128]{3,2,1,0:T(8,128)(2,1)S(1)}, u32[]{:S(2)}, u32[]{:S(2)}) collective-permute-start(bf16[2,6,32,128]{3,2,1,0:T(8,128)(2,1)S(1)} %get-tuple-element.48), channel_id=1, source_target_pairs={{0,0},{1,4},{2,2},{3,6},{4,1},{5,5},{6,3},{7,7},{8,8},{9,12},{10,1... | collective-permute-start | bytes 294920 | tf_op jit(solution)/shard_map/ppermute | solution.py:95
  88.9 8.5 %collective-permute-start.17 = (bf16[2,6,32,128]{3,2,1,0:T(8,128)(2,1)S(1)}, bf16[2,6,32,128]{3,2,1,0:T(8,128)(2,1)S(1)}, u32[]{:S(2)}, u32[]{:S(2)}) collective-permute-start(bf16[2,6,32,128]{3,2,1,0:T(8,128)(2,1)S(1)} %get-tuple-element.49), channel_id=1, source_target_pairs={{0,1},{1,5},{2,3},{3,7},{4,0},{5,4},{6,2},{7,6},{8,9},{9,13},{10,1... | collective-permute-start | bytes 294920 | tf_op jit(solution)/shard_map/ppermute | solution.py:95
  92.2 5.8 %collective-permute-start.18 = (bf16[2,6,32,128]{3,2,1,0:T(8,128)(2,1)S(1)}, bf16[2,6,32,128]{3,2,1,0:T(8,128)(2,1)S(1)}, u32[]{:S(2)}, u32[]{:S(2)}) collective-permute-start(bf16[2,6,32,128]{3,2,1,0:T(8,128)(2,1)S(1)} %get-tuple-element.50), channel_id=1, source_target_pairs={{0,2},{1,6},{2,0},{3,4},{4,3},{5,7},{6,1},{7,5},{8,10},{9,14},{10,... | collective-permute-start | bytes 294920 | tf_op jit(solution)/shard_map/ppermute | solution.py:95
  93.7 5.6 %collective-permute-start.19 = (bf16[2,6,32,128]{3,2,1,0:T(8,128)(2,1)S(1)}, bf16[2,6,32,128]{3,2,1,0:T(8,128)(2,1)S(1)}, u32[]{:S(2)}, u32[]{:S(2)}) collective-permute-start(bf16[2,6,32,128]{3,2,1,0:T(8,128)(2,1)S(1)} %get-tuple-element.51), channel_id=1, source_target_pairs={{0,3},{1,7},{2,1},{3,5},{4,2},{5,6},{6,0},{7,4},{8,11},{9,15},{10,... | collective-permute-start | bytes 294920 | tf_op jit(solution)/shard_map/ppermute | solution.py:95
  (2 other events, 17.3 us)
